TPU v7x, 256 devices: a whole 4x4x8 slice. The times are simulated.
256 devices in a mesh: island: 16 (over y_hi, z), inner: 16 (over y_lo, x, core).
Axes of the slice: x: 4, y: 4 (y_hi: 2, y_lo: 2; y = y_hi * 2 + y_lo), z: 8, core: 2. Of those that a mesh axis runs over, the one named last changes fastest.
Arguments:
- island_delta: float32 [16, 2, 8192, 512], P('island', None, 'inner'), may hold values from -200 to 200, as said below
- params: float32 [2, 8192, 512], P(None, 'inner'), may hold values from -6 to 6
- momentum: float32 [2, 8192, 512], P(None, 'inner'), may hold values from -6 to 6
Outputs:
- new_params: float32 [2, 8192, 512], P(None, 'inner')
- new_momentum: float32 [2, 8192, 512], P(None, 'inner')
Inputs may be any that keep to these rules, and one draw needn't show every extreme that they name: `island_delta`: entries are finite and of mixed sign.
All inputs are finite; a program needn't handle non-finite values.
Results may differ from a plain program's by a relative error of at most 0.0003.
Values sent between devices are 32-bit elements; how exact they have to be, the bound alone decides.
A program may use at most 64 MiB of HBM per device.

v0:
```python
import jax
import jax.numpy as jnp
from jax import lax
from jax.sharding import PartitionSpec as P

D = 8192
HEAD = 128
KVH = 4


def outer_update(average, params, momentum, mean_square):
    factor = jnp.minimum(jnp.float32(1.0), 0.5 / jnp.sqrt(mean_square + 1e-06))
    clipped = factor * average
    new_momentum = 0.9 * momentum + clipped
    new_params = params - 0.7 * (clipped + 0.9 * new_momentum)
    return (new_params, new_momentum)


def body(island_delta, params, momentum):
    replicas = lax.axis_size("island")
    count = 2 * D * KVH * HEAD
    own_delta = island_delta[0]
    average = lax.psum(own_delta, "island") / replicas
    total_sq = lax.psum(jnp.sum(average * average), "inner")
    return outer_update(average, params, momentum, total_sq / count)


def solution(mesh):
    in_specs = (P("island", None, "inner", None), P(None, "inner", None), P(None, "inner", None))
    out_specs = (P(None, "inner", None), P(None, "inner", None))
    return jax.shard_map(body, mesh=mesh, in_specs=in_specs, out_specs=out_specs, check_vma=False)
```

profile of v0, /device:TPU:32, one launch (start us, length us, event | category | flops | bytes accessed | tf_op | source)
XLA Modules:
  0.0 218.6 jit_solution(3867526521445673255)
XLA Ops:
  7.2 0.0 all-reduce.2.cloned.1.call-start
  7.2 0.7 all-reduce.2.cloned.1.call-update
  7.9 167.5 %all-reduce.2.cloned.1.call-done = f32[2,512,512]{2,1,0:T(8,128)} async-done(((f32[2,512,512]{2,1,0:T(8,128)}), f32[2,512,512]{2,1,0:T(8,128)}) %all-reduce.2.cloned.1.call-update) | async-done | bytes 2097168 | tf_op jit(solution)/shard_map/psum | solution.py:23
  175.4 0.0 copy-start
  175.4 2.9 %multiply_reduce_fusion = f32[]{:T(128)} fusion(f32[2,512,512]{2,1,0:T(8,128)} %all-reduce.2.cloned.1.call-done), kind=kLoop, calls=%fused_computation.2 | loop fusion | flops 1572863 | bytes 2097156 | tf_op jit(solution)/shard_map/reduce_sum | solution.py:24
  178.3 27.8 %psum.15 = f32[]{:T(128)} all-reduce(f32[]{:T(128)} %multiply_reduce_fusion), channel_id=1, replica_groups=mesh['island'=16,'inner'=16] {'inner'}, use_global_device_ids=true, to_apply=%region_2.0 | all-reduce | flops 1 | bytes 8 | tf_op jit(solution)/shard_map/psum | solution.py:24
  206.8 0.0 copy-done
  206.8 5.0 %multiply_subtract_fusion = (f32[2,512,512]{2,1,0:T(8,128)}, f32[2,512,512]{2,1,0:T(8,128)}) fusion(f32[2,512,512]{2,1,0:T(8,128)} %param.4, f32[2,512,512]{2,1,0:T(8,128)S(1)} %copy-done, f32[]{:T(128)S(6)} %mul.24, f32[2,512,512]{2,1,0:T(8,128)} %param.5), kind=kLoop, calls=%fused_computation | loop fusion | flops 3670016 | bytes 10485764 | tf_op jit(solution)/shard_map/sub | solution.py:15
Async XLA Ops:
  7.2 168.3 %all-reduce.2.cloned.1.call-start = ((), (), s32[]{:S(2)}) async-start(), calls=%async_computation | async-start | bytes 4194304 | tf_op jit(solution)/shard_map/psum | solution.py:23
  175.4 31.3 %copy-start = (f32[2,512,512]{2,1,0:T(8,128)S(1)}, f32[2,512,512]{2,1,0:T(8,128)}, u32[]{:S(2)}) copy-start(f32[2,512,512]{2,1,0:T(8,128)} %all-reduce.2.cloned.1.call-done) | copy-start | bytes 6291460
Sparse Core Ops, SparseCore 0:
  10.6 164.7 all-reduce.1
where the time goes:
time: 221 us; the launch traced here: 219 us
  waiting for transfers between devices  168 us (76%)
  blocking collectives  27.8 us (13%)
  between operations  14.7 us (7%)
  other arithmetic  7.91 us (4%)
    psum x1, waiting for transfers between devices, body(): average = lax.psum(own_delta, 'island') / replicas  168 us
    psum x1, blocking collectives, body(): total_sq = lax.psum(jnp.sum(average * average), 'inner')  27.8 us
    sub x1, other arithmetic, outer_update(): new_params = params - 0.7 * (clipped + 0.9 * new_momentum)  5.02 us
  transfers between devices with their start and end apart: 1, of which 1 were waited for; matrix products, arithmetic and copies ran while one was open for 0% of the time, Pallas kernels for 0%

commit v1 on v0

--- a/solution.py
+++ b/solution.py
@@ -20,8 +20,10 @@
     replicas = lax.axis_size("island")
     count = 2 * D * KVH * HEAD
     own_delta = island_delta[0]
-    average = lax.psum(own_delta, "island") / replicas
-    total_sq = lax.psum(jnp.sum(average * average), "inner")
+    part = lax.psum_scatter(own_delta, "island", scatter_dimension=1, tiled=True) / replicas
+    part_sq = jnp.sum(part * part)
+    average = lax.all_gather(part, "island", axis=1, tiled=True)
+    total_sq = lax.psum(part_sq, ("island", "inner"))
     return outer_update(average, params, momentum, total_sq / count)
 
 

time: 221 us -> 320 us (1.45)
  waiting for transfers between devices: 168 us -> 221 us
  blocking collectives: 27.8 us -> 75.7 us
    reduce_scatter x0 -> x1, waiting for transfers between devices: none -> 211 us  [body(): lax.psum_scatter(own_delta, 'island', scatter_dimension=1, tiled=True)]
    psum x1 -> x0, waiting for transfers between devices: 168 us -> none  [body(): average = lax.psum(own_delta, 'island') / replicas]
    psum x1, blocking collectives: 27.8 us -> 75.7 us  [body(): total_sq = lax.psum(part_sq, ('island', 'inner'))]
    all_gather x0 -> x1, waiting for transfers between devices: none -> 8.57 us  [body(): average = lax.all_gather(part, 'island', axis=1, tiled=True)]
  transfers between devices with their start and end apart: 1 -> 2, of which waited for: 1 -> 2; matrix products, arithmetic and copies ran while one was open for 0% -> 0% of each run, Pallas kernels for 0% -> 0%
where the time goes in v1:
time: 320 us; the launch traced here: 318 us
  waiting for transfers between devices  221 us (69%)
  blocking collectives  75.7 us (24%)
  between operations  14.7 us (5%)
  other arithmetic  7.19 us (2%)
    reduce_scatter x1, waiting for transfers between devices, body(): lax.psum_scatter(own_delta, 'island', scatter_dimension=1, tiled=True)  211 us
    psum x1, blocking collectives, body(): total_sq = lax.psum(part_sq, ('island', 'inner'))  75.7 us
    all_gather x1, waiting for transfers between devices, body(): average = lax.all_gather(part, 'island', axis=1, tiled=True)  8.57 us
  transfers between devices with their start and end apart: 2, of which 2 were waited for; matrix products, arithmetic and copies ran while one was open for 0% of the time, Pallas kernels for 0%

profile of v1, /device:TPU:32, one launch (start us, length us, event | category | flops | bytes accessed | tf_op | source)
XLA Modules:
  0.0 318.5 jit_solution(10462347991436961005)
XLA Ops:
  7.2 0.0 copy-start
  7.2 0.0 reduce-scatter.2.cloned.1.call-start
  7.2 0.7 reduce-scatter.2.cloned.1.call-update
  7.9 0.0 all-gather.2.cloned.1.call-start
  8.0 211.4 %reduce-scatter.2.cloned.1.call-done = f32[2,32,512]{2,1,0:T(8,128)} async-done(((f32[2,512,512]{2,1,0:T(8,128)}), f32[2,32,512]{2,1,0:T(8,128)}) %reduce-scatter.2.cloned.1.call-update) | async-done | bytes 131088 | tf_op jit(solution)/shard_map/reduce_scatter | solution.py:23
  219.4 2.2 multiply_reduce_fusion
  221.6 0.0 all-gather.2.cloned.1.call-update
  221.6 75.7 %psum.7 = f32[]{:T(128)} all-reduce(f32[]{:T(128)} %get-tuple-element.4), channel_id=1, replica_groups=mesh['island'=16,'inner'=16] {'island','inner'}, use_global_device_ids=true, to_apply=%region_2.0 | all-reduce | flops 1 | bytes 8 | tf_op jit(solution)/shard_map/psum | solution.py:26
  298.0 8.6 %all-gather.2.cloned.1.call-done = f32[2,512,512]{2,1,0:T(8,128)} async-done(((f32[2,32,512]{2,1,0:T(8,128)}), f32[2,512,512]{2,1,0:T(8,128)}) %all-gather.2.cloned.1.call-update) | async-done | bytes 2097168 | tf_op jit(solution)/shard_map/all_gather | solution.py:25
  306.6 0.0 copy-done
  306.6 5.0 %multiply_subtract_fusion = (f32[2,512,512]{2,1,0:T(8,128)}, f32[2,512,512]{2,1,0:T(8,128)}) fusion(f32[2,512,512]{2,1,0:T(8,128)S(1)} %copy-done, f32[2,512,512]{2,1,0:T(8,128)} %all-gather.2.cloned.1.call-done, f32[]{:T(128)S(6)} %min_shard_map.3, f32[2,512,512]{2,1,0:T(8,128)} %param.5), kind=kLoop, calls=%fused_computation | loop fusion | flops 3670016 | bytes 10485764 | tf_op jit(solution)/shard_map/sub | solution.py:15
Async XLA Ops:
  7.2 299.4 %copy-start = (f32[2,512,512]{2,1,0:T(8,128)S(1)}, f32[2,512,512]{2,1,0:T(8,128)}, u32[]{:S(2)}) copy-start(f32[2,512,512]{2,1,0:T(8,128)} %param.4) | copy-start | bytes 6291460
  7.2 212.2 %reduce-scatter.2.cloned.1.call-start = ((), (), s32[]{:S(2)}) async-start(), calls=%async_computation.1 | async-start | bytes 2228224 | tf_op jit(solution)/shard_map/reduce_scatter | solution.py:23
  7.9 298.7 %all-gather.2.cloned.1.call-start = ((), (), s32[]{:S(2)}) async-start(), calls=%async_computation.2 | async-start | bytes 2228224 | tf_op jit(solution)/shard_map/all_gather | solution.py:25
Sparse Core Ops, SparseCore 0:
  11.9 207.4 reduce-scatter.1
  222.6 83.9 all-gather.1

commit v2 on v0

--- a/solution.py
+++ b/solution.py
@@ -6,6 +6,7 @@
 D = 8192
 HEAD = 128
 KVH = 4
+RING = 8
 
 
 def outer_update(average, params, momentum, mean_square):
@@ -16,12 +17,49 @@
     return (new_params, new_momentum)
 
 
+def ring_pairs(islands, shift):
+    groups = islands // RING
+    return [(g * RING + z, g * RING + (z + shift) % RING) for g in range(groups) for z in range(RING)]
+
+
 def body(island_delta, params, momentum):
-    replicas = lax.axis_size("island")
+    islands = lax.axis_size("island")
     count = 2 * D * KVH * HEAD
-    own_delta = island_delta[0]
-    average = lax.psum(own_delta, "island") / replicas
-    total_sq = lax.psum(jnp.sum(average * average), "inner")
+    me = lax.axis_index("island")
+    z = me % RING
+    own = island_delta[0]
+    halves, rows, cols = own.shape
+    chunk = rows // RING
+    x = own.reshape(halves, RING, chunk, cols)
+    right, left = ring_pairs(islands, 1), ring_pairs(islands, RING - 1)
+
+    def take(h, c):
+        return lax.dynamic_index_in_dim(x[h], c % RING, axis=0, keepdims=False)
+
+    acc_r = take(0, z - 1)
+    acc_l = take(1, z + 1)
+    for s in range(RING - 1):
+        got_r = lax.ppermute(acc_r, "island", right)
+        got_l = lax.ppermute(acc_l, "island", left)
+        acc_r = got_r + take(0, z - 2 - s)
+        acc_l = got_l + take(1, z + 2 + s)
+    mine = jnp.stack([acc_r, acc_l])
+    partner = [(i, (i + RING) % islands) for i in range(islands)]
+    mine = (mine + lax.ppermute(mine, "island", partner)) / islands
+    part_sq = jnp.sum(mine * mine)
+
+    out = jnp.zeros((halves, RING, chunk, cols), jnp.float32)
+    out = lax.dynamic_update_index_in_dim(out, mine[:, None], z, axis=1)
+    sq = part_sq
+    cur_r, cur_l, cur_q = mine[0], mine[1], part_sq
+    for s in range(RING - 1):
+        cur_r, cur_q = lax.ppermute((cur_r, cur_q), "island", right)
+        cur_l = lax.ppermute(cur_l, "island", left)
+        sq = sq + cur_q
+        out = lax.dynamic_update_slice(out, cur_r[None, None], (0, (z - 1 - s) % RING, 0, 0))
+        out = lax.dynamic_update_slice(out, cur_l[None, None], (1, (z + 1 + s) % RING, 0, 0))
+    average = out.reshape(halves, rows, cols)
+    total_sq = lax.psum(sq, "inner")
     return outer_update(average, params, momentum, total_sq / count)
 
 

time: 221 us -> 171 us (0.77)
  waiting for transfers between devices: 168 us -> 71.2 us
  starting transfers between devices: 0.04 us -> 53.3 us
  between operations: 14.7 us -> 7.03 us
  local copies, waits for them, and re-layouts: 0.01 us -> 4.2 us
  other arithmetic: 7.91 us -> 3.98 us
    psum x1 -> x0, waiting for transfers between devices: 168 us -> none  [body(): average = lax.psum(own_delta, 'island') / replicas]
    ppermute x0 -> x36, waiting for transfers between devices: none -> 71.2 us  [the longest x14 25.7 us: body(): cur_r, cur_q = lax.ppermute((cur_r, cur_q), 'island', right)]
    ppermute x0 -> x36, starting transfers between devices: none -> 53.3 us  [the longest x7 16.3 us: body(): cur_l = lax.ppermute(cur_l, 'island', left)]
    sub x1, other arithmetic: 5.02 us -> 2.79 us  [outer_update(): new_params = params - 0.7 * (clipped + 0.9 * new_momentum)]
  transfers between devices with their start and end apart: 1 -> 36, of which waited for: 1 -> 29; matrix products, arithmetic and copies ran while one was open for 0% -> 0% of each run, Pallas kernels for 0% -> 0%
where the time goes in v2:
time: 171 us; the launch traced here: 167 us
  waiting for transfers between devices  71.2 us (42%)
  starting transfers between devices  53.3 us (31%)
  blocking collectives  27.6 us (16%)
  between operations  7.03 us (4%)
  local copies, waits for them, and re-layouts  4.2 us (2%)
  other arithmetic  3.98 us (2%)
    psum x1, blocking collectives, body(): total_sq = lax.psum(sq, 'inner')  27.6 us
    ppermute x14, waiting for transfers between devices, body(): cur_r, cur_q = lax.ppermute((cur_r, cur_q), 'island', right)  25.7 us
    ppermute x7, waiting for transfers between devices, body(): got_r = lax.ppermute(acc_r, 'island', right)  21.8 us
    ppermute x7, starting transfers between devices, body(): cur_l = lax.ppermute(cur_l, 'island', left)  16.3 us
    ppermute x7, starting transfers between devices, body(): got_l = lax.ppermute(acc_l, 'island', left)  15.4 us
    ppermute x7, waiting for transfers between devices, body(): cur_l = lax.ppermute(cur_l, 'island', left)  14.8 us
    ppermute x14, starting transfers between devices, body(): cur_r, cur_q = lax.ppermute((cur_r, cur_q), 'island', right)  13.4 us
    ppermute x7, starting transfers between devices, body(): got_r = lax.ppermute(acc_r, 'island', right)  4.81 us
  transfers between devices with their start and end apart: 36, of which 29 were waited for; matrix products, arithmetic and copies ran while one was open for 0% of the time, Pallas kernels for 0%

profile of v2, /device:TPU:32, one launch (start us, length us, event | category | flops | bytes accessed | tf_op | source)
XLA Modules:
  0.0 167.4 jit_solution(9450027725054532129)
XLA Ops:
  0.7 1.7 %fusion.4 = (f32[1,1,512,512]{3,2,1,0:T(8,128)S(1)}, f32[1,1,512,512]{3,2,1,0:T(8,128)S(1)}) fusion(f32[1,2,512,512]{3,2,1,0:T(8,128)} %param.3), kind=kLoop, calls=%fused_computation.43 | loop fusion | bytes 4194304 | tf_op jit(solution)/shard_map/slice | solution.py:37
  2.4 2.0 %collective-permute-start = (f32[64,512]{1,0:T(8,128)S(1)}, f32[64,512]{1,0:T(8,128)S(1)}, u32[]{:S(2)}, u32[]{:S(2)}) collective-permute-start(f32[64,512]{1,0:T(8,128)S(1)} %dynamic-slice_bitcast_fusion.1), channel_id=1, source_target_pairs={{0,16},{16,32},{32,48},{48,64},{64,80},{80,96},{96,112},{112,0},{1... | collective-permute-start | bytes 393224 | tf_op jit(solution)/shard_map/ppermute | solution.py:42
  4.4 0.2 collective-permute-start.7
  4.8 2.9 %collective-permute-done = f32[64,512]{1,0:T(8,128)S(1)} collective-permute-done((f32[64,512]{1,0:T(8,128)S(1)}, f32[64,512]{1,0:T(8,128)S(1)}, u32[]{:S(2)}, u32[]{:S(2)}) %collective-permute-start) | collective-permute-done | bytes 131104 | tf_op jit(solution)/shard_map/ppermute | solution.py:42
  7.7 2.0 %collective-permute-start.1 = (f32[64,512]{1,0:T(8,128)S(1)}, f32[64,512]{1,0:T(8,128)S(1)}, u32[]{:S(2)}, u32[]{:S(2)}) collective-permute-start(f32[64,512]{1,0:T(8,128)S(1)} %bitcast_add_fusion.15), channel_id=1, source_target_pairs={{0,16},{16,32},{32,48},{48,64},{64,80},{80,96},{96,112},{112,0},{1... | collective-permute-start | bytes 393224 | tf_op jit(solution)/shard_map/ppermute | solution.py:42
  9.8 2.4 %collective-permute-start.8 = (f32[64,512]{1,0:T(8,128)S(1)}, f32[64,512]{1,0:T(8,128)S(1)}, u32[]{:S(2)}, u32[]{:S(2)}) collective-permute-start(f32[64,512]{1,0:T(8,128)S(1)} %bitcast_add_fusion.8), channel_id=1, source_target_pairs={{0,112},{16,0},{32,16},{48,32},{64,48},{80,64},{96,80},{112,96},{1... | collective-permute-start | bytes 393224 | tf_op jit(solution)/shard_map/ppermute | solution.py:43
  12.2 2.8 %collective-permute-done.1 = f32[64,512]{1,0:T(8,128)S(1)} collective-permute-done((f32[64,512]{1,0:T(8,128)S(1)}, f32[64,512]{1,0:T(8,128)S(1)}, u32[]{:S(2)}, u32[]{:S(2)}) %collective-permute-start.1) | collective-permute-done | bytes 131104 | tf_op jit(solution)/shard_map/ppermute | solution.py:42
  15.1 0.7 collective-permute-done.8
  15.8 2.6 %collective-permute-start.9 = (f32[64,512]{1,0:T(8,128)S(1)}, f32[64,512]{1,0:T(8,128)S(1)}, u32[]{:S(2)}, u32[]{:S(2)}) collective-permute-start(f32[64,512]{1,0:T(8,128)S(1)} %bitcast_add_fusion.7), channel_id=1, source_target_pairs={{0,112},{16,0},{32,16},{48,32},{64,48},{80,64},{96,80},{112,96},{1... | collective-permute-start | bytes 393224 | tf_op jit(solution)/shard_map/ppermute | solution.py:43
  18.5 2.8 %collective-permute-done.2 = f32[64,512]{1,0:T(8,128)S(1)} collective-permute-done((f32[64,512]{1,0:T(8,128)S(1)}, f32[64,512]{1,0:T(8,128)S(1)}, u32[]{:S(2)}, u32[]{:S(2)}) %collective-permute-start.2) | collective-permute-done | bytes 131104 | tf_op jit(solution)/shard_map/ppermute | solution.py:42
  21.4 0.7 collective-permute-done.9
  22.1 2.6 %collective-permute-start.10 = (f32[64,512]{1,0:T(8,128)S(1)}, f32[64,512]{1,0:T(8,128)S(1)}, u32[]{:S(2)}, u32[]{:S(2)}) collective-permute-start(f32[64,512]{1,0:T(8,128)S(1)} %bitcast_add_fusion.6), channel_id=1, source_target_pairs={{0,112},{16,0},{32,16},{48,32},{64,48},{80,64},{96,80},{112,96},{1... | collective-permute-start | bytes 393224 | tf_op jit(solution)/shard_map/ppermute | solution.py:43
  24.7 2.8 %collective-permute-done.3 = f32[64,512]{1,0:T(8,128)S(1)} collective-permute-done((f32[64,512]{1,0:T(8,128)S(1)}, f32[64,512]{1,0:T(8,128)S(1)}, u32[]{:S(2)}, u32[]{:S(2)}) %collective-permute-start.3) | collective-permute-done | bytes 131104 | tf_op jit(solution)/shard_map/ppermute | solution.py:42
  27.6 0.2 collective-permute-start.4
  27.7 0.9 collective-permute-done.10
  28.7 2.6 %collective-permute-start.11 = (f32[64,512]{1,0:T(8,128)S(1)}, f32[64,512]{1,0:T(8,128)S(1)}, u32[]{:S(2)}, u32[]{:S(2)}) collective-permute-start(f32[64,512]{1,0:T(8,128)S(1)} %bitcast_add_fusion.5), channel_id=1, source_target_pairs={{0,112},{16,0},{32,16},{48,32},{64,48},{80,64},{96,80},{112,96},{1... | collective-permute-start | bytes 393224 | tf_op jit(solution)/shard_map/ppermute | solution.py:43
  31.3 4.0 %collective-permute-done.4 = f32[64,512]{1,0:T(8,128)S(1)} collective-permute-done((f32[64,512]{1,0:T(8,128)S(1)}, f32[64,512]{1,0:T(8,128)S(1)}, u32[]{:S(2)}, u32[]{:S(2)}) %collective-permute-start.4) | collective-permute-done | bytes 131104 | tf_op jit(solution)/shard_map/ppermute | solution.py:42
  35.3 0.4 collective-permute-start.5
  35.7 0.7 collective-permute-done.11
  36.4 2.6 %collective-permute-start.12 = (f32[64,512]{1,0:T(8,128)S(1)}, f32[64,512]{1,0:T(8,128)S(1)}, u32[]{:S(2)}, u32[]{:S(2)}) collective-permute-start(f32[64,512]{1,0:T(8,128)S(1)} %bitcast_add_fusion.4), channel_id=1, source_target_pairs={{0,112},{16,0},{32,16},{48,32},{64,48},{80,64},{96,80},{112,96},{1... | collective-permute-start | bytes 393224 | tf_op jit(solution)/shard_map/ppermute | solution.py:43
  38.9 3.6 %collective-permute-done.5 = f32[64,512]{1,0:T(8,128)S(1)} collective-permute-done((f32[64,512]{1,0:T(8,128)S(1)}, f32[64,512]{1,0:T(8,128)S(1)}, u32[]{:S(2)}, u32[]{:S(2)}) %collective-permute-start.5) | collective-permute-done | bytes 131104 | tf_op jit(solution)/shard_map/ppermute | solution.py:42
  42.6 0.1 collective-permute-start.6
  42.7 0.7 collective-permute-done.12
  43.4 2.3 %collective-permute-start.13 = (f32[64,512]{1,0:T(8,128)S(1)}, f32[64,512]{1,0:T(8,128)S(1)}, u32[]{:S(2)}, u32[]{:S(2)}) collective-permute-start(f32[64,512]{1,0:T(8,128)S(1)} %bitcast_add_fusion.3), channel_id=1, source_target_pairs={{0,112},{16,0},{32,16},{48,32},{64,48},{80,64},{96,80},{112,96},{1... | collective-permute-start | bytes 393224 | tf_op jit(solution)/shard_map/ppermute | solution.py:43
  45.7 2.8 %collective-permute-done.6 = f32[64,512]{1,0:T(8,128)S(1)} collective-permute-done((f32[64,512]{1,0:T(8,128)S(1)}, f32[64,512]{1,0:T(8,128)S(1)}, u32[]{:S(2)}, u32[]{:S(2)}) %collective-permute-start.6) | collective-permute-done | bytes 131104 | tf_op jit(solution)/shard_map/ppermute | solution.py:42
  48.6 0.5 collective-permute-done.13
  49.2 3.5 %collective-permute-start.14 = (f32[2,64,512]{2,1,0:T(8,128)S(1)}, f32[2,64,512]{2,1,0:T(8,128)S(1)}, u32[]{:S(2)}, u32[]{:S(2)}) collective-permute-start(f32[2,64,512]{2,1,0:T(8,128)S(1)} %pad_maximum_fusion), channel_id=1, source_target_pairs={{0,128},{16,144},{32,160},{48,176},{64,192},{80,208},{96,224},{112... | collective-permute-start | bytes 786440 | tf_op jit(solution)/shard_map/ppermute | solution.py:48
  52.6 4.7 %collective-permute-done.14 = f32[2,64,512]{2,1,0:T(8,128)S(1)} collective-permute-done((f32[2,64,512]{2,1,0:T(8,128)S(1)}, f32[2,64,512]{2,1,0:T(8,128)S(1)}, u32[]{:S(2)}, u32[]{:S(2)}) %collective-permute-start.14) | collective-permute-done | bytes 262176 | tf_op jit(solution)/shard_map/ppermute | solution.py:48
  57.3 0.7 multiply_reduce_fusion
  58.0 3.3 %collective-permute-start.15 = (f32[]{:T(128)}, f32[]{:T(128)}, u32[]{:S(2)}, u32[]{:S(2)}) collective-permute-start(f32[]{:T(128)} %get-tuple-element.4), channel_id=1, source_target_pairs={{0,16},{16,32},{32,48},{48,64},{64,80},{80,96},{96,112},{112,0},{1... | collective-permute-start | bytes 20 | tf_op jit(solution)/shard_map/ppermute | solution.py:56
  61.3 3.2 %collective-permute-start.22 = (f32[64,512]{1,0:T(8,128)S(1)}, f32[64,512]{1,0:T(8,128)S(1)}, u32[]{:S(2)}, u32[]{:S(2)}) collective-permute-start(f32[64,512]{1,0:T(8,128)S(1)} %get-tuple-element.9), channel_id=1, source_target_pairs={{0,16},{16,32},{32,48},{48,64},{64,80},{80,96},{96,112},{112,0},{1... | collective-permute-start | bytes 393224 | tf_op jit(solution)/shard_map/ppermute | solution.py:56
  65.9 2.1 %collective-permute-start.16 = (f32[]{:T(128)}, f32[]{:T(128)}, u32[]{:S(2)}, u32[]{:S(2)}) collective-permute-start(f32[]{:T(128)} %collective-permute-done.15), channel_id=1, source_target_pairs={{0,16},{16,32},{32,48},{48,64},{64,80},{80,96},{96,112},{112,0},{1... | collective-permute-start | bytes 20 | tf_op jit(solution)/shard_map/ppermute | solution.py:56
  68.0 1.7 %collective-permute-done.16 = f32[]{:T(128)} collective-permute-done((f32[]{:T(128)}, f32[]{:T(128)}, u32[]{:S(2)}, u32[]{:S(2)}) %collective-permute-start.16) | collective-permute-done | bytes 36 | tf_op jit(solution)/shard_map/ppermute | solution.py:56
  69.7 2.0 %collective-permute-start.17 = (f32[]{:T(128)}, f32[]{:T(128)}, u32[]{:S(2)}, u32[]{:S(2)}) collective-permute-start(f32[]{:T(128)} %collective-permute-done.16), channel_id=1, source_target_pairs={{0,16},{16,32},{32,48},{48,64},{64,80},{80,96},{96,112},{112,0},{1... | collective-permute-start | bytes 20 | tf_op jit(solution)/shard_map/ppermute | solution.py:56
  72.3 1.5 collective-permute-done.17
  73.8 1.6 collective-permute-start.18
  76.1 2.6 %collective-permute-done.18 = f32[]{:T(128)} collective-permute-done((f32[]{:T(128)}, f32[]{:T(128)}, u32[]{:S(2)}, u32[]{:S(2)}) %collective-permute-start.18) | collective-permute-done | bytes 36 | tf_op jit(solution)/shard_map/ppermute | solution.py:56
  78.7 0.4 collective-permute-start.19
  79.8 3.9 %collective-permute-done.19 = f32[]{:T(128)} collective-permute-done((f32[]{:T(128)}, f32[]{:T(128)}, u32[]{:S(2)}, u32[]{:S(2)}) %collective-permute-start.19) | collective-permute-done | bytes 36 | tf_op jit(solution)/shard_map/ppermute | solution.py:56
  84.4 4.2 %collective-permute-done.20 = f32[]{:T(128)} collective-permute-done((f32[]{:T(128)}, f32[]{:T(128)}, u32[]{:S(2)}, u32[]{:S(2)}) %collective-permute-start.20) | collective-permute-done | bytes 36 | tf_op jit(solution)/shard_map/ppermute | solution.py:56
  89.2 4.3 %collective-permute-done.21 = f32[]{:T(128)} collective-permute-done((f32[]{:T(128)}, f32[]{:T(128)}, u32[]{:S(2)}, u32[]{:S(2)}) %collective-permute-start.21) | collective-permute-done | bytes 36 | tf_op jit(solution)/shard_map/ppermute | solution.py:56
  94.2 0.2 broadcast_in_dim.48
  94.5 27.6 %psum.7 = f32[]{:T(128)} all-reduce(f32[]{:T(128)S(6)} %add.375), channel_id=1, replica_groups=mesh['island'=16,'inner'=16] {'inner'}, use_global_device_ids=true, to_apply=%region_1.2 | all-reduce | flops 1 | bytes 8 | tf_op jit(solution)/shard_map/psum | solution.py:62
  122.9 3.3 %collective-permute-start.25 = (f32[64,512]{1,0:T(8,128)S(1)}, f32[64,512]{1,0:T(8,128)S(1)}, u32[]{:S(2)}, u32[]{:S(2)}) collective-permute-start(f32[64,512]{1,0:T(8,128)S(1)} %collective-permute-done.23), channel_id=1, source_target_pairs={{0,112},{16,0},{32,16},{48,32},{64,48},{80,64},{96,80},{112,96},{1... | collective-permute-start | bytes 393224 | tf_op jit(solution)/shard_map/ppermute | solution.py:57
  126.2 2.8 %collective-permute-done.25 = f32[64,512]{1,0:T(8,128)S(1)} collective-permute-done((f32[64,512]{1,0:T(8,128)S(1)}, f32[64,512]{1,0:T(8,128)S(1)}, u32[]{:S(2)}, u32[]{:S(2)}) %collective-permute-start.25) | collective-permute-done | bytes 131104 | tf_op jit(solution)/shard_map/ppermute | solution.py:57
  129.0 2.5 %collective-permute-start.27 = (f32[64,512]{1,0:T(8,128)S(1)}, f32[64,512]{1,0:T(8,128)S(1)}, u32[]{:S(2)}, u32[]{:S(2)}) collective-permute-start(f32[64,512]{1,0:T(8,128)S(1)} %collective-permute-done.25), channel_id=1, source_target_pairs={{0,112},{16,0},{32,16},{48,32},{64,48},{80,64},{96,80},{112,96},{1... | collective-permute-start | bytes 393224 | tf_op jit(solution)/shard_map/ppermute | solution.py:57
  131.5 2.5 %collective-permute-done.27 = f32[64,512]{1,0:T(8,128)S(1)} collective-permute-done((f32[64,512]{1,0:T(8,128)S(1)}, f32[64,512]{1,0:T(8,128)S(1)}, u32[]{:S(2)}, u32[]{:S(2)}) %collective-permute-start.27) | collective-permute-done | bytes 131104 | tf_op jit(solution)/shard_map/ppermute | solution.py:57
  134.0 2.4 %collective-permute-start.29 = (f32[64,512]{1,0:T(8,128)S(1)}, f32[64,512]{1,0:T(8,128)S(1)}, u32[]{:S(2)}, u32[]{:S(2)}) collective-permute-start(f32[64,512]{1,0:T(8,128)S(1)} %collective-permute-done.27), channel_id=1, source_target_pairs={{0,112},{16,0},{32,16},{48,32},{64,48},{80,64},{96,80},{112,96},{1... | collective-permute-start | bytes 393224 | tf_op jit(solution)/shard_map/ppermute | solution.py:57
  136.5 2.8 %collective-permute-done.29 = f32[64,512]{1,0:T(8,128)S(1)} collective-permute-done((f32[64,512]{1,0:T(8,128)S(1)}, f32[64,512]{1,0:T(8,128)S(1)}, u32[]{:S(2)}, u32[]{:S(2)}) %collective-permute-start.29) | collective-permute-done | bytes 131104 | tf_op jit(solution)/shard_map/ppermute | solution.py:57
  139.4 2.3 %collective-permute-start.31 = (f32[64,512]{1,0:T(8,128)S(1)}, f32[64,512]{1,0:T(8,128)S(1)}, u32[]{:S(2)}, u32[]{:S(2)}) collective-permute-start(f32[64,512]{1,0:T(8,128)S(1)} %collective-permute-done.29), channel_id=1, source_target_pairs={{0,112},{16,0},{32,16},{48,32},{64,48},{80,64},{96,80},{112,96},{1... | collective-permute-start | bytes 393224 | tf_op jit(solution)/shard_map/ppermute | solution.py:57
  141.7 0.4 collective-permute-done.28
  142.1 0.4 collective-permute-start.30
  142.6 2.9 %collective-permute-done.31 = f32[64,512]{1,0:T(8,128)S(1)} collective-permute-done((f32[64,512]{1,0:T(8,128)S(1)}, f32[64,512]{1,0:T(8,128)S(1)}, u32[]{:S(2)}, u32[]{:S(2)}) %collective-permute-start.31) | collective-permute-done | bytes 131104 | tf_op jit(solution)/shard_map/ppermute | solution.py:57
  145.5 2.7 %collective-permute-start.33 = (f32[64,512]{1,0:T(8,128)S(1)}, f32[64,512]{1,0:T(8,128)S(1)}, u32[]{:S(2)}, u32[]{:S(2)}) collective-permute-start(f32[64,512]{1,0:T(8,128)S(1)} %collective-permute-done.31), channel_id=1, source_target_pairs={{0,112},{16,0},{32,16},{48,32},{64,48},{80,64},{96,80},{112,96},{1... | collective-permute-start | bytes 393224 | tf_op jit(solution)/shard_map/ppermute | solution.py:57
  148.2 0.5 collective-permute-done.30
  148.6 0.2 collective-permute-start.32
  148.8 3.8 %collective-permute-done.33 = f32[64,512]{1,0:T(8,128)S(1)} collective-permute-done((f32[64,512]{1,0:T(8,128)S(1)}, f32[64,512]{1,0:T(8,128)S(1)}, u32[]{:S(2)}, u32[]{:S(2)}) %collective-permute-start.33) | collective-permute-done | bytes 131104 | tf_op jit(solution)/shard_map/ppermute | solution.py:57
  152.6 3.0 %collective-permute-start.35 = (f32[64,512]{1,0:T(8,128)S(1)}, f32[64,512]{1,0:T(8,128)S(1)}, u32[]{:S(2)}, u32[]{:S(2)}) collective-permute-start(f32[64,512]{1,0:T(8,128)S(1)} %collective-permute-done.33), channel_id=1, source_target_pairs={{0,112},{16,0},{32,16},{48,32},{64,48},{80,64},{96,80},{112,96},{1... | collective-permute-start | bytes 393224 | tf_op jit(solution)/shard_map/ppermute | solution.py:57
  155.7 0.7 collective-permute-done.32
  156.5 5.8 %collective-permute-done.34 = f32[64,512]{1,0:T(8,128)S(1)} collective-permute-done((f32[64,512]{1,0:T(8,128)S(1)}, f32[64,512]{1,0:T(8,128)S(1)}, u32[]{:S(2)}, u32[]{:S(2)}) %collective-permute-start.34) | collective-permute-done | bytes 131104 | tf_op jit(solution)/shard_map/ppermute | solution.py:56
  162.4 0.2 broadcast_multiply_fusion
  162.6 1.3 copy-done
  164.0 0.6 copy-done.1
  164.6 2.8 %fusion.1 = (f32[2,512,512]{2,1,0:T(8,128)}, f32[2,512,512]{2,1,0:T(8,128)}) fusion(f32[2,512,512]{2,1,0:T(8,128)S(1)} %copy-done, f32[2,8,64,512]{3,2,1,0:T(8,128)S(1)} %broadcast_multiply_fusion, f32[2,512,512]{2,1,0:T(8,128)S(1)} %copy-done.1), kind=kLoop, calls=%fused_computation.3 | loop fusion | flops 3145728 | bytes 10485760 | tf_op jit(solution)/shard_map/sub | solution.py:16
  (51 shorter events, 0.8 us)
Async XLA Ops:
  2.4 5.3 %collective-permute-start = (f32[64,512]{1,0:T(8,128)S(1)}, f32[64,512]{1,0:T(8,128)S(1)}, u32[]{:S(2)}, u32[]{:S(2)}) collective-permute-start(f32[64,512]{1,0:T(8,128)S(1)} %dynamic-slice_bitcast_fusion.1), channel_id=1, source_target_pairs={{0,16},{16,32},{32,48},{48,64},{64,80},{80,96},{96,112},{112,0},{1... | collective-permute-start | bytes 393224 | tf_op jit(solution)/shard_map/ppermute | solution.py:42
  4.4 5.3 %collective-permute-start.7 = (f32[64,512]{1,0:T(8,128)S(1)}, f32[64,512]{1,0:T(8,128)S(1)}, u32[]{:S(2)}, u32[]{:S(2)}) collective-permute-start(f32[64,512]{1,0:T(8,128)S(1)} %dynamic-slice_bitcast_fusion), channel_id=1, source_target_pairs={{0,112},{16,0},{32,16},{48,32},{64,48},{80,64},{96,80},{112,96},{1... | collective-permute-start | bytes 393224 | tf_op jit(solution)/shard_map/ppermute | solution.py:43
  7.7 7.2 %collective-permute-start.1 = (f32[64,512]{1,0:T(8,128)S(1)}, f32[64,512]{1,0:T(8,128)S(1)}, u32[]{:S(2)}, u32[]{:S(2)}) collective-permute-start(f32[64,512]{1,0:T(8,128)S(1)} %bitcast_add_fusion.15), channel_id=1, source_target_pairs={{0,16},{16,32},{32,48},{48,64},{64,80},{80,96},{96,112},{112,0},{1... | collective-permute-start | bytes 393224 | tf_op jit(solution)/shard_map/ppermute | solution.py:42
  9.8 6.0 %collective-permute-start.8 = (f32[64,512]{1,0:T(8,128)S(1)}, f32[64,512]{1,0:T(8,128)S(1)}, u32[]{:S(2)}, u32[]{:S(2)}) collective-permute-start(f32[64,512]{1,0:T(8,128)S(1)} %bitcast_add_fusion.8), channel_id=1, source_target_pairs={{0,112},{16,0},{32,16},{48,32},{64,48},{80,64},{96,80},{112,96},{1... | collective-permute-start | bytes 393224 | tf_op jit(solution)/shard_map/ppermute | solution.py:43
  15.0 6.3 %collective-permute-start.2 = (f32[64,512]{1,0:T(8,128)S(1)}, f32[64,512]{1,0:T(8,128)S(1)}, u32[]{:S(2)}, u32[]{:S(2)}) collective-permute-start(f32[64,512]{1,0:T(8,128)S(1)} %bitcast_add_fusion.14), channel_id=1, source_target_pairs={{0,16},{16,32},{32,48},{48,64},{64,80},{80,96},{96,112},{112,0},{1... | collective-permute-start | bytes 393224 | tf_op jit(solution)/shard_map/ppermute | solution.py:42
  15.8 6.3 %collective-permute-start.9 = (f32[64,512]{1,0:T(8,128)S(1)}, f32[64,512]{1,0:T(8,128)S(1)}, u32[]{:S(2)}, u32[]{:S(2)}) collective-permute-start(f32[64,512]{1,0:T(8,128)S(1)} %bitcast_add_fusion.7), channel_id=1, source_target_pairs={{0,112},{16,0},{32,16},{48,32},{64,48},{80,64},{96,80},{112,96},{1... | collective-permute-start | bytes 393224 | tf_op jit(solution)/shard_map/ppermute | solution.py:43
  21.3 6.3 %collective-permute-start.3 = (f32[64,512]{1,0:T(8,128)S(1)}, f32[64,512]{1,0:T(8,128)S(1)}, u32[]{:S(2)}, u32[]{:S(2)}) collective-permute-start(f32[64,512]{1,0:T(8,128)S(1)} %bitcast_add_fusion.13), channel_id=1, source_target_pairs={{0,16},{16,32},{32,48},{48,64},{64,80},{80,96},{96,112},{112,0},{1... | collective-permute-start | bytes 393224 | tf_op jit(solution)/shard_map/ppermute | solution.py:42
  22.1 6.5 %collective-permute-start.10 = (f32[64,512]{1,0:T(8,128)S(1)}, f32[64,512]{1,0:T(8,128)S(1)}, u32[]{:S(2)}, u32[]{:S(2)}) collective-permute-start(f32[64,512]{1,0:T(8,128)S(1)} %bitcast_add_fusion.6), channel_id=1, source_target_pairs={{0,112},{16,0},{32,16},{48,32},{64,48},{80,64},{96,80},{112,96},{1... | collective-permute-start | bytes 393224 | tf_op jit(solution)/shard_map/ppermute | solution.py:43
  27.6 7.7 %collective-permute-start.4 = (f32[64,512]{1,0:T(8,128)S(1)}, f32[64,512]{1,0:T(8,128)S(1)}, u32[]{:S(2)}, u32[]{:S(2)}) collective-permute-start(f32[64,512]{1,0:T(8,128)S(1)} %bitcast_add_fusion.12), channel_id=1, source_target_pairs={{0,16},{16,32},{32,48},{48,64},{64,80},{80,96},{96,112},{112,0},{1... | collective-permute-start | bytes 393224 | tf_op jit(solution)/shard_map/ppermute | solution.py:42
  28.7 7.7 %collective-permute-start.11 = (f32[64,512]{1,0:T(8,128)S(1)}, f32[64,512]{1,0:T(8,128)S(1)}, u32[]{:S(2)}, u32[]{:S(2)}) collective-permute-start(f32[64,512]{1,0:T(8,128)S(1)} %bitcast_add_fusion.5), channel_id=1, source_target_pairs={{0,112},{16,0},{32,16},{48,32},{64,48},{80,64},{96,80},{112,96},{1... | collective-permute-start | bytes 393224 | tf_op jit(solution)/shard_map/ppermute | solution.py:43
  35.3 7.3 %collective-permute-start.5 = (f32[64,512]{1,0:T(8,128)S(1)}, f32[64,512]{1,0:T(8,128)S(1)}, u32[]{:S(2)}, u32[]{:S(2)}) collective-permute-start(f32[64,512]{1,0:T(8,128)S(1)} %bitcast_add_fusion.11), channel_id=1, source_target_pairs={{0,16},{16,32},{32,48},{48,64},{64,80},{80,96},{96,112},{112,0},{1... | collective-permute-start | bytes 393224 | tf_op jit(solution)/shard_map/ppermute | solution.py:42
  36.4 7.0 %collective-permute-start.12 = (f32[64,512]{1,0:T(8,128)S(1)}, f32[64,512]{1,0:T(8,128)S(1)}, u32[]{:S(2)}, u32[]{:S(2)}) collective-permute-start(f32[64,512]{1,0:T(8,128)S(1)} %bitcast_add_fusion.4), channel_id=1, source_target_pairs={{0,112},{16,0},{32,16},{48,32},{64,48},{80,64},{96,80},{112,96},{1... | collective-permute-start | bytes 393224 | tf_op jit(solution)/shard_map/ppermute | solution.py:43
  42.6 6.0 %collective-permute-start.6 = (f32[64,512]{1,0:T(8,128)S(1)}, f32[64,512]{1,0:T(8,128)S(1)}, u32[]{:S(2)}, u32[]{:S(2)}) collective-permute-start(f32[64,512]{1,0:T(8,128)S(1)} %bitcast_add_fusion.10), channel_id=1, source_target_pairs={{0,16},{16,32},{32,48},{48,64},{64,80},{80,96},{96,112},{112,0},{1... | collective-permute-start | bytes 393224 | tf_op jit(solution)/shard_map/ppermute | solution.py:42
  43.4 5.7 %collective-permute-start.13 = (f32[64,512]{1,0:T(8,128)S(1)}, f32[64,512]{1,0:T(8,128)S(1)}, u32[]{:S(2)}, u32[]{:S(2)}) collective-permute-start(f32[64,512]{1,0:T(8,128)S(1)} %bitcast_add_fusion.3), channel_id=1, source_target_pairs={{0,112},{16,0},{32,16},{48,32},{64,48},{80,64},{96,80},{112,96},{1... | collective-permute-start | bytes 393224 | tf_op jit(solution)/shard_map/ppermute | solution.py:43
  49.2 8.1 %collective-permute-start.14 = (f32[2,64,512]{2,1,0:T(8,128)S(1)}, f32[2,64,512]{2,1,0:T(8,128)S(1)}, u32[]{:S(2)}, u32[]{:S(2)}) collective-permute-start(f32[2,64,512]{2,1,0:T(8,128)S(1)} %pad_maximum_fusion), channel_id=1, source_target_pairs={{0,128},{16,144},{32,160},{48,176},{64,192},{80,208},{96,224},{112... | collective-permute-start | bytes 786440 | tf_op jit(solution)/shard_map/ppermute | solution.py:48
  58.0 6.5 %collective-permute-start.15 = (f32[]{:T(128)}, f32[]{:T(128)}, u32[]{:S(2)}, u32[]{:S(2)}) collective-permute-start(f32[]{:T(128)} %get-tuple-element.4), channel_id=1, source_target_pairs={{0,16},{16,32},{32,48},{48,64},{64,80},{80,96},{96,112},{112,0},{1... | collective-permute-start | bytes 20 | tf_op jit(solution)/shard_map/ppermute | solution.py:56
  61.3 61.6 %collective-permute-start.23 = (f32[64,512]{1,0:T(8,128)S(1)}, f32[64,512]{1,0:T(8,128)S(1)}, u32[]{:S(2)}, u32[]{:S(2)}) collective-permute-start(f32[64,512]{1,0:T(8,128)S(1)} %get-tuple-element.8), channel_id=1, source_target_pairs={{0,112},{16,0},{32,16},{48,32},{64,48},{80,64},{96,80},{112,96},{1... | collective-permute-start | bytes 393224 | tf_op jit(solution)/shard_map/ppermute | solution.py:57
  61.3 64.9 %collective-permute-start.22 = (f32[64,512]{1,0:T(8,128)S(1)}, f32[64,512]{1,0:T(8,128)S(1)}, u32[]{:S(2)}, u32[]{:S(2)}) collective-permute-start(f32[64,512]{1,0:T(8,128)S(1)} %get-tuple-element.9), channel_id=1, source_target_pairs={{0,16},{16,32},{32,48},{48,64},{64,80},{80,96},{96,112},{112,0},{1... | collective-permute-start | bytes 393224 | tf_op jit(solution)/shard_map/ppermute | solution.py:56
  65.9 3.8 %collective-permute-start.16 = (f32[]{:T(128)}, f32[]{:T(128)}, u32[]{:S(2)}, u32[]{:S(2)}) collective-permute-start(f32[]{:T(128)} %collective-permute-done.15), channel_id=1, source_target_pairs={{0,16},{16,32},{32,48},{48,64},{64,80},{80,96},{96,112},{112,0},{1... | collective-permute-start | bytes 20 | tf_op jit(solution)/shard_map/ppermute | solution.py:56
  69.7 4.1 %collective-permute-start.17 = (f32[]{:T(128)}, f32[]{:T(128)}, u32[]{:S(2)}, u32[]{:S(2)}) collective-permute-start(f32[]{:T(128)} %collective-permute-done.16), channel_id=1, source_target_pairs={{0,16},{16,32},{32,48},{48,64},{64,80},{80,96},{96,112},{112,0},{1... | collective-permute-start | bytes 20 | tf_op jit(solution)/shard_map/ppermute | solution.py:56
  73.8 4.9 %collective-permute-start.18 = (f32[]{:T(128)}, f32[]{:T(128)}, u32[]{:S(2)}, u32[]{:S(2)}) collective-permute-start(f32[]{:T(128)} %collective-permute-done.17), channel_id=1, source_target_pairs={{0,16},{16,32},{32,48},{48,64},{64,80},{80,96},{96,112},{112,0},{1... | collective-permute-start | bytes 20 | tf_op jit(solution)/shard_map/ppermute | solution.py:56
  78.7 4.9 %collective-permute-start.19 = (f32[]{:T(128)}, f32[]{:T(128)}, u32[]{:S(2)}, u32[]{:S(2)}) collective-permute-start(f32[]{:T(128)} %collective-permute-done.18), channel_id=1, source_target_pairs={{0,16},{16,32},{32,48},{48,64},{64,80},{80,96},{96,112},{112,0},{1... | collective-permute-start | bytes 20 | tf_op jit(solution)/shard_map/ppermute | solution.py:56
  83.7 4.9 %collective-permute-start.20 = (f32[]{:T(128)}, f32[]{:T(128)}, u32[]{:S(2)}, u32[]{:S(2)}) collective-permute-start(f32[]{:T(128)} %collective-permute-done.19), channel_id=1, source_target_pairs={{0,16},{16,32},{32,48},{48,64},{64,80},{80,96},{96,112},{112,0},{1... | collective-permute-start | bytes 20 | tf_op jit(solution)/shard_map/ppermute | solution.py:56
  88.6 4.9 %collective-permute-start.21 = (f32[]{:T(128)}, f32[]{:T(128)}, u32[]{:S(2)}, u32[]{:S(2)}) collective-permute-start(f32[]{:T(128)} %collective-permute-done.20), channel_id=1, source_target_pairs={{0,16},{16,32},{32,48},{48,64},{64,80},{80,96},{96,112},{112,0},{1... | collective-permute-start | bytes 20 | tf_op jit(solution)/shard_map/ppermute | solution.py:56
  122.9 6.1 %collective-permute-start.25 = (f32[64,512]{1,0:T(8,128)S(1)}, f32[64,512]{1,0:T(8,128)S(1)}, u32[]{:S(2)}, u32[]{:S(2)}) collective-permute-start(f32[64,512]{1,0:T(8,128)S(1)} %collective-permute-done.23), channel_id=1, source_target_pairs={{0,112},{16,0},{32,16},{48,32},{64,48},{80,64},{96,80},{112,96},{1... | collective-permute-start | bytes 393224 | tf_op jit(solution)/shard_map/ppermute | solution.py:57
  126.2 5.3 %collective-permute-start.24 = (f32[64,512]{1,0:T(8,128)S(1)}, f32[64,512]{1,0:T(8,128)S(1)}, u32[]{:S(2)}, u32[]{:S(2)}) collective-permute-start(f32[64,512]{1,0:T(8,128)S(1)} %collective-permute-done.22), channel_id=1, source_target_pairs={{0,16},{16,32},{32,48},{48,64},{64,80},{80,96},{96,112},{112,0},{1... | collective-permute-start | bytes 393224 | tf_op jit(solution)/shard_map/ppermute | solution.py:56
  129.0 5.0 %collective-permute-start.27 = (f32[64,512]{1,0:T(8,128)S(1)}, f32[64,512]{1,0:T(8,128)S(1)}, u32[]{:S(2)}, u32[]{:S(2)}) collective-permute-start(f32[64,512]{1,0:T(8,128)S(1)} %collective-permute-done.25), channel_id=1, source_target_pairs={{0,112},{16,0},{32,16},{48,32},{64,48},{80,64},{96,80},{112,96},{1... | collective-permute-start | bytes 393224 | tf_op jit(solution)/shard_map/ppermute | solution.py:57
  131.5 5.0 %collective-permute-start.26 = (f32[64,512]{1,0:T(8,128)S(1)}, f32[64,512]{1,0:T(8,128)S(1)}, u32[]{:S(2)}, u32[]{:S(2)}) collective-permute-start(f32[64,512]{1,0:T(8,128)S(1)} %collective-permute-done.24), channel_id=1, source_target_pairs={{0,16},{16,32},{32,48},{48,64},{64,80},{80,96},{96,112},{112,0},{1... | collective-permute-start | bytes 393224 | tf_op jit(solution)/shard_map/ppermute | solution.py:56
  134.0 5.3 %collective-permute-start.29 = (f32[64,512]{1,0:T(8,128)S(1)}, f32[64,512]{1,0:T(8,128)S(1)}, u32[]{:S(2)}, u32[]{:S(2)}) collective-permute-start(f32[64,512]{1,0:T(8,128)S(1)} %collective-permute-done.27), channel_id=1, source_target_pairs={{0,112},{16,0},{32,16},{48,32},{64,48},{80,64},{96,80},{112,96},{1... | collective-permute-start | bytes 393224 | tf_op jit(solution)/shard_map/ppermute | solution.py:57
  136.5 5.7 %collective-permute-start.28 = (f32[64,512]{1,0:T(8,128)S(1)}, f32[64,512]{1,0:T(8,128)S(1)}, u32[]{:S(2)}, u32[]{:S(2)}) collective-permute-start(f32[64,512]{1,0:T(8,128)S(1)} %collective-permute-done.26), channel_id=1, source_target_pairs={{0,16},{16,32},{32,48},{48,64},{64,80},{80,96},{96,112},{112,0},{1... | collective-permute-start | bytes 393224 | tf_op jit(solution)/shard_map/ppermute | solution.py:56
  139.4 6.1 %collective-permute-start.31 = (f32[64,512]{1,0:T(8,128)S(1)}, f32[64,512]{1,0:T(8,128)S(1)}, u32[]{:S(2)}, u32[]{:S(2)}) collective-permute-start(f32[64,512]{1,0:T(8,128)S(1)} %collective-permute-done.29), channel_id=1, source_target_pairs={{0,112},{16,0},{32,16},{48,32},{64,48},{80,64},{96,80},{112,96},{1... | collective-permute-start | bytes 393224 | tf_op jit(solution)/shard_map/ppermute | solution.py:57
  142.1 6.5 %collective-permute-start.30 = (f32[64,512]{1,0:T(8,128)S(1)}, f32[64,512]{1,0:T(8,128)S(1)}, u32[]{:S(2)}, u32[]{:S(2)}) collective-permute-start(f32[64,512]{1,0:T(8,128)S(1)} %collective-permute-done.28), channel_id=1, source_target_pairs={{0,16},{16,32},{32,48},{48,64},{64,80},{80,96},{96,112},{112,0},{1... | collective-permute-start | bytes 393224 | tf_op jit(solution)/shard_map/ppermute | solution.py:56
  145.5 7.1 %collective-permute-start.33 = (f32[64,512]{1,0:T(8,128)S(1)}, f32[64,512]{1,0:T(8,128)S(1)}, u32[]{:S(2)}, u32[]{:S(2)}) collective-permute-start(f32[64,512]{1,0:T(8,128)S(1)} %collective-permute-done.31), channel_id=1, source_target_pairs={{0,112},{16,0},{32,16},{48,32},{64,48},{80,64},{96,80},{112,96},{1... | collective-permute-start | bytes 393224 | tf_op jit(solution)/shard_map/ppermute | solution.py:57
  148.6 7.8 %collective-permute-start.32 = (f32[64,512]{1,0:T(8,128)S(1)}, f32[64,512]{1,0:T(8,128)S(1)}, u32[]{:S(2)}, u32[]{:S(2)}) collective-permute-start(f32[64,512]{1,0:T(8,128)S(1)} %collective-permute-done.30), channel_id=1, source_target_pairs={{0,16},{16,32},{32,48},{48,64},{64,80},{80,96},{96,112},{112,0},{1... | collective-permute-start | bytes 393224 | tf_op jit(solution)/shard_map/ppermute | solution.py:56
  152.6 9.7 %collective-permute-start.35 = (f32[64,512]{1,0:T(8,128)S(1)}, f32[64,512]{1,0:T(8,128)S(1)}, u32[]{:S(2)}, u32[]{:S(2)}) collective-permute-start(f32[64,512]{1,0:T(8,128)S(1)} %collective-permute-done.33), channel_id=1, source_target_pairs={{0,112},{16,0},{32,16},{48,32},{64,48},{80,64},{96,80},{112,96},{1... | collective-permute-start | bytes 393224 | tf_op jit(solution)/shard_map/ppermute | solution.py:57
  156.4 5.9 %collective-permute-start.34 = (f32[64,512]{1,0:T(8,128)S(1)}, f32[64,512]{1,0:T(8,128)S(1)}, u32[]{:S(2)}, u32[]{:S(2)}) collective-permute-start(f32[64,512]{1,0:T(8,128)S(1)} %collective-permute-done.32), channel_id=1, source_target_pairs={{0,16},{16,32},{32,48},{48,64},{64,80},{80,96},{96,112},{112,0},{1... | collective-permute-start | bytes 393224 | tf_op jit(solution)/shard_map/ppermute | solution.py:56
  162.4 1.6 copy-start
  162.4 2.2 %copy-start.1 = (f32[2,512,512]{2,1,0:T(8,128)S(1)}, f32[2,512,512]{2,1,0:T(8,128)}, u32[]{:S(2)}) copy-start(f32[2,512,512]{2,1,0:T(8,128)} %param.5) | copy-start | bytes 6291460

commit v3 on v2

--- a/solution.py
+++ b/solution.py
@@ -46,20 +46,25 @@
     mine = jnp.stack([acc_r, acc_l])
     partner = [(i, (i + RING) % islands) for i in range(islands)]
     mine = (mine + lax.ppermute(mine, "island", partner)) / islands
-    part_sq = jnp.sum(mine * mine)
+    sq = jnp.sum(mine * mine)
+    inner = lax.axis_size("inner")
+    flips = [("inner", [(i, i ^ bit) for i in range(inner)]) for bit in (1, 2, 4, 8)]
+    flips += [("island", [(g * RING + q, g * RING + (q ^ bit)) for g in range(islands // RING) for q in range(RING)])
+              for bit in (1, 2, 4)]
 
     out = jnp.zeros((halves, RING, chunk, cols), jnp.float32)
     out = lax.dynamic_update_index_in_dim(out, mine[:, None], z, axis=1)
-    sq = part_sq
-    cur_r, cur_l, cur_q = mine[0], mine[1], part_sq
+    cur_r, cur_l = mine[0], mine[1]
     for s in range(RING - 1):
-        cur_r, cur_q = lax.ppermute((cur_r, cur_q), "island", right)
+        cur_r = lax.ppermute(cur_r, "island", right)
         cur_l = lax.ppermute(cur_l, "island", left)
-        sq = sq + cur_q
+        axis, pairs = flips[s]
+        sq = sq + lax.ppermute(sq, axis, pairs)
+        cur_r, cur_l, sq = lax.optimization_barrier((cur_r, cur_l, sq))
         out = lax.dynamic_update_slice(out, cur_r[None, None], (0, (z - 1 - s) % RING, 0, 0))
         out = lax.dynamic_update_slice(out, cur_l[None, None], (1, (z + 1 + s) % RING, 0, 0))
+    total_sq = sq
     average = out.reshape(halves, rows, cols)
-    total_sq = lax.psum(sq, "inner")
     return outer_update(average, params, momentum, total_sq / count)
 
 

time: 171 us -> 137 us (0.80); the launches traced: 167 us -> 136 us
  blocking collectives: 27.6 us -> 0 us
  waiting for transfers between devices: 71.2 us -> 59 us
  starting transfers between devices: 53.3 us -> 62.9 us
    psum x1 -> x0, blocking collectives: 27.6 us -> none  [body(): total_sq = lax.psum(sq, 'inner')]
    ppermute x14, waiting for transfers between devices: 25.7 us -> 6.67 us  [the longest x7 4.14 us: body(): sq = sq + lax.ppermute(sq, axis, pairs)]
    ppermute x14, starting transfers between devices: 13.4 us -> 29.8 us  [the longest x7 19.4 us: body(): sq = sq + lax.ppermute(sq, axis, pairs)]
    ppermute x7, starting transfers between devices: 16.3 us -> 9.45 us  [body(): cur_l = lax.ppermute(cur_l, 'island', left)]
    ppermute x7, waiting for transfers between devices: 14.8 us -> 21.6 us  [body(): cur_l = lax.ppermute(cur_l, 'island', left)]
  transfers between devices with their start and end apart: 36 -> 36, of which waited for: 29 -> 27; matrix products, arithmetic and copies ran while one was open for 0% -> 0% of each run, Pallas kernels for 0% -> 0%
where the time goes in v3:
time: 137 us; the launch traced here: 136 us
  starting transfers between devices  62.9 us (46%)
  waiting for transfers between devices  59 us (43%)
  between operations  5.83 us (4%)
  local copies, waits for them, and re-layouts  4.18 us (3%)
  other arithmetic  3.98 us (3%)
    ppermute x7, waiting for transfers between devices, body(): got_r = lax.ppermute(acc_r, 'island', right)  21.8 us
    ppermute x7, waiting for transfers between devices, body(): cur_l = lax.ppermute(cur_l, 'island', left)  21.6 us
    ppermute x7, starting transfers between devices, body(): sq = sq + lax.ppermute(sq, axis, pairs)  19.4 us
    ppermute x7, starting transfers between devices, body(): got_l = lax.ppermute(acc_l, 'island', left)  15.4 us
    ppermute x7, starting transfers between devices, body(): cur_r = lax.ppermute(cur_r, 'island', right)  10.4 us
    ppermute x7, starting transfers between devices, body(): cur_l = lax.ppermute(cur_l, 'island', left)  9.45 us
    ppermute x7, starting transfers between devices, body(): got_r = lax.ppermute(acc_r, 'island', right)  4.81 us
    ppermute x1, waiting for transfers between devices, body(): mine = (mine + lax.ppermute(mine, 'island', partner)) / islands  4.69 us
  transfers between devices with their start and end apart: 36, of which 27 were waited for; matrix products, arithmetic and copies ran while one was open for 0% of the time, Pallas kernels for 0%

profile of v3, /device:TPU:32, one launch (start us, length us, event | category | flops | bytes accessed | tf_op | source)
XLA Modules:
  0.0 135.9 jit_solution(12680725873936944811)
XLA Ops:
  0.7 1.7 %fusion.4 = (f32[1,1,512,512]{3,2,1,0:T(8,128)S(1)}, f32[1,1,512,512]{3,2,1,0:T(8,128)S(1)}) fusion(f32[1,2,512,512]{3,2,1,0:T(8,128)} %param.3), kind=kLoop, calls=%fused_computation.43 | loop fusion | bytes 4194304 | tf_op jit(solution)/shard_map/slice | solution.py:37
  2.4 2.0 %collective-permute-start = (f32[64,512]{1,0:T(8,128)S(1)}, f32[64,512]{1,0:T(8,128)S(1)}, u32[]{:S(2)}, u32[]{:S(2)}) collective-permute-start(f32[64,512]{1,0:T(8,128)S(1)} %dynamic-slice_bitcast_fusion.1), channel_id=1, source_target_pairs={{0,16},{16,32},{32,48},{48,64},{64,80},{80,96},{96,112},{112,0},{1... | collective-permute-start | bytes 393224 | tf_op jit(solution)/shard_map/ppermute | solution.py:42
  4.4 0.2 collective-permute-start.7
  4.8 2.9 %collective-permute-done = f32[64,512]{1,0:T(8,128)S(1)} collective-permute-done((f32[64,512]{1,0:T(8,128)S(1)}, f32[64,512]{1,0:T(8,128)S(1)}, u32[]{:S(2)}, u32[]{:S(2)}) %collective-permute-start) | collective-permute-done | bytes 131104 | tf_op jit(solution)/shard_map/ppermute | solution.py:42
  7.7 2.0 %collective-permute-start.1 = (f32[64,512]{1,0:T(8,128)S(1)}, f32[64,512]{1,0:T(8,128)S(1)}, u32[]{:S(2)}, u32[]{:S(2)}) collective-permute-start(f32[64,512]{1,0:T(8,128)S(1)} %bitcast_add_fusion.15), channel_id=1, source_target_pairs={{0,16},{16,32},{32,48},{48,64},{64,80},{80,96},{96,112},{112,0},{1... | collective-permute-start | bytes 393224 | tf_op jit(solution)/shard_map/ppermute | solution.py:42
  9.8 2.4 %collective-permute-start.8 = (f32[64,512]{1,0:T(8,128)S(1)}, f32[64,512]{1,0:T(8,128)S(1)}, u32[]{:S(2)}, u32[]{:S(2)}) collective-permute-start(f32[64,512]{1,0:T(8,128)S(1)} %bitcast_add_fusion.8), channel_id=1, source_target_pairs={{0,112},{16,0},{32,16},{48,32},{64,48},{80,64},{96,80},{112,96},{1... | collective-permute-start | bytes 393224 | tf_op jit(solution)/shard_map/ppermute | solution.py:43
  12.2 2.8 %collective-permute-done.1 = f32[64,512]{1,0:T(8,128)S(1)} collective-permute-done((f32[64,512]{1,0:T(8,128)S(1)}, f32[64,512]{1,0:T(8,128)S(1)}, u32[]{:S(2)}, u32[]{:S(2)}) %collective-permute-start.1) | collective-permute-done | bytes 131104 | tf_op jit(solution)/shard_map/ppermute | solution.py:42
  15.1 0.7 collective-permute-done.8
  15.8 2.6 %collective-permute-start.9 = (f32[64,512]{1,0:T(8,128)S(1)}, f32[64,512]{1,0:T(8,128)S(1)}, u32[]{:S(2)}, u32[]{:S(2)}) collective-permute-start(f32[64,512]{1,0:T(8,128)S(1)} %bitcast_add_fusion.7), channel_id=1, source_target_pairs={{0,112},{16,0},{32,16},{48,32},{64,48},{80,64},{96,80},{112,96},{1... | collective-permute-start | bytes 393224 | tf_op jit(solution)/shard_map/ppermute | solution.py:43
  18.5 2.8 %collective-permute-done.2 = f32[64,512]{1,0:T(8,128)S(1)} collective-permute-done((f32[64,512]{1,0:T(8,128)S(1)}, f32[64,512]{1,0:T(8,128)S(1)}, u32[]{:S(2)}, u32[]{:S(2)}) %collective-permute-start.2) | collective-permute-done | bytes 131104 | tf_op jit(solution)/shard_map/ppermute | solution.py:42
  21.4 0.7 collective-permute-done.9
  22.1 2.6 %collective-permute-start.10 = (f32[64,512]{1,0:T(8,128)S(1)}, f32[64,512]{1,0:T(8,128)S(1)}, u32[]{:S(2)}, u32[]{:S(2)}) collective-permute-start(f32[64,512]{1,0:T(8,128)S(1)} %bitcast_add_fusion.6), channel_id=1, source_target_pairs={{0,112},{16,0},{32,16},{48,32},{64,48},{80,64},{96,80},{112,96},{1... | collective-permute-start | bytes 393224 | tf_op jit(solution)/shard_map/ppermute | solution.py:43
  24.7 2.8 %collective-permute-done.3 = f32[64,512]{1,0:T(8,128)S(1)} collective-permute-done((f32[64,512]{1,0:T(8,128)S(1)}, f32[64,512]{1,0:T(8,128)S(1)}, u32[]{:S(2)}, u32[]{:S(2)}) %collective-permute-start.3) | collective-permute-done | bytes 131104 | tf_op jit(solution)/shard_map/ppermute | solution.py:42
  27.6 0.2 collective-permute-start.4
  27.7 0.9 collective-permute-done.10
  28.7 2.6 %collective-permute-start.11 = (f32[64,512]{1,0:T(8,128)S(1)}, f32[64,512]{1,0:T(8,128)S(1)}, u32[]{:S(2)}, u32[]{:S(2)}) collective-permute-start(f32[64,512]{1,0:T(8,128)S(1)} %bitcast_add_fusion.5), channel_id=1, source_target_pairs={{0,112},{16,0},{32,16},{48,32},{64,48},{80,64},{96,80},{112,96},{1... | collective-permute-start | bytes 393224 | tf_op jit(solution)/shard_map/ppermute | solution.py:43
  31.3 4.0 %collective-permute-done.4 = f32[64,512]{1,0:T(8,128)S(1)} collective-permute-done((f32[64,512]{1,0:T(8,128)S(1)}, f32[64,512]{1,0:T(8,128)S(1)}, u32[]{:S(2)}, u32[]{:S(2)}) %collective-permute-start.4) | collective-permute-done | bytes 131104 | tf_op jit(solution)/shard_map/ppermute | solution.py:42
  35.3 0.4 collective-permute-start.5
  35.7 0.7 collective-permute-done.11
  36.4 2.6 %collective-permute-start.12 = (f32[64,512]{1,0:T(8,128)S(1)}, f32[64,512]{1,0:T(8,128)S(1)}, u32[]{:S(2)}, u32[]{:S(2)}) collective-permute-start(f32[64,512]{1,0:T(8,128)S(1)} %bitcast_add_fusion.4), channel_id=1, source_target_pairs={{0,112},{16,0},{32,16},{48,32},{64,48},{80,64},{96,80},{112,96},{1... | collective-permute-start | bytes 393224 | tf_op jit(solution)/shard_map/ppermute | solution.py:43
  38.9 3.6 %collective-permute-done.5 = f32[64,512]{1,0:T(8,128)S(1)} collective-permute-done((f32[64,512]{1,0:T(8,128)S(1)}, f32[64,512]{1,0:T(8,128)S(1)}, u32[]{:S(2)}, u32[]{:S(2)}) %collective-permute-start.5) | collective-permute-done | bytes 131104 | tf_op jit(solution)/shard_map/ppermute | solution.py:42
  42.7 0.7 collective-permute-done.12
  43.4 2.3 %collective-permute-start.13 = (f32[64,512]{1,0:T(8,128)S(1)}, f32[64,512]{1,0:T(8,128)S(1)}, u32[]{:S(2)}, u32[]{:S(2)}) collective-permute-start(f32[64,512]{1,0:T(8,128)S(1)} %bitcast_add_fusion.3), channel_id=1, source_target_pairs={{0,112},{16,0},{32,16},{48,32},{64,48},{80,64},{96,80},{112,96},{1... | collective-permute-start | bytes 393224 | tf_op jit(solution)/shard_map/ppermute | solution.py:43
  45.7 2.8 %collective-permute-done.6 = f32[64,512]{1,0:T(8,128)S(1)} collective-permute-done((f32[64,512]{1,0:T(8,128)S(1)}, f32[64,512]{1,0:T(8,128)S(1)}, u32[]{:S(2)}, u32[]{:S(2)}) %collective-permute-start.6) | collective-permute-done | bytes 131104 | tf_op jit(solution)/shard_map/ppermute | solution.py:42
  48.6 0.5 collective-permute-done.13
  49.2 3.5 %collective-permute-start.14 = (f32[2,64,512]{2,1,0:T(8,128)S(1)}, f32[2,64,512]{2,1,0:T(8,128)S(1)}, u32[]{:S(2)}, u32[]{:S(2)}) collective-permute-start(f32[2,64,512]{2,1,0:T(8,128)S(1)} %pad_maximum_fusion), channel_id=1, source_target_pairs={{0,128},{16,144},{32,160},{48,176},{64,192},{80,208},{96,224},{112... | collective-permute-start | bytes 786440 | tf_op jit(solution)/shard_map/ppermute | solution.py:48
  52.6 4.7 %collective-permute-done.14 = f32[2,64,512]{2,1,0:T(8,128)S(1)} collective-permute-done((f32[2,64,512]{2,1,0:T(8,128)S(1)}, f32[2,64,512]{2,1,0:T(8,128)S(1)}, u32[]{:S(2)}, u32[]{:S(2)}) %collective-permute-start.14) | collective-permute-done | bytes 262176 | tf_op jit(solution)/shard_map/ppermute | solution.py:48
  57.3 0.7 multiply_reduce_fusion
  58.1 2.8 %collective-permute-start.16 = (f32[64,512]{1,0:T(8,128)S(1)}, f32[64,512]{1,0:T(8,128)S(1)}, u32[]{:S(2)}, u32[]{:S(2)}) collective-permute-start(f32[64,512]{1,0:T(8,128)S(1)} %get-tuple-element.50), channel_id=1, source_target_pairs={{0,112},{16,0},{32,16},{48,32},{64,48},{80,64},{96,80},{112,96},{1... | collective-permute-start | bytes 393224 | tf_op jit(solution)/shard_map/ppermute | solution.py:60
  60.9 0.6 collective-permute-start.15
  61.5 0.2 broadcast_in_dim.48
  63.0 2.5 %collective-permute-done.16 = f32[64,512]{1,0:T(8,128)S(1)} collective-permute-done((f32[64,512]{1,0:T(8,128)S(1)}, f32[64,512]{1,0:T(8,128)S(1)}, u32[]{:S(2)}, u32[]{:S(2)}) %collective-permute-start.16) | collective-permute-done | bytes 131104 | tf_op jit(solution)/shard_map/ppermute | solution.py:60
  65.5 2.5 %collective-permute-done.15 = f32[64,512]{1,0:T(8,128)S(1)} collective-permute-done((f32[64,512]{1,0:T(8,128)S(1)}, f32[64,512]{1,0:T(8,128)S(1)}, u32[]{:S(2)}, u32[]{:S(2)}) %collective-permute-start.15) | collective-permute-done | bytes 131104 | tf_op jit(solution)/shard_map/ppermute | solution.py:59
  68.0 0.7 collective-permute-start.18
  68.7 2.9 %collective-permute-start.20 = (f32[]{:T(128)}, f32[]{:T(128)}, u32[]{:S(2)}, u32[]{:S(2)}) collective-permute-start(f32[]{:T(128)} %add.367), channel_id=1, source_target_pairs={{0,2},{1,3},{2,0},{3,1},{4,6},{5,7},{6,4},{7,5},{8,10},{9,11},{10,... | collective-permute-start | bytes 20 | tf_op jit(solution)/shard_map/ppermute | solution.py:62
  71.6 2.2 %collective-permute-start.19 = (f32[64,512]{1,0:T(8,128)S(1)}, f32[64,512]{1,0:T(8,128)S(1)}, u32[]{:S(2)}, u32[]{:S(2)}) collective-permute-start(f32[64,512]{1,0:T(8,128)S(1)} %collective-permute-done.16), channel_id=1, source_target_pairs={{0,112},{16,0},{32,16},{48,32},{64,48},{80,64},{96,80},{112,96},{1... | collective-permute-start | bytes 393224 | tf_op jit(solution)/shard_map/ppermute | solution.py:60
  74.4 3.1 %collective-permute-done.19 = f32[64,512]{1,0:T(8,128)S(1)} collective-permute-done((f32[64,512]{1,0:T(8,128)S(1)}, f32[64,512]{1,0:T(8,128)S(1)}, u32[]{:S(2)}, u32[]{:S(2)}) %collective-permute-start.19) | collective-permute-done | bytes 131104 | tf_op jit(solution)/shard_map/ppermute | solution.py:60
  77.5 3.0 %collective-permute-start.21 = (f32[64,512]{1,0:T(8,128)S(1)}, f32[64,512]{1,0:T(8,128)S(1)}, u32[]{:S(2)}, u32[]{:S(2)}) collective-permute-start(f32[64,512]{1,0:T(8,128)S(1)} %collective-permute-done.18), channel_id=1, source_target_pairs={{0,16},{16,32},{32,48},{48,64},{64,80},{80,96},{96,112},{112,0},{1... | collective-permute-start | bytes 393224 | tf_op jit(solution)/shard_map/ppermute | solution.py:59
  80.5 4.1 %collective-permute-start.23 = (f32[]{:T(128)}, f32[]{:T(128)}, u32[]{:S(2)}, u32[]{:S(2)}) collective-permute-start(f32[]{:T(128)} %add.368), channel_id=1, source_target_pairs={{0,4},{1,5},{2,6},{3,7},{4,0},{5,1},{6,2},{7,3},{8,12},{9,13},{10,... | collective-permute-start | bytes 20 | tf_op jit(solution)/shard_map/ppermute | solution.py:62
  84.6 1.1 collective-permute-done.23
  86.3 4.4 %collective-permute-done.22 = f32[64,512]{1,0:T(8,128)S(1)} collective-permute-done((f32[64,512]{1,0:T(8,128)S(1)}, f32[64,512]{1,0:T(8,128)S(1)}, u32[]{:S(2)}, u32[]{:S(2)}) %collective-permute-start.22) | collective-permute-done | bytes 131104 | tf_op jit(solution)/shard_map/ppermute | solution.py:60
  90.8 2.0 %collective-permute-start.24 = (f32[64,512]{1,0:T(8,128)S(1)}, f32[64,512]{1,0:T(8,128)S(1)}, u32[]{:S(2)}, u32[]{:S(2)}) collective-permute-start(f32[64,512]{1,0:T(8,128)S(1)} %collective-permute-done.21), channel_id=1, source_target_pairs={{0,16},{16,32},{32,48},{48,64},{64,80},{80,96},{96,112},{112,0},{1... | collective-permute-start | bytes 393224 | tf_op jit(solution)/shard_map/ppermute | solution.py:59
  92.8 3.3 %collective-permute-start.26 = (f32[]{:T(128)}, f32[]{:T(128)}, u32[]{:S(2)}, u32[]{:S(2)}) collective-permute-start(f32[]{:T(128)} %add.369), channel_id=1, source_target_pairs={{0,8},{1,9},{2,10},{3,11},{4,12},{5,13},{6,14},{7,15},{8,0},{9,1},... | collective-permute-start | bytes 20 | tf_op jit(solution)/shard_map/ppermute | solution.py:62
  96.2 0.4 collective-permute-done.26
  97.1 4.6 %collective-permute-done.25 = f32[64,512]{1,0:T(8,128)S(1)} collective-permute-done((f32[64,512]{1,0:T(8,128)S(1)}, f32[64,512]{1,0:T(8,128)S(1)}, u32[]{:S(2)}, u32[]{:S(2)}) %collective-permute-start.25) | collective-permute-done | bytes 131104 | tf_op jit(solution)/shard_map/ppermute | solution.py:60
  101.7 1.7 %collective-permute-start.27 = (f32[64,512]{1,0:T(8,128)S(1)}, f32[64,512]{1,0:T(8,128)S(1)}, u32[]{:S(2)}, u32[]{:S(2)}) collective-permute-start(f32[64,512]{1,0:T(8,128)S(1)} %collective-permute-done.24), channel_id=1, source_target_pairs={{0,16},{16,32},{32,48},{48,64},{64,80},{80,96},{96,112},{112,0},{1... | collective-permute-start | bytes 393224 | tf_op jit(solution)/shard_map/ppermute | solution.py:59
  103.5 1.7 %collective-permute-start.29 = (f32[]{:T(128)}, f32[]{:T(128)}, u32[]{:S(2)}, u32[]{:S(2)}) collective-permute-start(f32[]{:T(128)} %add.370), channel_id=1, source_target_pairs={{0,16},{16,0},{32,48},{48,32},{64,80},{80,64},{96,112},{112,96},{1... | collective-permute-start | bytes 20 | tf_op jit(solution)/shard_map/ppermute | solution.py:62
  105.1 1.7 %collective-permute-start.28 = (f32[64,512]{1,0:T(8,128)S(1)}, f32[64,512]{1,0:T(8,128)S(1)}, u32[]{:S(2)}, u32[]{:S(2)}) collective-permute-start(f32[64,512]{1,0:T(8,128)S(1)} %collective-permute-done.25), channel_id=1, source_target_pairs={{0,112},{16,0},{32,16},{48,32},{64,48},{80,64},{96,80},{112,96},{1... | collective-permute-start | bytes 393224 | tf_op jit(solution)/shard_map/ppermute | solution.py:60
  106.9 0.3 collective-permute-done.29
  107.8 3.3 %collective-permute-done.28 = f32[64,512]{1,0:T(8,128)S(1)} collective-permute-done((f32[64,512]{1,0:T(8,128)S(1)}, f32[64,512]{1,0:T(8,128)S(1)}, u32[]{:S(2)}, u32[]{:S(2)}) %collective-permute-start.28) | collective-permute-done | bytes 131104 | tf_op jit(solution)/shard_map/ppermute | solution.py:60
  111.1 1.4 %collective-permute-start.30 = (f32[64,512]{1,0:T(8,128)S(1)}, f32[64,512]{1,0:T(8,128)S(1)}, u32[]{:S(2)}, u32[]{:S(2)}) collective-permute-start(f32[64,512]{1,0:T(8,128)S(1)} %collective-permute-done.27), channel_id=1, source_target_pairs={{0,16},{16,32},{32,48},{48,64},{64,80},{80,96},{96,112},{112,0},{1... | collective-permute-start | bytes 393224 | tf_op jit(solution)/shard_map/ppermute | solution.py:59
  112.5 2.5 %collective-permute-start.32 = (f32[]{:T(128)}, f32[]{:T(128)}, u32[]{:S(2)}, u32[]{:S(2)}) collective-permute-start(f32[]{:T(128)} %add.371), channel_id=1, source_target_pairs={{0,32},{16,48},{32,0},{48,16},{64,96},{80,112},{96,64},{112,80},{1... | collective-permute-start | bytes 20 | tf_op jit(solution)/shard_map/ppermute | solution.py:62
  115.0 1.8 %collective-permute-start.31 = (f32[64,512]{1,0:T(8,128)S(1)}, f32[64,512]{1,0:T(8,128)S(1)}, u32[]{:S(2)}, u32[]{:S(2)}) collective-permute-start(f32[64,512]{1,0:T(8,128)S(1)} %collective-permute-done.28), channel_id=1, source_target_pairs={{0,112},{16,0},{32,16},{48,32},{64,48},{80,64},{96,80},{112,96},{1... | collective-permute-start | bytes 393224 | tf_op jit(solution)/shard_map/ppermute | solution.py:60
  116.8 0.3 collective-permute-done.32
  117.7 2.3 %collective-permute-done.31 = f32[64,512]{1,0:T(8,128)S(1)} collective-permute-done((f32[64,512]{1,0:T(8,128)S(1)}, f32[64,512]{1,0:T(8,128)S(1)}, u32[]{:S(2)}, u32[]{:S(2)}) %collective-permute-start.31) | collective-permute-done | bytes 131104 | tf_op jit(solution)/shard_map/ppermute | solution.py:60
  120.0 1.0 collective-permute-start.33
  121.0 4.8 %collective-permute-start.35 = (f32[]{:T(128)}, f32[]{:T(128)}, u32[]{:S(2)}, u32[]{:S(2)}) collective-permute-start(f32[]{:T(128)} %add.372), channel_id=1, source_target_pairs={{0,64},{16,80},{32,96},{48,112},{64,0},{80,16},{96,32},{112,48},{1... | collective-permute-start | bytes 20 | tf_op jit(solution)/shard_map/ppermute | solution.py:62
  125.8 0.9 collective-permute-start.34
  126.7 1.9 %collective-permute-done.35 = f32[]{:T(128)} collective-permute-done((f32[]{:T(128)}, f32[]{:T(128)}, u32[]{:S(2)}, u32[]{:S(2)}) %collective-permute-start.35) | collective-permute-done | bytes 36 | tf_op jit(solution)/shard_map/ppermute | solution.py:62
  129.2 1.5 %collective-permute-done.34 = f32[64,512]{1,0:T(8,128)S(1)} collective-permute-done((f32[64,512]{1,0:T(8,128)S(1)}, f32[64,512]{1,0:T(8,128)S(1)}, u32[]{:S(2)}, u32[]{:S(2)}) %collective-permute-start.34) | collective-permute-done | bytes 131104 | tf_op jit(solution)/shard_map/ppermute | solution.py:60
  130.9 0.2 broadcast_multiply_fusion
  131.1 1.3 copy-done
  132.4 0.6 copy-done.1
  133.1 2.8 %fusion.1 = (f32[2,512,512]{2,1,0:T(8,128)}, f32[2,512,512]{2,1,0:T(8,128)}) fusion(f32[2,512,512]{2,1,0:T(8,128)S(1)} %copy-done, f32[2,8,64,512]{3,2,1,0:T(8,128)S(1)} %broadcast_multiply_fusion, f32[2,512,512]{2,1,0:T(8,128)S(1)} %copy-done.1), kind=kLoop, calls=%fused_computation.3 | loop fusion | flops 3145728 | bytes 10485760 | tf_op jit(solution)/shard_map/sub | solution.py:16
  (50 shorter events, 0.9 us)
Async XLA Ops:
  2.4 5.3 %collective-permute-start = (f32[64,512]{1,0:T(8,128)S(1)}, f32[64,512]{1,0:T(8,128)S(1)}, u32[]{:S(2)}, u32[]{:S(2)}) collective-permute-start(f32[64,512]{1,0:T(8,128)S(1)} %dynamic-slice_bitcast_fusion.1), channel_id=1, source_target_pairs={{0,16},{16,32},{32,48},{48,64},{64,80},{80,96},{96,112},{112,0},{1... | collective-permute-start | bytes 393224 | tf_op jit(solution)/shard_map/ppermute | solution.py:42
  4.4 5.3 %collective-permute-start.7 = (f32[64,512]{1,0:T(8,128)S(1)}, f32[64,512]{1,0:T(8,128)S(1)}, u32[]{:S(2)}, u32[]{:S(2)}) collective-permute-start(f32[64,512]{1,0:T(8,128)S(1)} %dynamic-slice_bitcast_fusion), channel_id=1, source_target_pairs={{0,112},{16,0},{32,16},{48,32},{64,48},{80,64},{96,80},{112,96},{1... | collective-permute-start | bytes 393224 | tf_op jit(solution)/shard_map/ppermute | solution.py:43
  7.7 7.2 %collective-permute-start.1 = (f32[64,512]{1,0:T(8,128)S(1)}, f32[64,512]{1,0:T(8,128)S(1)}, u32[]{:S(2)}, u32[]{:S(2)}) collective-permute-start(f32[64,512]{1,0:T(8,128)S(1)} %bitcast_add_fusion.15), channel_id=1, source_target_pairs={{0,16},{16,32},{32,48},{48,64},{64,80},{80,96},{96,112},{112,0},{1... | collective-permute-start | bytes 393224 | tf_op jit(solution)/shard_map/ppermute | solution.py:42
  9.8 6.0 %collective-permute-start.8 = (f32[64,512]{1,0:T(8,128)S(1)}, f32[64,512]{1,0:T(8,128)S(1)}, u32[]{:S(2)}, u32[]{:S(2)}) collective-permute-start(f32[64,512]{1,0:T(8,128)S(1)} %bitcast_add_fusion.8), channel_id=1, source_target_pairs={{0,112},{16,0},{32,16},{48,32},{64,48},{80,64},{96,80},{112,96},{1... | collective-permute-start | bytes 393224 | tf_op jit(solution)/shard_map/ppermute | solution.py:43
  15.0 6.3 %collective-permute-start.2 = (f32[64,512]{1,0:T(8,128)S(1)}, f32[64,512]{1,0:T(8,128)S(1)}, u32[]{:S(2)}, u32[]{:S(2)}) collective-permute-start(f32[64,512]{1,0:T(8,128)S(1)} %bitcast_add_fusion.14), channel_id=1, source_target_pairs={{0,16},{16,32},{32,48},{48,64},{64,80},{80,96},{96,112},{112,0},{1... | collective-permute-start | bytes 393224 | tf_op jit(solution)/shard_map/ppermute | solution.py:42
  15.8 6.3 %collective-permute-start.9 = (f32[64,512]{1,0:T(8,128)S(1)}, f32[64,512]{1,0:T(8,128)S(1)}, u32[]{:S(2)}, u32[]{:S(2)}) collective-permute-start(f32[64,512]{1,0:T(8,128)S(1)} %bitcast_add_fusion.7), channel_id=1, source_target_pairs={{0,112},{16,0},{32,16},{48,32},{64,48},{80,64},{96,80},{112,96},{1... | collective-permute-start | bytes 393224 | tf_op jit(solution)/shard_map/ppermute | solution.py:43
  21.3 6.3 %collective-permute-start.3 = (f32[64,512]{1,0:T(8,128)S(1)}, f32[64,512]{1,0:T(8,128)S(1)}, u32[]{:S(2)}, u32[]{:S(2)}) collective-permute-start(f32[64,512]{1,0:T(8,128)S(1)} %bitcast_add_fusion.13), channel_id=1, source_target_pairs={{0,16},{16,32},{32,48},{48,64},{64,80},{80,96},{96,112},{112,0},{1... | collective-permute-start | bytes 393224 | tf_op jit(solution)/shard_map/ppermute | solution.py:42
  22.1 6.5 %collective-permute-start.10 = (f32[64,512]{1,0:T(8,128)S(1)}, f32[64,512]{1,0:T(8,128)S(1)}, u32[]{:S(2)}, u32[]{:S(2)}) collective-permute-start(f32[64,512]{1,0:T(8,128)S(1)} %bitcast_add_fusion.6), channel_id=1, source_target_pairs={{0,112},{16,0},{32,16},{48,32},{64,48},{80,64},{96,80},{112,96},{1... | collective-permute-start | bytes 393224 | tf_op jit(solution)/shard_map/ppermute | solution.py:43
  27.6 7.7 %collective-permute-start.4 = (f32[64,512]{1,0:T(8,128)S(1)}, f32[64,512]{1,0:T(8,128)S(1)}, u32[]{:S(2)}, u32[]{:S(2)}) collective-permute-start(f32[64,512]{1,0:T(8,128)S(1)} %bitcast_add_fusion.12), channel_id=1, source_target_pairs={{0,16},{16,32},{32,48},{48,64},{64,80},{80,96},{96,112},{112,0},{1... | collective-permute-start | bytes 393224 | tf_op jit(solution)/shard_map/ppermute | solution.py:42
  28.7 7.7 %collective-permute-start.11 = (f32[64,512]{1,0:T(8,128)S(1)}, f32[64,512]{1,0:T(8,128)S(1)}, u32[]{:S(2)}, u32[]{:S(2)}) collective-permute-start(f32[64,512]{1,0:T(8,128)S(1)} %bitcast_add_fusion.5), channel_id=1, source_target_pairs={{0,112},{16,0},{32,16},{48,32},{64,48},{80,64},{96,80},{112,96},{1... | collective-permute-start | bytes 393224 | tf_op jit(solution)/shard_map/ppermute | solution.py:43
  35.3 7.3 %collective-permute-start.5 = (f32[64,512]{1,0:T(8,128)S(1)}, f32[64,512]{1,0:T(8,128)S(1)}, u32[]{:S(2)}, u32[]{:S(2)}) collective-permute-start(f32[64,512]{1,0:T(8,128)S(1)} %bitcast_add_fusion.11), channel_id=1, source_target_pairs={{0,16},{16,32},{32,48},{48,64},{64,80},{80,96},{96,112},{112,0},{1... | collective-permute-start | bytes 393224 | tf_op jit(solution)/shard_map/ppermute | solution.py:42
  36.4 7.0 %collective-permute-start.12 = (f32[64,512]{1,0:T(8,128)S(1)}, f32[64,512]{1,0:T(8,128)S(1)}, u32[]{:S(2)}, u32[]{:S(2)}) collective-permute-start(f32[64,512]{1,0:T(8,128)S(1)} %bitcast_add_fusion.4), channel_id=1, source_target_pairs={{0,112},{16,0},{32,16},{48,32},{64,48},{80,64},{96,80},{112,96},{1... | collective-permute-start | bytes 393224 | tf_op jit(solution)/shard_map/ppermute | solution.py:43
  42.6 6.0 %collective-permute-start.6 = (f32[64,512]{1,0:T(8,128)S(1)}, f32[64,512]{1,0:T(8,128)S(1)}, u32[]{:S(2)}, u32[]{:S(2)}) collective-permute-start(f32[64,512]{1,0:T(8,128)S(1)} %bitcast_add_fusion.10), channel_id=1, source_target_pairs={{0,16},{16,32},{32,48},{48,64},{64,80},{80,96},{96,112},{112,0},{1... | collective-permute-start | bytes 393224 | tf_op jit(solution)/shard_map/ppermute | solution.py:42
  43.4 5.7 %collective-permute-start.13 = (f32[64,512]{1,0:T(8,128)S(1)}, f32[64,512]{1,0:T(8,128)S(1)}, u32[]{:S(2)}, u32[]{:S(2)}) collective-permute-start(f32[64,512]{1,0:T(8,128)S(1)} %bitcast_add_fusion.3), channel_id=1, source_target_pairs={{0,112},{16,0},{32,16},{48,32},{64,48},{80,64},{96,80},{112,96},{1... | collective-permute-start | bytes 393224 | tf_op jit(solution)/shard_map/ppermute | solution.py:43
  49.2 8.1 %collective-permute-start.14 = (f32[2,64,512]{2,1,0:T(8,128)S(1)}, f32[2,64,512]{2,1,0:T(8,128)S(1)}, u32[]{:S(2)}, u32[]{:S(2)}) collective-permute-start(f32[2,64,512]{2,1,0:T(8,128)S(1)} %pad_maximum_fusion), channel_id=1, source_target_pairs={{0,128},{16,144},{32,160},{48,176},{64,192},{80,208},{96,224},{112... | collective-permute-start | bytes 786440 | tf_op jit(solution)/shard_map/ppermute | solution.py:48
  58.0 3.8 %collective-permute-start.17 = (f32[]{:T(128)}, f32[]{:T(128)}, u32[]{:S(2)}, u32[]{:S(2)}) collective-permute-start(f32[]{:T(128)} %get-tuple-element.46), channel_id=1, source_target_pairs={{0,1},{1,0},{2,3},{3,2},{4,5},{5,4},{6,7},{7,6},{8,9},{9,8},{10,11... | collective-permute-start | bytes 20 | tf_op jit(solution)/shard_map/ppermute | solution.py:62
  58.1 7.4 %collective-permute-start.16 = (f32[64,512]{1,0:T(8,128)S(1)}, f32[64,512]{1,0:T(8,128)S(1)}, u32[]{:S(2)}, u32[]{:S(2)}) collective-permute-start(f32[64,512]{1,0:T(8,128)S(1)} %get-tuple-element.50), channel_id=1, source_target_pairs={{0,112},{16,0},{32,16},{48,32},{64,48},{80,64},{96,80},{112,96},{1... | collective-permute-start | bytes 393224 | tf_op jit(solution)/shard_map/ppermute | solution.py:60
  60.9 7.1 %collective-permute-start.15 = (f32[64,512]{1,0:T(8,128)S(1)}, f32[64,512]{1,0:T(8,128)S(1)}, u32[]{:S(2)}, u32[]{:S(2)}) collective-permute-start(f32[64,512]{1,0:T(8,128)S(1)} %get-tuple-element.51), channel_id=1, source_target_pairs={{0,16},{16,32},{32,48},{48,64},{64,80},{80,96},{96,112},{112,0},{1... | collective-permute-start | bytes 393224 | tf_op jit(solution)/shard_map/ppermute | solution.py:59
  68.0 6.4 %collective-permute-start.18 = (f32[64,512]{1,0:T(8,128)S(1)}, f32[64,512]{1,0:T(8,128)S(1)}, u32[]{:S(2)}, u32[]{:S(2)}) collective-permute-start(f32[64,512]{1,0:T(8,128)S(1)} %collective-permute-done.15), channel_id=1, source_target_pairs={{0,16},{16,32},{32,48},{48,64},{64,80},{80,96},{96,112},{112,0},{1... | collective-permute-start | bytes 393224 | tf_op jit(solution)/shard_map/ppermute | solution.py:59
  68.7 5.1 %collective-permute-start.20 = (f32[]{:T(128)}, f32[]{:T(128)}, u32[]{:S(2)}, u32[]{:S(2)}) collective-permute-start(f32[]{:T(128)} %add.367), channel_id=1, source_target_pairs={{0,2},{1,3},{2,0},{3,1},{4,6},{5,7},{6,4},{7,5},{8,10},{9,11},{10,... | collective-permute-start | bytes 20 | tf_op jit(solution)/shard_map/ppermute | solution.py:62
  71.6 5.9 %collective-permute-start.19 = (f32[64,512]{1,0:T(8,128)S(1)}, f32[64,512]{1,0:T(8,128)S(1)}, u32[]{:S(2)}, u32[]{:S(2)}) collective-permute-start(f32[64,512]{1,0:T(8,128)S(1)} %collective-permute-done.16), channel_id=1, source_target_pairs={{0,112},{16,0},{32,16},{48,32},{64,48},{80,64},{96,80},{112,96},{1... | collective-permute-start | bytes 393224 | tf_op jit(solution)/shard_map/ppermute | solution.py:60
  77.5 8.8 %collective-permute-start.21 = (f32[64,512]{1,0:T(8,128)S(1)}, f32[64,512]{1,0:T(8,128)S(1)}, u32[]{:S(2)}, u32[]{:S(2)}) collective-permute-start(f32[64,512]{1,0:T(8,128)S(1)} %collective-permute-done.18), channel_id=1, source_target_pairs={{0,16},{16,32},{32,48},{48,64},{64,80},{80,96},{96,112},{112,0},{1... | collective-permute-start | bytes 393224 | tf_op jit(solution)/shard_map/ppermute | solution.py:59
  80.5 5.3 %collective-permute-start.23 = (f32[]{:T(128)}, f32[]{:T(128)}, u32[]{:S(2)}, u32[]{:S(2)}) collective-permute-start(f32[]{:T(128)} %add.368), channel_id=1, source_target_pairs={{0,4},{1,5},{2,6},{3,7},{4,0},{5,1},{6,2},{7,3},{8,12},{9,13},{10,... | collective-permute-start | bytes 20 | tf_op jit(solution)/shard_map/ppermute | solution.py:62
  84.6 6.2 %collective-permute-start.22 = (f32[64,512]{1,0:T(8,128)S(1)}, f32[64,512]{1,0:T(8,128)S(1)}, u32[]{:S(2)}, u32[]{:S(2)}) collective-permute-start(f32[64,512]{1,0:T(8,128)S(1)} %collective-permute-done.19), channel_id=1, source_target_pairs={{0,112},{16,0},{32,16},{48,32},{64,48},{80,64},{96,80},{112,96},{1... | collective-permute-start | bytes 393224 | tf_op jit(solution)/shard_map/ppermute | solution.py:60
  90.8 6.4 %collective-permute-start.24 = (f32[64,512]{1,0:T(8,128)S(1)}, f32[64,512]{1,0:T(8,128)S(1)}, u32[]{:S(2)}, u32[]{:S(2)}) collective-permute-start(f32[64,512]{1,0:T(8,128)S(1)} %collective-permute-done.21), channel_id=1, source_target_pairs={{0,16},{16,32},{32,48},{48,64},{64,80},{80,96},{96,112},{112,0},{1... | collective-permute-start | bytes 393224 | tf_op jit(solution)/shard_map/ppermute | solution.py:59
  92.8 3.8 %collective-permute-start.26 = (f32[]{:T(128)}, f32[]{:T(128)}, u32[]{:S(2)}, u32[]{:S(2)}) collective-permute-start(f32[]{:T(128)} %add.369), channel_id=1, source_target_pairs={{0,8},{1,9},{2,10},{3,11},{4,12},{5,13},{6,14},{7,15},{8,0},{9,1},... | collective-permute-start | bytes 20 | tf_op jit(solution)/shard_map/ppermute | solution.py:62
  96.1 5.6 %collective-permute-start.25 = (f32[64,512]{1,0:T(8,128)S(1)}, f32[64,512]{1,0:T(8,128)S(1)}, u32[]{:S(2)}, u32[]{:S(2)}) collective-permute-start(f32[64,512]{1,0:T(8,128)S(1)} %collective-permute-done.22), channel_id=1, source_target_pairs={{0,112},{16,0},{32,16},{48,32},{64,48},{80,64},{96,80},{112,96},{1... | collective-permute-start | bytes 393224 | tf_op jit(solution)/shard_map/ppermute | solution.py:60
  101.7 6.1 %collective-permute-start.27 = (f32[64,512]{1,0:T(8,128)S(1)}, f32[64,512]{1,0:T(8,128)S(1)}, u32[]{:S(2)}, u32[]{:S(2)}) collective-permute-start(f32[64,512]{1,0:T(8,128)S(1)} %collective-permute-done.24), channel_id=1, source_target_pairs={{0,16},{16,32},{32,48},{48,64},{64,80},{80,96},{96,112},{112,0},{1... | collective-permute-start | bytes 393224 | tf_op jit(solution)/shard_map/ppermute | solution.py:59
  103.5 3.8 %collective-permute-start.29 = (f32[]{:T(128)}, f32[]{:T(128)}, u32[]{:S(2)}, u32[]{:S(2)}) collective-permute-start(f32[]{:T(128)} %add.370), channel_id=1, source_target_pairs={{0,16},{16,0},{32,48},{48,32},{64,80},{80,64},{96,112},{112,96},{1... | collective-permute-start | bytes 20 | tf_op jit(solution)/shard_map/ppermute | solution.py:62
  105.1 6.0 %collective-permute-start.28 = (f32[64,512]{1,0:T(8,128)S(1)}, f32[64,512]{1,0:T(8,128)S(1)}, u32[]{:S(2)}, u32[]{:S(2)}) collective-permute-start(f32[64,512]{1,0:T(8,128)S(1)} %collective-permute-done.25), channel_id=1, source_target_pairs={{0,112},{16,0},{32,16},{48,32},{64,48},{80,64},{96,80},{112,96},{1... | collective-permute-start | bytes 393224 | tf_op jit(solution)/shard_map/ppermute | solution.py:60
  111.1 6.6 %collective-permute-start.30 = (f32[64,512]{1,0:T(8,128)S(1)}, f32[64,512]{1,0:T(8,128)S(1)}, u32[]{:S(2)}, u32[]{:S(2)}) collective-permute-start(f32[64,512]{1,0:T(8,128)S(1)} %collective-permute-done.27), channel_id=1, source_target_pairs={{0,16},{16,32},{32,48},{48,64},{64,80},{80,96},{96,112},{112,0},{1... | collective-permute-start | bytes 393224 | tf_op jit(solution)/shard_map/ppermute | solution.py:59
  112.5 4.7 %collective-permute-start.32 = (f32[]{:T(128)}, f32[]{:T(128)}, u32[]{:S(2)}, u32[]{:S(2)}) collective-permute-start(f32[]{:T(128)} %add.371), channel_id=1, source_target_pairs={{0,32},{16,48},{32,0},{48,16},{64,96},{80,112},{96,64},{112,80},{1... | collective-permute-start | bytes 20 | tf_op jit(solution)/shard_map/ppermute | solution.py:62
  115.0 5.0 %collective-permute-start.31 = (f32[64,512]{1,0:T(8,128)S(1)}, f32[64,512]{1,0:T(8,128)S(1)}, u32[]{:S(2)}, u32[]{:S(2)}) collective-permute-start(f32[64,512]{1,0:T(8,128)S(1)} %collective-permute-done.28), channel_id=1, source_target_pairs={{0,112},{16,0},{32,16},{48,32},{64,48},{80,64},{96,80},{112,96},{1... | collective-permute-start | bytes 393224 | tf_op jit(solution)/shard_map/ppermute | solution.py:60
  120.0 9.2 %collective-permute-start.33 = (f32[64,512]{1,0:T(8,128)S(1)}, f32[64,512]{1,0:T(8,128)S(1)}, u32[]{:S(2)}, u32[]{:S(2)}) collective-permute-start(f32[64,512]{1,0:T(8,128)S(1)} %collective-permute-done.30), channel_id=1, source_target_pairs={{0,16},{16,32},{32,48},{48,64},{64,80},{80,96},{96,112},{112,0},{1... | collective-permute-start | bytes 393224 | tf_op jit(solution)/shard_map/ppermute | solution.py:59
  121.0 7.7 %collective-permute-start.35 = (f32[]{:T(128)}, f32[]{:T(128)}, u32[]{:S(2)}, u32[]{:S(2)}) collective-permute-start(f32[]{:T(128)} %add.372), channel_id=1, source_target_pairs={{0,64},{16,80},{32,96},{48,112},{64,0},{80,16},{96,32},{112,48},{1... | collective-permute-start | bytes 20 | tf_op jit(solution)/shard_map/ppermute | solution.py:62
  125.8 5.0 %collective-permute-start.34 = (f32[64,512]{1,0:T(8,128)S(1)}, f32[64,512]{1,0:T(8,128)S(1)}, u32[]{:S(2)}, u32[]{:S(2)}) collective-permute-start(f32[64,512]{1,0:T(8,128)S(1)} %collective-permute-done.31), channel_id=1, source_target_pairs={{0,112},{16,0},{32,16},{48,32},{64,48},{80,64},{96,80},{112,96},{1... | collective-permute-start | bytes 393224 | tf_op jit(solution)/shard_map/ppermute | solution.py:60
  130.8 1.6 %copy-start = (f32[2,512,512]{2,1,0:T(8,128)S(1)}, f32[2,512,512]{2,1,0:T(8,128)}, u32[]{:S(2)}) copy-start(f32[2,512,512]{2,1,0:T(8,128)} %param.4) | copy-start | bytes 6291460
  130.9 2.2 %copy-start.1 = (f32[2,512,512]{2,1,0:T(8,128)S(1)}, f32[2,512,512]{2,1,0:T(8,128)}, u32[]{:S(2)}) copy-start(f32[2,512,512]{2,1,0:T(8,128)} %param.5) | copy-start | bytes 6291460

commit v4 on v2

--- a/solution.py
+++ b/solution.py
@@ -22,7 +22,7 @@
     return [(g * RING + z, g * RING + (z + shift) % RING) for g in range(groups) for z in range(RING)]
 
 
-def body(island_delta, params, momentum):
+def step(island_delta, params, momentum):
     islands = lax.axis_size("island")
     count = 2 * D * KVH * HEAD
     me = lax.axis_index("island")
@@ -47,23 +47,22 @@
     partner = [(i, (i + RING) % islands) for i in range(islands)]
     mine = (mine + lax.ppermute(mine, "island", partner)) / islands
     part_sq = jnp.sum(mine * mine)
+    part_sq = jnp.where(me < RING, part_sq, jnp.float32(0.0))
+    total_sq = lax.psum(jnp.full((128, 128), part_sq), ("island", "inner"))[0, 0]
 
     out = jnp.zeros((halves, RING, chunk, cols), jnp.float32)
     out = lax.dynamic_update_index_in_dim(out, mine[:, None], z, axis=1)
-    sq = part_sq
-    cur_r, cur_l, cur_q = mine[0], mine[1], part_sq
+    cur_r, cur_l = mine[0], mine[1]
     for s in range(RING - 1):
-        cur_r, cur_q = lax.ppermute((cur_r, cur_q), "island", right)
+        cur_r = lax.ppermute(cur_r, "island", right)
         cur_l = lax.ppermute(cur_l, "island", left)
-        sq = sq + cur_q
         out = lax.dynamic_update_slice(out, cur_r[None, None], (0, (z - 1 - s) % RING, 0, 0))
         out = lax.dynamic_update_slice(out, cur_l[None, None], (1, (z + 1 + s) % RING, 0, 0))
     average = out.reshape(halves, rows, cols)
-    total_sq = lax.psum(sq, "inner")
     return outer_update(average, params, momentum, total_sq / count)
 
 
 def solution(mesh):
     in_specs = (P("island", None, "inner", None), P(None, "inner", None), P(None, "inner", None))
     out_specs = (P(None, "inner", None), P(None, "inner", None))
-    return jax.shard_map(body, mesh=mesh, in_specs=in_specs, out_specs=out_specs, check_vma=False)
+    return jax.shard_map(step, mesh=mesh, in_specs=in_specs, out_specs=out_specs, check_vma=False)

time: 171 us -> 363 us (2.12)
  waiting for transfers between devices: 71.2 us -> 295 us
  blocking collectives: 27.6 us -> 0 us
  starting transfers between devices: 53.3 us -> 39.8 us
  between operations: 7.03 us -> 15.9 us
    psum x0 -> x1, waiting for transfers between devices: none -> 239 us  [step(): lax.psum(jnp.full((128, 128), part_sq), ('island', 'inner'))[0, 0]]
    psum x1 -> x0, blocking collectives: 27.6 us -> none  [body(): total_sq = lax.psum(sq, 'inner')]
    ppermute x36 -> x29, waiting for transfers between devices: 71.2 us -> 55.2 us  [the longest x7 21.8 us: step(): got_r = lax.ppermute(acc_r, 'island', right)]
    ppermute x36 -> x29, starting transfers between devices: 53.3 us -> 39.8 us  [the longest x7 15.4 us: step(): got_l = lax.ppermute(acc_l, 'island', left)]
  transfers between devices with their start and end apart: 36 -> 30, of which waited for: 29 -> 24; matrix products, arithmetic and copies ran while one was open for 0% -> 1% of each run, Pallas kernels for 0% -> 0%
where the time goes in v4:
time: 363 us; the launch traced here: 360 us
  waiting for transfers between devices  295 us (81%)
  starting transfers between devices  39.8 us (11%)
  between operations  15.9 us (4%)
  local copies, waits for them, and re-layouts  6.03 us (2%)
  other arithmetic  3.94 us (1%)
    psum x1, waiting for transfers between devices, step(): lax.psum(jnp.full((128, 128), part_sq), ('island', 'inner'))[0, 0]  239 us
    ppermute x7, waiting for transfers between devices, step(): got_r = lax.ppermute(acc_r, 'island', right)  21.8 us
    ppermute x7, waiting for transfers between devices, step(): cur_l = lax.ppermute(cur_l, 'island', left)  17.9 us
    ppermute x7, starting transfers between devices, step(): got_l = lax.ppermute(acc_l, 'island', left)  15.4 us
    ppermute x7, starting transfers between devices, step(): cur_l = lax.ppermute(cur_l, 'island', left)  9.7 us
  transfers between devices with their start and end apart: 30, of which 24 were waited for; matrix products, arithmetic and copies ran while one was open for 1% of the time, Pallas kernels for 0%

profile of v4, /device:TPU:32, one launch (start us, length us, event | category | flops | bytes accessed | tf_op | source)
XLA Modules:
  0.0 360.3 jit_solution(12103211681847454181)
XLA Ops:
  7.2 0.0 all-reduce.2.cloned.1.call-start
  7.2 1.7 fusion.4
  9.0 2.0 collective-permute-start
  11.0 0.2 collective-permute-start.7
  11.4 2.9 collective-permute-done
  14.3 2.0 collective-permute-start.1
  16.3 2.4 collective-permute-start.8
  18.8 2.8 collective-permute-done.1
  21.6 0.1 collective-permute-start.2
  21.7 0.7 collective-permute-done.8
  22.4 2.6 collective-permute-start.9
  25.0 2.8 collective-permute-done.2
  27.9 0.1 collective-permute-start.3
  28.0 0.7 collective-permute-done.9
  28.7 2.6 collective-permute-start.10
  31.3 2.8 collective-permute-done.3
  34.2 0.2 collective-permute-start.4
  34.3 0.9 collective-permute-done.10
  35.3 2.6 collective-permute-start.11
  37.9 4.0 %collective-permute-done.4 = f32[64,512]{1,0:T(8,128)S(1)} collective-permute-done((f32[64,512]{1,0:T(8,128)S(1)}, f32[64,512]{1,0:T(8,128)S(1)}, u32[]{:S(2)}, u32[]{:S(2)}) %collective-permute-start.4) | collective-permute-done | bytes 131104 | tf_op jit(solution)/shard_map/ppermute | solution.py:42
  41.9 0.4 collective-permute-start.5
  42.3 0.7 collective-permute-done.11
  42.9 2.6 collective-permute-start.12
  45.5 3.6 %collective-permute-done.5 = f32[64,512]{1,0:T(8,128)S(1)} collective-permute-done((f32[64,512]{1,0:T(8,128)S(1)}, f32[64,512]{1,0:T(8,128)S(1)}, u32[]{:S(2)}, u32[]{:S(2)}) %collective-permute-start.5) | collective-permute-done | bytes 131104 | tf_op jit(solution)/shard_map/ppermute | solution.py:42
  49.2 0.1 collective-permute-start.6
  49.2 0.7 collective-permute-done.12
  50.0 2.3 collective-permute-start.13
  52.3 2.8 collective-permute-done.6
  55.2 0.5 collective-permute-done.13
  55.7 3.5 collective-permute-start.14
  59.2 4.7 %collective-permute-done.14 = f32[2,64,512]{2,1,0:T(8,128)S(1)} collective-permute-done((f32[2,64,512]{2,1,0:T(8,128)S(1)}, f32[2,64,512]{2,1,0:T(8,128)S(1)}, u32[]{:S(2)}, u32[]{:S(2)}) %collective-permute-start.14) | collective-permute-done | bytes 262176 | tf_op jit(solution)/shard_map/ppermute | solution.py:48
  63.9 0.7 multiply_reduce_fusion
  65.2 0.6 broadcast_in_dim.51
  65.8 0.0 all-reduce.2.cloned.1.call-update
  65.9 2.8 collective-permute-start.16
  68.7 0.6 collective-permute-start.15
  69.3 0.2 broadcast_in_dim.52
  69.6 239.5 %all-reduce.2.cloned.1.call-done = f32[128,128]{1,0:T(8,128)} async-done(((f32[128,128]{1,0:T(8,128)}), f32[128,128]{1,0:T(8,128)}) %all-reduce.2.cloned.1.call-update) | async-done | bytes 65552 | tf_op jit(solution)/shard_map/psum | solution.py:51
  309.1 1.2 slice.17
  311.0 1.0 collective-permute-start.18
  312.0 1.1 collective-permute-start.17
  313.1 3.6 collective-permute-done.18
  316.7 1.6 collective-permute-start.20
  318.3 0.7 collective-permute-start.19
  319.0 3.9 %collective-permute-done.20 = f32[64,512]{1,0:T(8,128)S(1)} collective-permute-done((f32[64,512]{1,0:T(8,128)S(1)}, f32[64,512]{1,0:T(8,128)S(1)}, u32[]{:S(2)}, u32[]{:S(2)}) %collective-permute-start.20) | collective-permute-done | bytes 131104 | tf_op jit(solution)/shard_map/ppermute | solution.py:58
  322.9 1.0 collective-permute-start.22
  323.9 1.1 collective-permute-start.21
  325.0 3.3 collective-permute-done.22
  328.3 0.6 collective-permute-start.24
  328.8 0.4 collective-permute-done.21
  329.2 1.1 collective-permute-start.23
  330.4 2.9 collective-permute-done.24
  333.3 1.7 collective-permute-start.26
  335.0 0.4 collective-permute-done.23
  335.4 0.9 collective-permute-start.25
  336.3 4.2 %collective-permute-done.26 = f32[64,512]{1,0:T(8,128)S(1)} collective-permute-done((f32[64,512]{1,0:T(8,128)S(1)}, f32[64,512]{1,0:T(8,128)S(1)}, u32[]{:S(2)}, u32[]{:S(2)}) %collective-permute-start.26) | collective-permute-done | bytes 131104 | tf_op jit(solution)/shard_map/ppermute | solution.py:58
  340.5 1.0 collective-permute-start.28
  341.5 0.5 collective-permute-done.25
  342.0 1.1 collective-permute-start.27
  343.0 5.4 %collective-permute-done.27 = f32[64,512]{1,0:T(8,128)S(1)} collective-permute-done((f32[64,512]{1,0:T(8,128)S(1)}, f32[64,512]{1,0:T(8,128)S(1)}, u32[]{:S(2)}, u32[]{:S(2)}) %collective-permute-start.27) | collective-permute-done | bytes 131104 | tf_op jit(solution)/shard_map/ppermute | solution.py:57
  348.5 0.2 broadcast_multiply_fusion
  348.7 1.3 copy-done
  350.1 0.6 copy-done.1
  350.7 2.8 fusion.1
  (41 shorter events, 0.5 us)
Async XLA Ops:
  7.2 301.9 %all-reduce.2.cloned.1.call-start = ((), (), s32[]{:S(2)}) async-start(), calls=%async_computation | async-start | bytes 131072 | tf_op jit(solution)/shard_map/psum | solution.py:51
  9.0 5.3 %collective-permute-start = (f32[64,512]{1,0:T(8,128)S(1)}, f32[64,512]{1,0:T(8,128)S(1)}, u32[]{:S(2)}, u32[]{:S(2)}) collective-permute-start(f32[64,512]{1,0:T(8,128)S(1)} %dynamic-slice_bitcast_fusion.1), channel_id=1, source_target_pairs={{0,16},{16,32},{32,48},{48,64},{64,80},{80,96},{96,112},{112,0},{1... | collective-permute-start | bytes 393224 | tf_op jit(solution)/shard_map/ppermute | solution.py:42
  11.0 5.3 %collective-permute-start.7 = (f32[64,512]{1,0:T(8,128)S(1)}, f32[64,512]{1,0:T(8,128)S(1)}, u32[]{:S(2)}, u32[]{:S(2)}) collective-permute-start(f32[64,512]{1,0:T(8,128)S(1)} %dynamic-slice_bitcast_fusion), channel_id=1, source_target_pairs={{0,112},{16,0},{32,16},{48,32},{64,48},{80,64},{96,80},{112,96},{1... | collective-permute-start | bytes 393224 | tf_op jit(solution)/shard_map/ppermute | solution.py:43
  14.3 7.2 %collective-permute-start.1 = (f32[64,512]{1,0:T(8,128)S(1)}, f32[64,512]{1,0:T(8,128)S(1)}, u32[]{:S(2)}, u32[]{:S(2)}) collective-permute-start(f32[64,512]{1,0:T(8,128)S(1)} %bitcast_add_fusion.15), channel_id=1, source_target_pairs={{0,16},{16,32},{32,48},{48,64},{64,80},{80,96},{96,112},{112,0},{1... | collective-permute-start | bytes 393224 | tf_op jit(solution)/shard_map/ppermute | solution.py:42
  16.3 6.0 %collective-permute-start.8 = (f32[64,512]{1,0:T(8,128)S(1)}, f32[64,512]{1,0:T(8,128)S(1)}, u32[]{:S(2)}, u32[]{:S(2)}) collective-permute-start(f32[64,512]{1,0:T(8,128)S(1)} %bitcast_add_fusion.8), channel_id=1, source_target_pairs={{0,112},{16,0},{32,16},{48,32},{64,48},{80,64},{96,80},{112,96},{1... | collective-permute-start | bytes 393224 | tf_op jit(solution)/shard_map/ppermute | solution.py:43
  21.6 6.3 %collective-permute-start.2 = (f32[64,512]{1,0:T(8,128)S(1)}, f32[64,512]{1,0:T(8,128)S(1)}, u32[]{:S(2)}, u32[]{:S(2)}) collective-permute-start(f32[64,512]{1,0:T(8,128)S(1)} %bitcast_add_fusion.14), channel_id=1, source_target_pairs={{0,16},{16,32},{32,48},{48,64},{64,80},{80,96},{96,112},{112,0},{1... | collective-permute-start | bytes 393224 | tf_op jit(solution)/shard_map/ppermute | solution.py:42
  22.4 6.3 %collective-permute-start.9 = (f32[64,512]{1,0:T(8,128)S(1)}, f32[64,512]{1,0:T(8,128)S(1)}, u32[]{:S(2)}, u32[]{:S(2)}) collective-permute-start(f32[64,512]{1,0:T(8,128)S(1)} %bitcast_add_fusion.7), channel_id=1, source_target_pairs={{0,112},{16,0},{32,16},{48,32},{64,48},{80,64},{96,80},{112,96},{1... | collective-permute-start | bytes 393224 | tf_op jit(solution)/shard_map/ppermute | solution.py:43
  27.9 6.3 %collective-permute-start.3 = (f32[64,512]{1,0:T(8,128)S(1)}, f32[64,512]{1,0:T(8,128)S(1)}, u32[]{:S(2)}, u32[]{:S(2)}) collective-permute-start(f32[64,512]{1,0:T(8,128)S(1)} %bitcast_add_fusion.13), channel_id=1, source_target_pairs={{0,16},{16,32},{32,48},{48,64},{64,80},{80,96},{96,112},{112,0},{1... | collective-permute-start | bytes 393224 | tf_op jit(solution)/shard_map/ppermute | solution.py:42
  28.7 6.5 %collective-permute-start.10 = (f32[64,512]{1,0:T(8,128)S(1)}, f32[64,512]{1,0:T(8,128)S(1)}, u32[]{:S(2)}, u32[]{:S(2)}) collective-permute-start(f32[64,512]{1,0:T(8,128)S(1)} %bitcast_add_fusion.6), channel_id=1, source_target_pairs={{0,112},{16,0},{32,16},{48,32},{64,48},{80,64},{96,80},{112,96},{1... | collective-permute-start | bytes 393224 | tf_op jit(solution)/shard_map/ppermute | solution.py:43
  34.2 7.7 %collective-permute-start.4 = (f32[64,512]{1,0:T(8,128)S(1)}, f32[64,512]{1,0:T(8,128)S(1)}, u32[]{:S(2)}, u32[]{:S(2)}) collective-permute-start(f32[64,512]{1,0:T(8,128)S(1)} %bitcast_add_fusion.12), channel_id=1, source_target_pairs={{0,16},{16,32},{32,48},{48,64},{64,80},{80,96},{96,112},{112,0},{1... | collective-permute-start | bytes 393224 | tf_op jit(solution)/shard_map/ppermute | solution.py:42
  35.3 7.7 %collective-permute-start.11 = (f32[64,512]{1,0:T(8,128)S(1)}, f32[64,512]{1,0:T(8,128)S(1)}, u32[]{:S(2)}, u32[]{:S(2)}) collective-permute-start(f32[64,512]{1,0:T(8,128)S(1)} %bitcast_add_fusion.5), channel_id=1, source_target_pairs={{0,112},{16,0},{32,16},{48,32},{64,48},{80,64},{96,80},{112,96},{1... | collective-permute-start | bytes 393224 | tf_op jit(solution)/shard_map/ppermute | solution.py:43
  41.9 7.3 %collective-permute-start.5 = (f32[64,512]{1,0:T(8,128)S(1)}, f32[64,512]{1,0:T(8,128)S(1)}, u32[]{:S(2)}, u32[]{:S(2)}) collective-permute-start(f32[64,512]{1,0:T(8,128)S(1)} %bitcast_add_fusion.11), channel_id=1, source_target_pairs={{0,16},{16,32},{32,48},{48,64},{64,80},{80,96},{96,112},{112,0},{1... | collective-permute-start | bytes 393224 | tf_op jit(solution)/shard_map/ppermute | solution.py:42
  42.9 7.0 %collective-permute-start.12 = (f32[64,512]{1,0:T(8,128)S(1)}, f32[64,512]{1,0:T(8,128)S(1)}, u32[]{:S(2)}, u32[]{:S(2)}) collective-permute-start(f32[64,512]{1,0:T(8,128)S(1)} %bitcast_add_fusion.4), channel_id=1, source_target_pairs={{0,112},{16,0},{32,16},{48,32},{64,48},{80,64},{96,80},{112,96},{1... | collective-permute-start | bytes 393224 | tf_op jit(solution)/shard_map/ppermute | solution.py:43
  49.2 6.0 %collective-permute-start.6 = (f32[64,512]{1,0:T(8,128)S(1)}, f32[64,512]{1,0:T(8,128)S(1)}, u32[]{:S(2)}, u32[]{:S(2)}) collective-permute-start(f32[64,512]{1,0:T(8,128)S(1)} %bitcast_add_fusion.10), channel_id=1, source_target_pairs={{0,16},{16,32},{32,48},{48,64},{64,80},{80,96},{96,112},{112,0},{1... | collective-permute-start | bytes 393224 | tf_op jit(solution)/shard_map/ppermute | solution.py:42
  50.0 5.7 %collective-permute-start.13 = (f32[64,512]{1,0:T(8,128)S(1)}, f32[64,512]{1,0:T(8,128)S(1)}, u32[]{:S(2)}, u32[]{:S(2)}) collective-permute-start(f32[64,512]{1,0:T(8,128)S(1)} %bitcast_add_fusion.3), channel_id=1, source_target_pairs={{0,112},{16,0},{32,16},{48,32},{64,48},{80,64},{96,80},{112,96},{1... | collective-permute-start | bytes 393224 | tf_op jit(solution)/shard_map/ppermute | solution.py:43
  55.7 8.1 %collective-permute-start.14 = (f32[2,64,512]{2,1,0:T(8,128)S(1)}, f32[2,64,512]{2,1,0:T(8,128)S(1)}, u32[]{:S(2)}, u32[]{:S(2)}) collective-permute-start(f32[2,64,512]{2,1,0:T(8,128)S(1)} %pad_maximum_fusion), channel_id=1, source_target_pairs={{0,128},{16,144},{32,160},{48,176},{64,192},{80,208},{96,224},{112... | collective-permute-start | bytes 786440 | tf_op jit(solution)/shard_map/ppermute | solution.py:48
  65.9 245.1 %collective-permute-start.16 = (f32[64,512]{1,0:T(8,128)S(1)}, f32[64,512]{1,0:T(8,128)S(1)}, u32[]{:S(2)}, u32[]{:S(2)}) collective-permute-start(f32[64,512]{1,0:T(8,128)S(1)} %get-tuple-element.8), channel_id=1, source_target_pairs={{0,112},{16,0},{32,16},{48,32},{64,48},{80,64},{96,80},{112,96},{1... | collective-permute-start | bytes 393224 | tf_op jit(solution)/shard_map/ppermute | solution.py:58
  68.7 243.3 %collective-permute-start.15 = (f32[64,512]{1,0:T(8,128)S(1)}, f32[64,512]{1,0:T(8,128)S(1)}, u32[]{:S(2)}, u32[]{:S(2)}) collective-permute-start(f32[64,512]{1,0:T(8,128)S(1)} %get-tuple-element.9), channel_id=1, source_target_pairs={{0,16},{16,32},{32,48},{48,64},{64,80},{80,96},{96,112},{112,0},{1... | collective-permute-start | bytes 393224 | tf_op jit(solution)/shard_map/ppermute | solution.py:57
  311.0 5.7 %collective-permute-start.18 = (f32[64,512]{1,0:T(8,128)S(1)}, f32[64,512]{1,0:T(8,128)S(1)}, u32[]{:S(2)}, u32[]{:S(2)}) collective-permute-start(f32[64,512]{1,0:T(8,128)S(1)} %collective-permute-done.16), channel_id=1, source_target_pairs={{0,112},{16,0},{32,16},{48,32},{64,48},{80,64},{96,80},{112,96},{1... | collective-permute-start | bytes 393224 | tf_op jit(solution)/shard_map/ppermute | solution.py:58
  312.0 6.3 %collective-permute-start.17 = (f32[64,512]{1,0:T(8,128)S(1)}, f32[64,512]{1,0:T(8,128)S(1)}, u32[]{:S(2)}, u32[]{:S(2)}) collective-permute-start(f32[64,512]{1,0:T(8,128)S(1)} %collective-permute-done.15), channel_id=1, source_target_pairs={{0,16},{16,32},{32,48},{48,64},{64,80},{80,96},{96,112},{112,0},{1... | collective-permute-start | bytes 393224 | tf_op jit(solution)/shard_map/ppermute | solution.py:57
  316.7 6.2 %collective-permute-start.20 = (f32[64,512]{1,0:T(8,128)S(1)}, f32[64,512]{1,0:T(8,128)S(1)}, u32[]{:S(2)}, u32[]{:S(2)}) collective-permute-start(f32[64,512]{1,0:T(8,128)S(1)} %collective-permute-done.18), channel_id=1, source_target_pairs={{0,112},{16,0},{32,16},{48,32},{64,48},{80,64},{96,80},{112,96},{1... | collective-permute-start | bytes 393224 | tf_op jit(solution)/shard_map/ppermute | solution.py:58
  318.3 5.5 %collective-permute-start.19 = (f32[64,512]{1,0:T(8,128)S(1)}, f32[64,512]{1,0:T(8,128)S(1)}, u32[]{:S(2)}, u32[]{:S(2)}) collective-permute-start(f32[64,512]{1,0:T(8,128)S(1)} %collective-permute-done.17), channel_id=1, source_target_pairs={{0,16},{16,32},{32,48},{48,64},{64,80},{80,96},{96,112},{112,0},{1... | collective-permute-start | bytes 393224 | tf_op jit(solution)/shard_map/ppermute | solution.py:57
  322.9 5.4 %collective-permute-start.22 = (f32[64,512]{1,0:T(8,128)S(1)}, f32[64,512]{1,0:T(8,128)S(1)}, u32[]{:S(2)}, u32[]{:S(2)}) collective-permute-start(f32[64,512]{1,0:T(8,128)S(1)} %collective-permute-done.20), channel_id=1, source_target_pairs={{0,112},{16,0},{32,16},{48,32},{64,48},{80,64},{96,80},{112,96},{1... | collective-permute-start | bytes 393224 | tf_op jit(solution)/shard_map/ppermute | solution.py:58
  323.9 5.3 %collective-permute-start.21 = (f32[64,512]{1,0:T(8,128)S(1)}, f32[64,512]{1,0:T(8,128)S(1)}, u32[]{:S(2)}, u32[]{:S(2)}) collective-permute-start(f32[64,512]{1,0:T(8,128)S(1)} %collective-permute-done.19), channel_id=1, source_target_pairs={{0,16},{16,32},{32,48},{48,64},{64,80},{80,96},{96,112},{112,0},{1... | collective-permute-start | bytes 393224 | tf_op jit(solution)/shard_map/ppermute | solution.py:57
  328.3 5.0 %collective-permute-start.24 = (f32[64,512]{1,0:T(8,128)S(1)}, f32[64,512]{1,0:T(8,128)S(1)}, u32[]{:S(2)}, u32[]{:S(2)}) collective-permute-start(f32[64,512]{1,0:T(8,128)S(1)} %collective-permute-done.22), channel_id=1, source_target_pairs={{0,112},{16,0},{32,16},{48,32},{64,48},{80,64},{96,80},{112,96},{1... | collective-permute-start | bytes 393224 | tf_op jit(solution)/shard_map/ppermute | solution.py:58
  329.2 6.2 %collective-permute-start.23 = (f32[64,512]{1,0:T(8,128)S(1)}, f32[64,512]{1,0:T(8,128)S(1)}, u32[]{:S(2)}, u32[]{:S(2)}) collective-permute-start(f32[64,512]{1,0:T(8,128)S(1)} %collective-permute-done.21), channel_id=1, source_target_pairs={{0,16},{16,32},{32,48},{48,64},{64,80},{80,96},{96,112},{112,0},{1... | collective-permute-start | bytes 393224 | tf_op jit(solution)/shard_map/ppermute | solution.py:57
  333.3 7.2 %collective-permute-start.26 = (f32[64,512]{1,0:T(8,128)S(1)}, f32[64,512]{1,0:T(8,128)S(1)}, u32[]{:S(2)}, u32[]{:S(2)}) collective-permute-start(f32[64,512]{1,0:T(8,128)S(1)} %collective-permute-done.24), channel_id=1, source_target_pairs={{0,112},{16,0},{32,16},{48,32},{64,48},{80,64},{96,80},{112,96},{1... | collective-permute-start | bytes 393224 | tf_op jit(solution)/shard_map/ppermute | solution.py:58
  335.4 6.6 %collective-permute-start.25 = (f32[64,512]{1,0:T(8,128)S(1)}, f32[64,512]{1,0:T(8,128)S(1)}, u32[]{:S(2)}, u32[]{:S(2)}) collective-permute-start(f32[64,512]{1,0:T(8,128)S(1)} %collective-permute-done.23), channel_id=1, source_target_pairs={{0,16},{16,32},{32,48},{48,64},{64,80},{80,96},{96,112},{112,0},{1... | collective-permute-start | bytes 393224 | tf_op jit(solution)/shard_map/ppermute | solution.py:57
  340.5 7.9 %collective-permute-start.28 = (f32[64,512]{1,0:T(8,128)S(1)}, f32[64,512]{1,0:T(8,128)S(1)}, u32[]{:S(2)}, u32[]{:S(2)}) collective-permute-start(f32[64,512]{1,0:T(8,128)S(1)} %collective-permute-done.26), channel_id=1, source_target_pairs={{0,112},{16,0},{32,16},{48,32},{64,48},{80,64},{96,80},{112,96},{1... | collective-permute-start | bytes 393224 | tf_op jit(solution)/shard_map/ppermute | solution.py:58
  342.0 6.5 %collective-permute-start.27 = (f32[64,512]{1,0:T(8,128)S(1)}, f32[64,512]{1,0:T(8,128)S(1)}, u32[]{:S(2)}, u32[]{:S(2)}) collective-permute-start(f32[64,512]{1,0:T(8,128)S(1)} %collective-permute-done.25), channel_id=1, source_target_pairs={{0,16},{16,32},{32,48},{48,64},{64,80},{80,96},{96,112},{112,0},{1... | collective-permute-start | bytes 393224 | tf_op jit(solution)/shard_map/ppermute | solution.py:57
  348.5 1.6 copy-start
  348.5 2.2 copy-start.1
Sparse Core Ops, SparseCore 0:
  66.0 243.0 all-reduce.1

commit v5 on v2

v5 whole, which is shorter than its diff:
```python
import jax
import jax.numpy as jnp
from jax import lax
from jax.sharding import PartitionSpec as P

D = 8192
HEAD = 128
KVH = 4
RING = 8


def outer_update(average, params, momentum, mean_square):
    factor = jnp.minimum(jnp.float32(1.0), 0.5 / jnp.sqrt(mean_square + 1e-06))
    clipped = factor * average
    new_momentum = 0.9 * momentum + clipped
    new_params = params - 0.7 * (clipped + 0.9 * new_momentum)
    return (new_params, new_momentum)


def ring_pairs(islands, shift):
    groups = islands // RING
    return [(g * RING + z, g * RING + (z + shift) % RING) for g in range(groups) for z in range(RING)]


def body(island_delta, params, momentum):
    islands = lax.axis_size("island")
    inner = lax.axis_size("inner")
    count = 2 * D * KVH * HEAD
    me = lax.axis_index("island")
    z = me % RING
    own = island_delta[0]
    halves, rows, cols = own.shape
    chunk = rows // RING
    x = own.reshape(halves, RING, chunk, cols)
    right, left = ring_pairs(islands, 1), ring_pairs(islands, RING - 1)
    reach_r, reach_l = (RING - 1) // 2, RING // 2

    def take(c):
        return lax.dynamic_index_in_dim(x, c % RING, axis=1, keepdims=False)

    acc_r = take(z + reach_r)
    acc_l = take(z - reach_l)
    for s in range(reach_l):
        if s < reach_r:
            got_r = lax.ppermute(acc_r, "island", right)
            acc_r = got_r if s == reach_r - 1 else got_r + take(z + reach_r - 1 - s)
        got_l = lax.ppermute(acc_l, "island", left)
        acc_l = got_l if s == reach_l - 1 else got_l + take(z - reach_l + 1 + s)
    mine = take(z) + acc_r + acc_l
    partner = [(i, (i + RING) % islands) for i in range(islands)]
    mine = (mine + lax.ppermute(mine, "island", partner)) / islands

    out = jnp.zeros((halves, RING, chunk, cols), jnp.float32)
    out = lax.dynamic_update_slice(out, mine[:, None], (0, z, 0, 0))
    sq = jnp.sum(mine * mine)
    cur_r, cur_l = mine, mine
    for s in range(reach_l):
        if s < reach_r:
            cur_r = lax.ppermute(cur_r, "island", right)
            sq = sq + jnp.sum(cur_r * cur_r)
            out = lax.dynamic_update_slice(out, cur_r[:, None], (0, (z - 1 - s) % RING, 0, 0))
        cur_l = lax.ppermute(cur_l, "island", left)
        sq = sq + jnp.sum(cur_l * cur_l)
        out = lax.dynamic_update_slice(out, cur_l[:, None], (0, (z + 1 + s) % RING, 0, 0))
    average = out.reshape(halves, rows, cols)
    bit = 1
    while bit < inner:
        sq = sq + lax.ppermute(sq, "inner", [(i, i ^ bit) for i in range(inner)])
        bit *= 2
    return outer_update(average, params, momentum, sq / count)


def solution(mesh):
    in_specs = (P("island", None, "inner", None), P(None, "inner", None), P(None, "inner", None))
    out_specs = (P(None, "inner", None), P(None, "inner", None))
    return jax.shard_map(body, mesh=mesh, in_specs=in_specs, out_specs=out_specs, check_vma=False)
```

time: 171 us -> 115 us (0.67)
  the two profiles are of different devices: /device:TPU:32 before, /device:TPU:2 now
where the time goes in v5:
time: 115 us
  waiting for transfers between devices  47.6 us (41%)
  starting transfers between devices  42.2 us (37%)
  other arithmetic  12.6 us (11%)
  between operations  8.66 us (8%)
  local copies, waits for them, and re-layouts  3.47 us (3%)
    ppermute x4, starting transfers between devices, body(): got_l = lax.ppermute(acc_l, 'island', left)  16.6 us
    ppermute x4, waiting for transfers between devices, body(): got_l = lax.ppermute(acc_l, 'island', left)  14.2 us
    ppermute x3, waiting for transfers between devices, body(): cur_r = lax.ppermute(cur_r, 'island', right)  14 us
    ppermute x4, starting transfers between devices, body(): cur_l = lax.ppermute(cur_l, 'island', left)  12.6 us
    ppermute x4, starting transfers between devices, body(): sq = sq + lax.ppermute(sq, 'inner', [(i, i ^ bit) for i in range(inner)])  9.43 us
    ppermute x3, waiting for transfers between devices, body(): got_r = lax.ppermute(acc_r, 'island', right)  8.2 us
    ppermute x4, waiting for transfers between devices, body(): sq = sq + lax.ppermute(sq, 'inner', [(i, i ^ bit) for i in range(inner)])  4.71 us
    ppermute x1, waiting for transfers between devices, body(): mine = (mine + lax.ppermute(mine, 'island', partner)) / islands  4.68 us
  transfers between devices with their start and end apart: 19, of which 14 were waited for; matrix products, arithmetic and copies ran while one was open for 4% of the time, Pallas kernels for 0%

profile of v5, /device:TPU:2, one launch (start us, length us, event | category | flops | bytes accessed | tf_op | source)
XLA Modules:
  0.0 114.5 jit_solution(990974252257903043)
XLA Ops:
  0.7 1.1 dynamic-slice_bitcast_fusion.1
  1.8 5.9 %collective-permute-start.3 = (f32[2,64,512]{2,1,0:T(8,128)S(1)}, f32[2,64,512]{2,1,0:T(8,128)S(1)}, u32[]{:S(2)}, u32[]{:S(2)}) collective-permute-start(f32[2,64,512]{2,1,0:T(8,128)S(1)} %get-tuple-element.11), channel_id=1, source_target_pairs={{0,112},{16,0},{32,16},{48,32},{64,48},{80,64},{96,80},{112,96},{1... | collective-permute-start | bytes 786440 | tf_op jit(solution)/shard_map/ppermute | solution.py:47
  7.7 0.0 collective-permute-start
  7.7 5.6 %collective-permute-done.3 = f32[2,64,512]{2,1,0:T(8,128)S(1)} collective-permute-done((f32[2,64,512]{2,1,0:T(8,128)S(1)}, f32[2,64,512]{2,1,0:T(8,128)S(1)}, u32[]{:S(2)}, u32[]{:S(2)}) %collective-permute-start.3) | collective-permute-done | bytes 262176 | tf_op jit(solution)/shard_map/ppermute | solution.py:47
  13.3 1.0 bitcast_add_fusion.4
  14.2 3.8 %collective-permute-start.4 = (f32[2,64,512]{2,1,0:T(8,128)S(1)}, f32[2,64,512]{2,1,0:T(8,128)S(1)}, u32[]{:S(2)}, u32[]{:S(2)}) collective-permute-start(f32[2,64,512]{2,1,0:T(8,128)S(1)} %bitcast_add_fusion.4), channel_id=1, source_target_pairs={{0,112},{16,0},{32,16},{48,32},{64,48},{80,64},{96,80},{112,96},{1... | collective-permute-start | bytes 786440 | tf_op jit(solution)/shard_map/ppermute | solution.py:47
  18.0 0.0 collective-permute-done
  18.0 4.7 %collective-permute-done.4 = f32[2,64,512]{2,1,0:T(8,128)S(1)} collective-permute-done((f32[2,64,512]{2,1,0:T(8,128)S(1)}, f32[2,64,512]{2,1,0:T(8,128)S(1)}, u32[]{:S(2)}, u32[]{:S(2)}) %collective-permute-start.4) | collective-permute-done | bytes 262176 | tf_op jit(solution)/shard_map/ppermute | solution.py:47
  22.7 1.1 bitcast_add_fusion.6
  23.8 0.1 collective-permute-start.1
  23.9 3.8 %collective-permute-start.5 = (f32[2,64,512]{2,1,0:T(8,128)S(1)}, f32[2,64,512]{2,1,0:T(8,128)S(1)}, u32[]{:S(2)}, u32[]{:S(2)}) collective-permute-start(f32[2,64,512]{2,1,0:T(8,128)S(1)} %get-tuple-element.9), channel_id=1, source_target_pairs={{0,112},{16,0},{32,16},{48,32},{64,48},{80,64},{96,80},{112,96},{1... | collective-permute-start | bytes 786440 | tf_op jit(solution)/shard_map/ppermute | solution.py:47
  27.7 4.5 %collective-permute-done.1 = f32[2,64,512]{2,1,0:T(8,128)S(1)} collective-permute-done((f32[2,64,512]{2,1,0:T(8,128)S(1)}, f32[2,64,512]{2,1,0:T(8,128)S(1)}, u32[]{:S(2)}, u32[]{:S(2)}) %collective-permute-start.1) | collective-permute-done | bytes 262176 | tf_op jit(solution)/shard_map/ppermute | solution.py:45
  32.2 0.0 collective-permute-done.5
  32.2 1.1 bitcast_add_fusion.5
  33.3 3.1 %collective-permute-start.6 = (f32[2,64,512]{2,1,0:T(8,128)S(1)}, f32[2,64,512]{2,1,0:T(8,128)S(1)}, u32[]{:S(2)}, u32[]{:S(2)}) collective-permute-start(f32[2,64,512]{2,1,0:T(8,128)S(1)} %get-tuple-element.7), channel_id=1, source_target_pairs={{0,112},{16,0},{32,16},{48,32},{64,48},{80,64},{96,80},{112,96},{1... | collective-permute-start | bytes 786440 | tf_op jit(solution)/shard_map/ppermute | solution.py:47
  36.5 0.0 collective-permute-start.2
  36.5 3.9 %collective-permute-done.6 = f32[2,64,512]{2,1,0:T(8,128)S(1)} collective-permute-done((f32[2,64,512]{2,1,0:T(8,128)S(1)}, f32[2,64,512]{2,1,0:T(8,128)S(1)}, u32[]{:S(2)}, u32[]{:S(2)}) %collective-permute-start.6) | collective-permute-done | bytes 262176 | tf_op jit(solution)/shard_map/ppermute | solution.py:47
  40.4 3.7 %collective-permute-done.2 = f32[2,64,512]{2,1,0:T(8,128)S(1)} collective-permute-done((f32[2,64,512]{2,1,0:T(8,128)S(1)}, f32[2,64,512]{2,1,0:T(8,128)S(1)}, u32[]{:S(2)}, u32[]{:S(2)}) %collective-permute-start.2) | collective-permute-done | bytes 262176 | tf_op jit(solution)/shard_map/ppermute | solution.py:45
  44.0 1.0 fusion.2
  45.1 3.3 %collective-permute-start.7 = (f32[2,64,512]{2,1,0:T(8,128)S(1)}, f32[2,64,512]{2,1,0:T(8,128)S(1)}, u32[]{:S(2)}, u32[]{:S(2)}) collective-permute-start(f32[2,64,512]{2,1,0:T(8,128)S(1)} %fusion.2), channel_id=1, source_target_pairs={{0,128},{16,144},{32,160},{48,176},{64,192},{80,208},{96,224},{112... | collective-permute-start | bytes 786440 | tf_op jit(solution)/shard_map/ppermute | solution.py:51
  48.3 4.7 %collective-permute-done.7 = f32[2,64,512]{2,1,0:T(8,128)S(1)} collective-permute-done((f32[2,64,512]{2,1,0:T(8,128)S(1)}, f32[2,64,512]{2,1,0:T(8,128)S(1)}, u32[]{:S(2)}, u32[]{:S(2)}) %collective-permute-start.7) | collective-permute-done | bytes 262176 | tf_op jit(solution)/shard_map/ppermute | solution.py:51
  53.0 0.7 multiply_reduce_fusion.7
  53.7 0.0 collective-permute-start.8
  53.7 3.2 %collective-permute-start.9 = (f32[2,64,512]{2,1,0:T(8,128)S(1)}, f32[2,64,512]{2,1,0:T(8,128)S(1)}, u32[]{:S(2)}, u32[]{:S(2)}) collective-permute-start(f32[2,64,512]{2,1,0:T(8,128)S(1)} %get-tuple-element.5), channel_id=1, source_target_pairs={{0,112},{16,0},{32,16},{48,32},{64,48},{80,64},{96,80},{112,96},{1... | collective-permute-start | bytes 786440 | tf_op jit(solution)/shard_map/ppermute | solution.py:62
  56.9 0.2 broadcast_in_dim.27
  57.2 4.1 %collective-permute-done.8 = f32[2,64,512]{2,1,0:T(8,128)S(1)} collective-permute-done((f32[2,64,512]{2,1,0:T(8,128)S(1)}, f32[2,64,512]{2,1,0:T(8,128)S(1)}, u32[]{:S(2)}, u32[]{:S(2)}) %collective-permute-start.8) | collective-permute-done | bytes 262176 | tf_op jit(solution)/shard_map/ppermute | solution.py:59
  61.3 0.7 multiply_reduce_fusion.6
  63.2 0.0 collective-permute-done.9
  63.3 0.7 multiply_reduce_fusion.5
  64.6 0.1 collective-permute-start.10
  64.7 3.2 %collective-permute-start.11 = (f32[2,64,512]{2,1,0:T(8,128)S(1)}, f32[2,64,512]{2,1,0:T(8,128)S(1)}, u32[]{:S(2)}, u32[]{:S(2)}) collective-permute-start(f32[2,64,512]{2,1,0:T(8,128)S(1)} %collective-permute-done.9), channel_id=1, source_target_pairs={{0,112},{16,0},{32,16},{48,32},{64,48},{80,64},{96,80},{112,96},{1... | collective-permute-start | bytes 786440 | tf_op jit(solution)/shard_map/ppermute | solution.py:62
  68.0 5.7 %collective-permute-done.10 = f32[2,64,512]{2,1,0:T(8,128)S(1)} collective-permute-done((f32[2,64,512]{2,1,0:T(8,128)S(1)}, f32[2,64,512]{2,1,0:T(8,128)S(1)}, u32[]{:S(2)}, u32[]{:S(2)}) %collective-permute-start.10) | collective-permute-done | bytes 262176 | tf_op jit(solution)/shard_map/ppermute | solution.py:59
  73.6 0.7 multiply_reduce_fusion.4
  74.9 0.0 collective-permute-done.11
  74.9 0.7 multiply_reduce_fusion.3
  76.3 0.1 collective-permute-start.12
  76.3 3.2 %collective-permute-start.13 = (f32[2,64,512]{2,1,0:T(8,128)S(1)}, f32[2,64,512]{2,1,0:T(8,128)S(1)}, u32[]{:S(2)}, u32[]{:S(2)}) collective-permute-start(f32[2,64,512]{2,1,0:T(8,128)S(1)} %collective-permute-done.11), channel_id=1, source_target_pairs={{0,112},{16,0},{32,16},{48,32},{64,48},{80,64},{96,80},{112,96},{1... | collective-permute-start | bytes 786440 | tf_op jit(solution)/shard_map/ppermute | solution.py:62
  79.6 4.3 %collective-permute-done.12 = f32[2,64,512]{2,1,0:T(8,128)S(1)} collective-permute-done((f32[2,64,512]{2,1,0:T(8,128)S(1)}, f32[2,64,512]{2,1,0:T(8,128)S(1)}, u32[]{:S(2)}, u32[]{:S(2)}) %collective-permute-start.12) | collective-permute-done | bytes 262176 | tf_op jit(solution)/shard_map/ppermute | solution.py:59
  83.9 0.7 multiply_reduce_fusion.2
  84.6 0.0 collective-permute-done.13
  84.6 2.9 %collective-permute-start.14 = (f32[2,64,512]{2,1,0:T(8,128)S(1)}, f32[2,64,512]{2,1,0:T(8,128)S(1)}, u32[]{:S(2)}, u32[]{:S(2)}) collective-permute-start(f32[2,64,512]{2,1,0:T(8,128)S(1)} %collective-permute-done.13), channel_id=1, source_target_pairs={{0,112},{16,0},{32,16},{48,32},{64,48},{80,64},{96,80},{112,96},{1... | collective-permute-start | bytes 786440 | tf_op jit(solution)/shard_map/ppermute | solution.py:62
  87.5 0.7 multiply_reduce_fusion.1
  89.5 1.9 %collective-permute-done.14 = f32[2,64,512]{2,1,0:T(8,128)S(1)} collective-permute-done((f32[2,64,512]{2,1,0:T(8,128)S(1)}, f32[2,64,512]{2,1,0:T(8,128)S(1)}, u32[]{:S(2)}, u32[]{:S(2)}) %collective-permute-start.14) | collective-permute-done | bytes 262176 | tf_op jit(solution)/shard_map/ppermute | solution.py:62
  91.4 0.7 multiply_reduce_fusion
  92.7 1.0 collective-permute-start.15
  93.8 0.3 collective-permute-done.15
  94.8 1.9 %collective-permute-start.16 = (f32[]{:T(128)}, f32[]{:T(128)}, u32[]{:S(2)}, u32[]{:S(2)}) collective-permute-start(f32[]{:T(128)} %add.231), channel_id=1, source_target_pairs={{0,2},{1,3},{2,0},{3,1},{4,6},{5,7},{6,4},{7,5},{8,10},{9,11},{10,... | collective-permute-start | bytes 20 | tf_op jit(solution)/shard_map/ppermute | solution.py:68
  96.7 1.8 %collective-permute-done.16 = f32[]{:T(128)} collective-permute-done((f32[]{:T(128)}, f32[]{:T(128)}, u32[]{:S(2)}, u32[]{:S(2)}) %collective-permute-start.16) | collective-permute-done | bytes 36 | tf_op jit(solution)/shard_map/ppermute | solution.py:68
  99.2 3.5 %collective-permute-start.17 = (f32[]{:T(128)}, f32[]{:T(128)}, u32[]{:S(2)}, u32[]{:S(2)}) collective-permute-start(f32[]{:T(128)} %add.232), channel_id=1, source_target_pairs={{0,4},{1,5},{2,6},{3,7},{4,0},{5,1},{6,2},{7,3},{8,12},{9,13},{10,... | collective-permute-start | bytes 20 | tf_op jit(solution)/shard_map/ppermute | solution.py:68
  102.7 1.8 %collective-permute-done.17 = f32[]{:T(128)} collective-permute-done((f32[]{:T(128)}, f32[]{:T(128)}, u32[]{:S(2)}, u32[]{:S(2)}) %collective-permute-start.17) | collective-permute-done | bytes 36 | tf_op jit(solution)/shard_map/ppermute | solution.py:68
  105.1 3.0 %collective-permute-start.18 = (f32[]{:T(128)}, f32[]{:T(128)}, u32[]{:S(2)}, u32[]{:S(2)}) collective-permute-start(f32[]{:T(128)} %add.233), channel_id=1, source_target_pairs={{0,8},{1,9},{2,10},{3,11},{4,12},{5,13},{6,14},{7,15},{8,0},{9,1},... | collective-permute-start | bytes 20 | tf_op jit(solution)/shard_map/ppermute | solution.py:68
  108.0 0.8 collective-permute-done.18
  109.5 0.0 copy-start
  109.5 0.0 copy-start.1
  109.5 0.2 broadcast_multiply_fusion
  109.8 1.3 %copy-done = f32[2,512,512]{2,1,0:T(8,128)S(1)} copy-done((f32[2,512,512]{2,1,0:T(8,128)S(1)}, f32[2,512,512]{2,1,0:T(8,128)}, u32[]{:S(2)}) %copy-start) | copy-done | bytes 2097176
  111.1 0.6 copy-done.1
  111.7 2.8 %fusion.1 = (f32[2,512,512]{2,1,0:T(8,128)}, f32[2,512,512]{2,1,0:T(8,128)}) fusion(f32[2,512,512]{2,1,0:T(8,128)S(1)} %copy-done, f32[2,8,64,512]{3,2,1,0:T(8,128)S(1)} %broadcast_multiply_fusion, f32[2,512,512]{2,1,0:T(8,128)S(1)} %copy-done.1), kind=kLoop, calls=%fused_computation.3 | loop fusion | flops 3145728 | bytes 10485760 | tf_op jit(solution)/shard_map/sub | solution.py:16
  (8 shorter events, 0.2 us)
Async XLA Ops:
  1.8 11.5 %collective-permute-start.3 = (f32[2,64,512]{2,1,0:T(8,128)S(1)}, f32[2,64,512]{2,1,0:T(8,128)S(1)}, u32[]{:S(2)}, u32[]{:S(2)}) collective-permute-start(f32[2,64,512]{2,1,0:T(8,128)S(1)} %get-tuple-element.11), channel_id=1, source_target_pairs={{0,112},{16,0},{32,16},{48,32},{64,48},{80,64},{96,80},{112,96},{1... | collective-permute-start | bytes 786440 | tf_op jit(solution)/shard_map/ppermute | solution.py:47
  7.7 10.3 %collective-permute-start = (f32[2,64,512]{2,1,0:T(8,128)S(1)}, f32[2,64,512]{2,1,0:T(8,128)S(1)}, u32[]{:S(2)}, u32[]{:S(2)}) collective-permute-start(f32[2,64,512]{2,1,0:T(8,128)S(1)} %get-tuple-element.10), channel_id=1, source_target_pairs={{0,16},{16,32},{32,48},{48,64},{64,80},{80,96},{96,112},{112,0},{1... | collective-permute-start | bytes 786440 | tf_op jit(solution)/shard_map/ppermute | solution.py:45
  14.2 8.5 %collective-permute-start.4 = (f32[2,64,512]{2,1,0:T(8,128)S(1)}, f32[2,64,512]{2,1,0:T(8,128)S(1)}, u32[]{:S(2)}, u32[]{:S(2)}) collective-permute-start(f32[2,64,512]{2,1,0:T(8,128)S(1)} %bitcast_add_fusion.4), channel_id=1, source_target_pairs={{0,112},{16,0},{32,16},{48,32},{64,48},{80,64},{96,80},{112,96},{1... | collective-permute-start | bytes 786440 | tf_op jit(solution)/shard_map/ppermute | solution.py:47
  23.8 8.4 %collective-permute-start.1 = (f32[2,64,512]{2,1,0:T(8,128)S(1)}, f32[2,64,512]{2,1,0:T(8,128)S(1)}, u32[]{:S(2)}, u32[]{:S(2)}) collective-permute-start(f32[2,64,512]{2,1,0:T(8,128)S(1)} %get-tuple-element.8), channel_id=1, source_target_pairs={{0,16},{16,32},{32,48},{48,64},{64,80},{80,96},{96,112},{112,0},{1... | collective-permute-start | bytes 786440 | tf_op jit(solution)/shard_map/ppermute | solution.py:45
  23.9 8.3 %collective-permute-start.5 = (f32[2,64,512]{2,1,0:T(8,128)S(1)}, f32[2,64,512]{2,1,0:T(8,128)S(1)}, u32[]{:S(2)}, u32[]{:S(2)}) collective-permute-start(f32[2,64,512]{2,1,0:T(8,128)S(1)} %get-tuple-element.9), channel_id=1, source_target_pairs={{0,112},{16,0},{32,16},{48,32},{64,48},{80,64},{96,80},{112,96},{1... | collective-permute-start | bytes 786440 | tf_op jit(solution)/shard_map/ppermute | solution.py:47
  33.3 7.0 %collective-permute-start.6 = (f32[2,64,512]{2,1,0:T(8,128)S(1)}, f32[2,64,512]{2,1,0:T(8,128)S(1)}, u32[]{:S(2)}, u32[]{:S(2)}) collective-permute-start(f32[2,64,512]{2,1,0:T(8,128)S(1)} %get-tuple-element.7), channel_id=1, source_target_pairs={{0,112},{16,0},{32,16},{48,32},{64,48},{80,64},{96,80},{112,96},{1... | collective-permute-start | bytes 786440 | tf_op jit(solution)/shard_map/ppermute | solution.py:47
  36.5 7.6 %collective-permute-start.2 = (f32[2,64,512]{2,1,0:T(8,128)S(1)}, f32[2,64,512]{2,1,0:T(8,128)S(1)}, u32[]{:S(2)}, u32[]{:S(2)}) collective-permute-start(f32[2,64,512]{2,1,0:T(8,128)S(1)} %get-tuple-element.6), channel_id=1, source_target_pairs={{0,16},{16,32},{32,48},{48,64},{64,80},{80,96},{96,112},{112,0},{1... | collective-permute-start | bytes 786440 | tf_op jit(solution)/shard_map/ppermute | solution.py:45
  45.1 8.0 %collective-permute-start.7 = (f32[2,64,512]{2,1,0:T(8,128)S(1)}, f32[2,64,512]{2,1,0:T(8,128)S(1)}, u32[]{:S(2)}, u32[]{:S(2)}) collective-permute-start(f32[2,64,512]{2,1,0:T(8,128)S(1)} %fusion.2), channel_id=1, source_target_pairs={{0,128},{16,144},{32,160},{48,176},{64,192},{80,208},{96,224},{112... | collective-permute-start | bytes 786440 | tf_op jit(solution)/shard_map/ppermute | solution.py:51
  53.7 7.6 %collective-permute-start.8 = (f32[2,64,512]{2,1,0:T(8,128)S(1)}, f32[2,64,512]{2,1,0:T(8,128)S(1)}, u32[]{:S(2)}, u32[]{:S(2)}) collective-permute-start(f32[2,64,512]{2,1,0:T(8,128)S(1)} %get-tuple-element.5), channel_id=1, source_target_pairs={{0,16},{16,32},{32,48},{48,64},{64,80},{80,96},{96,112},{112,0},{1... | collective-permute-start | bytes 786440 | tf_op jit(solution)/shard_map/ppermute | solution.py:59
  53.7 9.5 %collective-permute-start.9 = (f32[2,64,512]{2,1,0:T(8,128)S(1)}, f32[2,64,512]{2,1,0:T(8,128)S(1)}, u32[]{:S(2)}, u32[]{:S(2)}) collective-permute-start(f32[2,64,512]{2,1,0:T(8,128)S(1)} %get-tuple-element.5), channel_id=1, source_target_pairs={{0,112},{16,0},{32,16},{48,32},{64,48},{80,64},{96,80},{112,96},{1... | collective-permute-start | bytes 786440 | tf_op jit(solution)/shard_map/ppermute | solution.py:62
  64.6 9.0 %collective-permute-start.10 = (f32[2,64,512]{2,1,0:T(8,128)S(1)}, f32[2,64,512]{2,1,0:T(8,128)S(1)}, u32[]{:S(2)}, u32[]{:S(2)}) collective-permute-start(f32[2,64,512]{2,1,0:T(8,128)S(1)} %collective-permute-done.8), channel_id=1, source_target_pairs={{0,16},{16,32},{32,48},{48,64},{64,80},{80,96},{96,112},{112,0},{1... | collective-permute-start | bytes 786440 | tf_op jit(solution)/shard_map/ppermute | solution.py:59
  64.7 10.3 %collective-permute-start.11 = (f32[2,64,512]{2,1,0:T(8,128)S(1)}, f32[2,64,512]{2,1,0:T(8,128)S(1)}, u32[]{:S(2)}, u32[]{:S(2)}) collective-permute-start(f32[2,64,512]{2,1,0:T(8,128)S(1)} %collective-permute-done.9), channel_id=1, source_target_pairs={{0,112},{16,0},{32,16},{48,32},{64,48},{80,64},{96,80},{112,96},{1... | collective-permute-start | bytes 786440 | tf_op jit(solution)/shard_map/ppermute | solution.py:62
  76.3 7.7 %collective-permute-start.12 = (f32[2,64,512]{2,1,0:T(8,128)S(1)}, f32[2,64,512]{2,1,0:T(8,128)S(1)}, u32[]{:S(2)}, u32[]{:S(2)}) collective-permute-start(f32[2,64,512]{2,1,0:T(8,128)S(1)} %collective-permute-done.10), channel_id=1, source_target_pairs={{0,16},{16,32},{32,48},{48,64},{64,80},{80,96},{96,112},{112,0},{1... | collective-permute-start | bytes 786440 | tf_op jit(solution)/shard_map/ppermute | solution.py:59
  76.3 8.3 %collective-permute-start.13 = (f32[2,64,512]{2,1,0:T(8,128)S(1)}, f32[2,64,512]{2,1,0:T(8,128)S(1)}, u32[]{:S(2)}, u32[]{:S(2)}) collective-permute-start(f32[2,64,512]{2,1,0:T(8,128)S(1)} %collective-permute-done.11), channel_id=1, source_target_pairs={{0,112},{16,0},{32,16},{48,32},{64,48},{80,64},{96,80},{112,96},{1... | collective-permute-start | bytes 786440 | tf_op jit(solution)/shard_map/ppermute | solution.py:62
  84.6 6.8 %collective-permute-start.14 = (f32[2,64,512]{2,1,0:T(8,128)S(1)}, f32[2,64,512]{2,1,0:T(8,128)S(1)}, u32[]{:S(2)}, u32[]{:S(2)}) collective-permute-start(f32[2,64,512]{2,1,0:T(8,128)S(1)} %collective-permute-done.13), channel_id=1, source_target_pairs={{0,112},{16,0},{32,16},{48,32},{64,48},{80,64},{96,80},{112,96},{1... | collective-permute-start | bytes 786440 | tf_op jit(solution)/shard_map/ppermute | solution.py:62
  92.7 1.4 %collective-permute-start.15 = (f32[]{:T(128)}, f32[]{:T(128)}, u32[]{:S(2)}, u32[]{:S(2)}) collective-permute-start(f32[]{:T(128)} %add.230), channel_id=1, source_target_pairs={{0,1},{1,0},{2,3},{3,2},{4,5},{5,4},{6,7},{7,6},{8,9},{9,8},{10,11... | collective-permute-start | bytes 20 | tf_op jit(solution)/shard_map/ppermute | solution.py:68
  94.8 3.8 %collective-permute-start.16 = (f32[]{:T(128)}, f32[]{:T(128)}, u32[]{:S(2)}, u32[]{:S(2)}) collective-permute-start(f32[]{:T(128)} %add.231), channel_id=1, source_target_pairs={{0,2},{1,3},{2,0},{3,1},{4,6},{5,7},{6,4},{7,5},{8,10},{9,11},{10,... | collective-permute-start | bytes 20 | tf_op jit(solution)/shard_map/ppermute | solution.py:68
  99.2 5.3 %collective-permute-start.17 = (f32[]{:T(128)}, f32[]{:T(128)}, u32[]{:S(2)}, u32[]{:S(2)}) collective-permute-start(f32[]{:T(128)} %add.232), channel_id=1, source_target_pairs={{0,4},{1,5},{2,6},{3,7},{4,0},{5,1},{6,2},{7,3},{8,12},{9,13},{10,... | collective-permute-start | bytes 20 | tf_op jit(solution)/shard_map/ppermute | solution.py:68
  105.1 3.8 %collective-permute-start.18 = (f32[]{:T(128)}, f32[]{:T(128)}, u32[]{:S(2)}, u32[]{:S(2)}) collective-permute-start(f32[]{:T(128)} %add.233), channel_id=1, source_target_pairs={{0,8},{1,9},{2,10},{3,11},{4,12},{5,13},{6,14},{7,15},{8,0},{9,1},... | collective-permute-start | bytes 20 | tf_op jit(solution)/shard_map/ppermute | solution.py:68
  109.5 1.6 %copy-start = (f32[2,512,512]{2,1,0:T(8,128)S(1)}, f32[2,512,512]{2,1,0:T(8,128)}, u32[]{:S(2)}) copy-start(f32[2,512,512]{2,1,0:T(8,128)} %param.4) | copy-start | bytes 6291460
  109.5 2.2 %copy-start.1 = (f32[2,512,512]{2,1,0:T(8,128)S(1)}, f32[2,512,512]{2,1,0:T(8,128)}, u32[]{:S(2)}) copy-start(f32[2,512,512]{2,1,0:T(8,128)} %param.5) | copy-start | bytes 6291460

commit v6 on v5

--- a/solution.py
+++ b/solution.py
@@ -63,10 +63,7 @@
         sq = sq + jnp.sum(cur_l * cur_l)
         out = lax.dynamic_update_slice(out, cur_l[:, None], (0, (z + 1 + s) % RING, 0, 0))
     average = out.reshape(halves, rows, cols)
-    bit = 1
-    while bit < inner:
-        sq = sq + lax.ppermute(sq, "inner", [(i, i ^ bit) for i in range(inner)])
-        bit *= 2
+    sq = jnp.sum(lax.all_to_all(jnp.full((inner, 1), sq), "inner", 0, 0, tiled=True))
     return outer_update(average, params, momentum, sq / count)
 
 

time: 115 us -> 112 us (0.974)
  the two profiles are of different devices: /device:TPU:2 before, /device:TPU:1 now
where the time goes in v6:
time: 112 us
  starting transfers between devices  44.3 us (40%)
  waiting for transfers between devices  43.6 us (39%)
  other arithmetic  13.2 us (12%)
  between operations  6.75 us (6%)
  local copies, waits for them, and re-layouts  4.07 us (4%)
    ppermute x4, starting transfers between devices, body(): got_l = lax.ppermute(acc_l, 'island', left)  15.7 us
    all_to_all x1, starting transfers between devices, body(): lax.all_to_all(jnp.full((inner, 1), sq), 'inner', 0, 0, tiled=True)  15 us
    ppermute x4, waiting for transfers between devices, body(): got_l = lax.ppermute(acc_l, 'island', left)  12.4 us
    ppermute x3, waiting for transfers between devices, body(): cur_r = lax.ppermute(cur_r, 'island', right)  12.2 us
    ppermute x4, starting transfers between devices, body(): cur_l = lax.ppermute(cur_l, 'island', left)  10.3 us
    ppermute x3, waiting for transfers between devices, body(): got_r = lax.ppermute(acc_r, 'island', right)  7.33 us
    all_to_all x1, waiting for transfers between devices, body(): lax.all_to_all(jnp.full((inner, 1), sq), 'inner', 0, 0, tiled=True)  5.41 us
    ppermute x1, waiting for transfers between devices, body(): mine = (mine + lax.ppermute(mine, 'island', partner)) / islands  3.81 us
  transfers between devices with their start and end apart: 16, of which 11 were waited for; matrix products, arithmetic and copies ran while one was open for 4% of the time, Pallas kernels for 0%

profile of v6, /device:TPU:1, one launch (start us, length us, event | category | flops | bytes accessed | tf_op | source)
XLA Modules:
  0.0 111.9 jit_solution(4331486105968212366)
XLA Ops:
  0.7 1.1 dynamic-slice_bitcast_fusion.1
  1.8 6.5 %collective-permute-start.3 = (f32[2,64,512]{2,1,0:T(8,128)S(1)}, f32[2,64,512]{2,1,0:T(8,128)S(1)}, u32[]{:S(2)}, u32[]{:S(2)}) collective-permute-start(f32[2,64,512]{2,1,0:T(8,128)S(1)} %get-tuple-element.11), channel_id=1, source_target_pairs={{0,112},{16,0},{32,16},{48,32},{64,48},{80,64},{96,80},{112,96},{1... | collective-permute-start | bytes 786440 | tf_op jit(solution)/shard_map/ppermute | solution.py:47
  8.2 0.0 collective-permute-start
  8.2 5.0 %collective-permute-done.3 = f32[2,64,512]{2,1,0:T(8,128)S(1)} collective-permute-done((f32[2,64,512]{2,1,0:T(8,128)S(1)}, f32[2,64,512]{2,1,0:T(8,128)S(1)}, u32[]{:S(2)}, u32[]{:S(2)}) %collective-permute-start.3) | collective-permute-done | bytes 262176 | tf_op jit(solution)/shard_map/ppermute | solution.py:47
  13.2 1.0 bitcast_add_fusion.4
  14.2 3.5 %collective-permute-start.4 = (f32[2,64,512]{2,1,0:T(8,128)S(1)}, f32[2,64,512]{2,1,0:T(8,128)S(1)}, u32[]{:S(2)}, u32[]{:S(2)}) collective-permute-start(f32[2,64,512]{2,1,0:T(8,128)S(1)} %bitcast_add_fusion.4), channel_id=1, source_target_pairs={{0,112},{16,0},{32,16},{48,32},{64,48},{80,64},{96,80},{112,96},{1... | collective-permute-start | bytes 786440 | tf_op jit(solution)/shard_map/ppermute | solution.py:47
  17.7 0.0 collective-permute-done
  17.7 4.1 %collective-permute-done.4 = f32[2,64,512]{2,1,0:T(8,128)S(1)} collective-permute-done((f32[2,64,512]{2,1,0:T(8,128)S(1)}, f32[2,64,512]{2,1,0:T(8,128)S(1)}, u32[]{:S(2)}, u32[]{:S(2)}) %collective-permute-start.4) | collective-permute-done | bytes 262176 | tf_op jit(solution)/shard_map/ppermute | solution.py:47
  21.8 1.1 bitcast_add_fusion.6
  22.9 0.1 collective-permute-start.1
  23.0 3.5 %collective-permute-start.5 = (f32[2,64,512]{2,1,0:T(8,128)S(1)}, f32[2,64,512]{2,1,0:T(8,128)S(1)}, u32[]{:S(2)}, u32[]{:S(2)}) collective-permute-start(f32[2,64,512]{2,1,0:T(8,128)S(1)} %get-tuple-element.9), channel_id=1, source_target_pairs={{0,112},{16,0},{32,16},{48,32},{64,48},{80,64},{96,80},{112,96},{1... | collective-permute-start | bytes 786440 | tf_op jit(solution)/shard_map/ppermute | solution.py:47
  26.5 4.2 %collective-permute-done.1 = f32[2,64,512]{2,1,0:T(8,128)S(1)} collective-permute-done((f32[2,64,512]{2,1,0:T(8,128)S(1)}, f32[2,64,512]{2,1,0:T(8,128)S(1)}, u32[]{:S(2)}, u32[]{:S(2)}) %collective-permute-start.1) | collective-permute-done | bytes 262176 | tf_op jit(solution)/shard_map/ppermute | solution.py:45
  30.7 0.0 collective-permute-done.5
  30.7 1.1 bitcast_add_fusion.5
  31.8 2.3 %collective-permute-start.6 = (f32[2,64,512]{2,1,0:T(8,128)S(1)}, f32[2,64,512]{2,1,0:T(8,128)S(1)}, u32[]{:S(2)}, u32[]{:S(2)}) collective-permute-start(f32[2,64,512]{2,1,0:T(8,128)S(1)} %get-tuple-element.7), channel_id=1, source_target_pairs={{0,112},{16,0},{32,16},{48,32},{64,48},{80,64},{96,80},{112,96},{1... | collective-permute-start | bytes 786440 | tf_op jit(solution)/shard_map/ppermute | solution.py:47
  34.1 0.0 collective-permute-start.2
  34.1 3.3 %collective-permute-done.6 = f32[2,64,512]{2,1,0:T(8,128)S(1)} collective-permute-done((f32[2,64,512]{2,1,0:T(8,128)S(1)}, f32[2,64,512]{2,1,0:T(8,128)S(1)}, u32[]{:S(2)}, u32[]{:S(2)}) %collective-permute-start.6) | collective-permute-done | bytes 262176 | tf_op jit(solution)/shard_map/ppermute | solution.py:47
  37.5 3.1 %collective-permute-done.2 = f32[2,64,512]{2,1,0:T(8,128)S(1)} collective-permute-done((f32[2,64,512]{2,1,0:T(8,128)S(1)}, f32[2,64,512]{2,1,0:T(8,128)S(1)}, u32[]{:S(2)}, u32[]{:S(2)}) %collective-permute-start.2) | collective-permute-done | bytes 262176 | tf_op jit(solution)/shard_map/ppermute | solution.py:45
  40.6 1.0 fusion.2
  41.6 3.0 %collective-permute-start.7 = (f32[2,64,512]{2,1,0:T(8,128)S(1)}, f32[2,64,512]{2,1,0:T(8,128)S(1)}, u32[]{:S(2)}, u32[]{:S(2)}) collective-permute-start(f32[2,64,512]{2,1,0:T(8,128)S(1)} %fusion.2), channel_id=1, source_target_pairs={{0,128},{16,144},{32,160},{48,176},{64,192},{80,208},{96,224},{112... | collective-permute-start | bytes 786440 | tf_op jit(solution)/shard_map/ppermute | solution.py:51
  44.6 3.8 %collective-permute-done.7 = f32[2,64,512]{2,1,0:T(8,128)S(1)} collective-permute-done((f32[2,64,512]{2,1,0:T(8,128)S(1)}, f32[2,64,512]{2,1,0:T(8,128)S(1)}, u32[]{:S(2)}, u32[]{:S(2)}) %collective-permute-start.7) | collective-permute-done | bytes 262176 | tf_op jit(solution)/shard_map/ppermute | solution.py:51
  48.4 0.7 multiply_reduce_fusion.7
  49.1 0.0 collective-permute-start.8
  49.1 2.7 %collective-permute-start.9 = (f32[2,64,512]{2,1,0:T(8,128)S(1)}, f32[2,64,512]{2,1,0:T(8,128)S(1)}, u32[]{:S(2)}, u32[]{:S(2)}) collective-permute-start(f32[2,64,512]{2,1,0:T(8,128)S(1)} %get-tuple-element.5), channel_id=1, source_target_pairs={{0,112},{16,0},{32,16},{48,32},{64,48},{80,64},{96,80},{112,96},{1... | collective-permute-start | bytes 786440 | tf_op jit(solution)/shard_map/ppermute | solution.py:62
  51.8 0.2 broadcast_in_dim.31
  52.0 3.5 %collective-permute-done.8 = f32[2,64,512]{2,1,0:T(8,128)S(1)} collective-permute-done((f32[2,64,512]{2,1,0:T(8,128)S(1)}, f32[2,64,512]{2,1,0:T(8,128)S(1)}, u32[]{:S(2)}, u32[]{:S(2)}) %collective-permute-start.8) | collective-permute-done | bytes 262176 | tf_op jit(solution)/shard_map/ppermute | solution.py:59
  55.5 0.7 multiply_reduce_fusion.6
  57.5 0.0 collective-permute-done.9
  57.5 0.7 multiply_reduce_fusion.5
  58.8 0.1 collective-permute-start.10
  58.9 2.7 %collective-permute-start.11 = (f32[2,64,512]{2,1,0:T(8,128)S(1)}, f32[2,64,512]{2,1,0:T(8,128)S(1)}, u32[]{:S(2)}, u32[]{:S(2)}) collective-permute-start(f32[2,64,512]{2,1,0:T(8,128)S(1)} %collective-permute-done.9), channel_id=1, source_target_pairs={{0,112},{16,0},{32,16},{48,32},{64,48},{80,64},{96,80},{112,96},{1... | collective-permute-start | bytes 786440 | tf_op jit(solution)/shard_map/ppermute | solution.py:62
  61.6 3.7 %collective-permute-done.10 = f32[2,64,512]{2,1,0:T(8,128)S(1)} collective-permute-done((f32[2,64,512]{2,1,0:T(8,128)S(1)}, f32[2,64,512]{2,1,0:T(8,128)S(1)}, u32[]{:S(2)}, u32[]{:S(2)}) %collective-permute-start.10) | collective-permute-done | bytes 262176 | tf_op jit(solution)/shard_map/ppermute | solution.py:59
  65.3 0.7 multiply_reduce_fusion.4
  66.6 0.0 collective-permute-done.11
  66.6 0.7 multiply_reduce_fusion.3
  68.0 0.1 collective-permute-start.12
  68.1 2.7 %collective-permute-start.13 = (f32[2,64,512]{2,1,0:T(8,128)S(1)}, f32[2,64,512]{2,1,0:T(8,128)S(1)}, u32[]{:S(2)}, u32[]{:S(2)}) collective-permute-start(f32[2,64,512]{2,1,0:T(8,128)S(1)} %collective-permute-done.11), channel_id=1, source_target_pairs={{0,112},{16,0},{32,16},{48,32},{64,48},{80,64},{96,80},{112,96},{1... | collective-permute-start | bytes 786440 | tf_op jit(solution)/shard_map/ppermute | solution.py:62
  70.8 5.1 %collective-permute-done.12 = f32[2,64,512]{2,1,0:T(8,128)S(1)} collective-permute-done((f32[2,64,512]{2,1,0:T(8,128)S(1)}, f32[2,64,512]{2,1,0:T(8,128)S(1)}, u32[]{:S(2)}, u32[]{:S(2)}) %collective-permute-start.12) | collective-permute-done | bytes 262176 | tf_op jit(solution)/shard_map/ppermute | solution.py:59
  75.9 0.7 multiply_reduce_fusion.2
  76.5 0.0 collective-permute-done.13
  76.6 2.3 %collective-permute-start.14 = (f32[2,64,512]{2,1,0:T(8,128)S(1)}, f32[2,64,512]{2,1,0:T(8,128)S(1)}, u32[]{:S(2)}, u32[]{:S(2)}) collective-permute-start(f32[2,64,512]{2,1,0:T(8,128)S(1)} %collective-permute-done.13), channel_id=1, source_target_pairs={{0,112},{16,0},{32,16},{48,32},{64,48},{80,64},{96,80},{112,96},{1... | collective-permute-start | bytes 786440 | tf_op jit(solution)/shard_map/ppermute | solution.py:62
  78.8 0.7 multiply_reduce_fusion.1
  80.8 2.4 %collective-permute-done.14 = f32[2,64,512]{2,1,0:T(8,128)S(1)} collective-permute-done((f32[2,64,512]{2,1,0:T(8,128)S(1)}, f32[2,64,512]{2,1,0:T(8,128)S(1)}, u32[]{:S(2)}, u32[]{:S(2)}) %collective-permute-start.14) | collective-permute-done | bytes 262176 | tf_op jit(solution)/shard_map/ppermute | solution.py:62
  83.2 0.7 multiply_reduce_fusion
  84.5 0.6 broadcast_in_dim.30
  85.1 15.0 %all-to-all-start = ((f32[16,1,1]{2,1,0:T(1,128)}), f32[16,1,1]{2,1,0:T(1,128)S(1)}, u32[]{:S(2)}, u32[]{:S(2)}) async-start(f32[16,1,1]{2,1,0:T(1,128)} %broadcast_in_dim.30), calls=%async_computation | async-start | bytes 16384 | tf_op jit(solution)/shard_map/all_to_all | solution.py:66
  100.2 5.4 %all-to-all-done = f32[16,1,1]{2,1,0:T(1,128)S(1)} async-done(((f32[16,1,1]{2,1,0:T(1,128)}), f32[16,1,1]{2,1,0:T(1,128)S(1)}, u32[]{:S(2)}, u32[]{:S(2)}) %all-to-all-start) | async-done | bytes 96 | tf_op jit(solution)/shard_map/all_to_all | solution.py:66
  105.6 0.6 reduce_sum.89
  106.9 0.0 copy-start
  106.9 0.0 copy-start.1
  106.9 0.2 broadcast_multiply_fusion
  107.2 1.3 %copy-done = f32[2,512,512]{2,1,0:T(8,128)S(1)} copy-done((f32[2,512,512]{2,1,0:T(8,128)S(1)}, f32[2,512,512]{2,1,0:T(8,128)}, u32[]{:S(2)}) %copy-start) | copy-done | bytes 2097176
  108.5 0.6 copy-done.1
  109.1 2.8 %fusion.1 = (f32[2,512,512]{2,1,0:T(8,128)}, f32[2,512,512]{2,1,0:T(8,128)}) fusion(f32[2,512,512]{2,1,0:T(8,128)S(1)} %copy-done, f32[2,8,64,512]{3,2,1,0:T(8,128)S(1)} %broadcast_multiply_fusion, f32[2,512,512]{2,1,0:T(8,128)S(1)} %copy-done.1), kind=kLoop, calls=%fused_computation.3 | loop fusion | flops 3145728 | bytes 10485760 | tf_op jit(solution)/shard_map/sub | solution.py:16
  (8 shorter events, 0.2 us)
Async XLA Ops:
  1.8 11.5 %collective-permute-start.3 = (f32[2,64,512]{2,1,0:T(8,128)S(1)}, f32[2,64,512]{2,1,0:T(8,128)S(1)}, u32[]{:S(2)}, u32[]{:S(2)}) collective-permute-start(f32[2,64,512]{2,1,0:T(8,128)S(1)} %get-tuple-element.11), channel_id=1, source_target_pairs={{0,112},{16,0},{32,16},{48,32},{64,48},{80,64},{96,80},{112,96},{1... | collective-permute-start | bytes 786440 | tf_op jit(solution)/shard_map/ppermute | solution.py:47
  8.2 9.5 %collective-permute-start = (f32[2,64,512]{2,1,0:T(8,128)S(1)}, f32[2,64,512]{2,1,0:T(8,128)S(1)}, u32[]{:S(2)}, u32[]{:S(2)}) collective-permute-start(f32[2,64,512]{2,1,0:T(8,128)S(1)} %get-tuple-element.10), channel_id=1, source_target_pairs={{0,16},{16,32},{32,48},{48,64},{64,80},{80,96},{96,112},{112,0},{1... | collective-permute-start | bytes 786440 | tf_op jit(solution)/shard_map/ppermute | solution.py:45
  14.2 7.6 %collective-permute-start.4 = (f32[2,64,512]{2,1,0:T(8,128)S(1)}, f32[2,64,512]{2,1,0:T(8,128)S(1)}, u32[]{:S(2)}, u32[]{:S(2)}) collective-permute-start(f32[2,64,512]{2,1,0:T(8,128)S(1)} %bitcast_add_fusion.4), channel_id=1, source_target_pairs={{0,112},{16,0},{32,16},{48,32},{64,48},{80,64},{96,80},{112,96},{1... | collective-permute-start | bytes 786440 | tf_op jit(solution)/shard_map/ppermute | solution.py:47
  22.9 7.8 %collective-permute-start.1 = (f32[2,64,512]{2,1,0:T(8,128)S(1)}, f32[2,64,512]{2,1,0:T(8,128)S(1)}, u32[]{:S(2)}, u32[]{:S(2)}) collective-permute-start(f32[2,64,512]{2,1,0:T(8,128)S(1)} %get-tuple-element.8), channel_id=1, source_target_pairs={{0,16},{16,32},{32,48},{48,64},{64,80},{80,96},{96,112},{112,0},{1... | collective-permute-start | bytes 786440 | tf_op jit(solution)/shard_map/ppermute | solution.py:45
  23.0 7.7 %collective-permute-start.5 = (f32[2,64,512]{2,1,0:T(8,128)S(1)}, f32[2,64,512]{2,1,0:T(8,128)S(1)}, u32[]{:S(2)}, u32[]{:S(2)}) collective-permute-start(f32[2,64,512]{2,1,0:T(8,128)S(1)} %get-tuple-element.9), channel_id=1, source_target_pairs={{0,112},{16,0},{32,16},{48,32},{64,48},{80,64},{96,80},{112,96},{1... | collective-permute-start | bytes 786440 | tf_op jit(solution)/shard_map/ppermute | solution.py:47
  31.8 5.6 %collective-permute-start.6 = (f32[2,64,512]{2,1,0:T(8,128)S(1)}, f32[2,64,512]{2,1,0:T(8,128)S(1)}, u32[]{:S(2)}, u32[]{:S(2)}) collective-permute-start(f32[2,64,512]{2,1,0:T(8,128)S(1)} %get-tuple-element.7), channel_id=1, source_target_pairs={{0,112},{16,0},{32,16},{48,32},{64,48},{80,64},{96,80},{112,96},{1... | collective-permute-start | bytes 786440 | tf_op jit(solution)/shard_map/ppermute | solution.py:47
  34.1 6.4 %collective-permute-start.2 = (f32[2,64,512]{2,1,0:T(8,128)S(1)}, f32[2,64,512]{2,1,0:T(8,128)S(1)}, u32[]{:S(2)}, u32[]{:S(2)}) collective-permute-start(f32[2,64,512]{2,1,0:T(8,128)S(1)} %get-tuple-element.6), channel_id=1, source_target_pairs={{0,16},{16,32},{32,48},{48,64},{64,80},{80,96},{96,112},{112,0},{1... | collective-permute-start | bytes 786440 | tf_op jit(solution)/shard_map/ppermute | solution.py:45
  41.6 6.8 %collective-permute-start.7 = (f32[2,64,512]{2,1,0:T(8,128)S(1)}, f32[2,64,512]{2,1,0:T(8,128)S(1)}, u32[]{:S(2)}, u32[]{:S(2)}) collective-permute-start(f32[2,64,512]{2,1,0:T(8,128)S(1)} %fusion.2), channel_id=1, source_target_pairs={{0,128},{16,144},{32,160},{48,176},{64,192},{80,208},{96,224},{112... | collective-permute-start | bytes 786440 | tf_op jit(solution)/shard_map/ppermute | solution.py:51
  49.1 6.4 %collective-permute-start.8 = (f32[2,64,512]{2,1,0:T(8,128)S(1)}, f32[2,64,512]{2,1,0:T(8,128)S(1)}, u32[]{:S(2)}, u32[]{:S(2)}) collective-permute-start(f32[2,64,512]{2,1,0:T(8,128)S(1)} %get-tuple-element.5), channel_id=1, source_target_pairs={{0,16},{16,32},{32,48},{48,64},{64,80},{80,96},{96,112},{112,0},{1... | collective-permute-start | bytes 786440 | tf_op jit(solution)/shard_map/ppermute | solution.py:59
  49.1 8.4 %collective-permute-start.9 = (f32[2,64,512]{2,1,0:T(8,128)S(1)}, f32[2,64,512]{2,1,0:T(8,128)S(1)}, u32[]{:S(2)}, u32[]{:S(2)}) collective-permute-start(f32[2,64,512]{2,1,0:T(8,128)S(1)} %get-tuple-element.5), channel_id=1, source_target_pairs={{0,112},{16,0},{32,16},{48,32},{64,48},{80,64},{96,80},{112,96},{1... | collective-permute-start | bytes 786440 | tf_op jit(solution)/shard_map/ppermute | solution.py:62
  58.8 6.5 %collective-permute-start.10 = (f32[2,64,512]{2,1,0:T(8,128)S(1)}, f32[2,64,512]{2,1,0:T(8,128)S(1)}, u32[]{:S(2)}, u32[]{:S(2)}) collective-permute-start(f32[2,64,512]{2,1,0:T(8,128)S(1)} %collective-permute-done.8), channel_id=1, source_target_pairs={{0,16},{16,32},{32,48},{48,64},{64,80},{80,96},{96,112},{112,0},{1... | collective-permute-start | bytes 786440 | tf_op jit(solution)/shard_map/ppermute | solution.py:59
  58.9 7.7 %collective-permute-start.11 = (f32[2,64,512]{2,1,0:T(8,128)S(1)}, f32[2,64,512]{2,1,0:T(8,128)S(1)}, u32[]{:S(2)}, u32[]{:S(2)}) collective-permute-start(f32[2,64,512]{2,1,0:T(8,128)S(1)} %collective-permute-done.9), channel_id=1, source_target_pairs={{0,112},{16,0},{32,16},{48,32},{64,48},{80,64},{96,80},{112,96},{1... | collective-permute-start | bytes 786440 | tf_op jit(solution)/shard_map/ppermute | solution.py:62
  68.0 7.9 %collective-permute-start.12 = (f32[2,64,512]{2,1,0:T(8,128)S(1)}, f32[2,64,512]{2,1,0:T(8,128)S(1)}, u32[]{:S(2)}, u32[]{:S(2)}) collective-permute-start(f32[2,64,512]{2,1,0:T(8,128)S(1)} %collective-permute-done.10), channel_id=1, source_target_pairs={{0,16},{16,32},{32,48},{48,64},{64,80},{80,96},{96,112},{112,0},{1... | collective-permute-start | bytes 786440 | tf_op jit(solution)/shard_map/ppermute | solution.py:59
  68.1 8.5 %collective-permute-start.13 = (f32[2,64,512]{2,1,0:T(8,128)S(1)}, f32[2,64,512]{2,1,0:T(8,128)S(1)}, u32[]{:S(2)}, u32[]{:S(2)}) collective-permute-start(f32[2,64,512]{2,1,0:T(8,128)S(1)} %collective-permute-done.11), channel_id=1, source_target_pairs={{0,112},{16,0},{32,16},{48,32},{64,48},{80,64},{96,80},{112,96},{1... | collective-permute-start | bytes 786440 | tf_op jit(solution)/shard_map/ppermute | solution.py:62
  76.6 6.7 %collective-permute-start.14 = (f32[2,64,512]{2,1,0:T(8,128)S(1)}, f32[2,64,512]{2,1,0:T(8,128)S(1)}, u32[]{:S(2)}, u32[]{:S(2)}) collective-permute-start(f32[2,64,512]{2,1,0:T(8,128)S(1)} %collective-permute-done.13), channel_id=1, source_target_pairs={{0,112},{16,0},{32,16},{48,32},{64,48},{80,64},{96,80},{112,96},{1... | collective-permute-start | bytes 786440 | tf_op jit(solution)/shard_map/ppermute | solution.py:62
  85.1 20.5 %all-to-all-start = ((f32[16,1,1]{2,1,0:T(1,128)}), f32[16,1,1]{2,1,0:T(1,128)S(1)}, u32[]{:S(2)}, u32[]{:S(2)}) async-start(f32[16,1,1]{2,1,0:T(1,128)} %broadcast_in_dim.30), calls=%async_computation | async-start | bytes 16384 | tf_op jit(solution)/shard_map/all_to_all | solution.py:66
  106.9 1.6 %copy-start = (f32[2,512,512]{2,1,0:T(8,128)S(1)}, f32[2,512,512]{2,1,0:T(8,128)}, u32[]{:S(2)}) copy-start(f32[2,512,512]{2,1,0:T(8,128)} %param.4) | copy-start | bytes 6291460
  106.9 2.2 %copy-start.1 = (f32[2,512,512]{2,1,0:T(8,128)S(1)}, f32[2,512,512]{2,1,0:T(8,128)}, u32[]{:S(2)}) copy-start(f32[2,512,512]{2,1,0:T(8,128)} %param.5) | copy-start | bytes 6291460

commit v7 on v0

--- a/solution.py
+++ b/solution.py
@@ -1,11 +1,23 @@
+import functools
+
 import jax
 import jax.numpy as jnp
 from jax import lax
+from jax.experimental import pallas as pl
+from jax.experimental.pallas import tpu as pltpu
 from jax.sharding import PartitionSpec as P
 
 D = 8192
 HEAD = 128
 KVH = 4
+RING = 8
+MESH = pl.DeviceIdType.MESH
+REACH_R, REACH_L = (RING - 1) // 2, RING // 2
+RS_R, RS_L = 0, REACH_R
+Y = REACH_R + REACH_L
+AG_R = Y + 1
+AG_L = AG_R + REACH_R
+COPIES = AG_L + REACH_L
 
 
 def outer_update(average, params, momentum, mean_square):
@@ -16,13 +28,91 @@
     return (new_params, new_momentum)
 
 
+def ring_kernel(islands, x_ref, out_ref, sbuf, rbuf, ssem, rsem):
+    chunk = x_ref.shape[1] // RING
+    me = lax.axis_index("island")
+    col = lax.axis_index("inner")
+    z = me % RING
+    base = me - z
+    right = base + (z + 1) % RING
+    left = base + (z + RING - 1) % RING
+    partner = (me + RING) % islands
+
+    def rows(k):
+        return pl.ds(pl.multiple_of(((z + k) % RING) * chunk, chunk), chunk)
+
+    def send(k, src, dst, target):
+        cp = pltpu.make_async_remote_copy(
+            src_ref=src, dst_ref=dst, send_sem=ssem.at[k], recv_sem=rsem.at[k],
+            device_id={"island": target}, device_id_type=MESH)
+        cp.start()
+        return cp
+
+    barrier = pltpu.get_barrier_semaphore()
+    for target in (left, right, partner):
+        pl.semaphore_signal(barrier, inc=1, device_id={"island": target}, device_id_type=MESH)
+    pl.semaphore_wait(barrier, 3)
+
+    cr = send(RS_R, x_ref.at[:, rows(REACH_R)], rbuf.at[RS_R], right)
+    cl = send(RS_L, x_ref.at[:, rows(RING - REACH_L)], rbuf.at[RS_L], left)
+    for s in range(REACH_L):
+        if s < REACH_R:
+            cr.wait()
+            if s < REACH_R - 1:
+                k = RS_R + s
+                sbuf[k + 1] = rbuf[k] + x_ref[:, rows(REACH_R - 1 - s)]
+                cr = send(k + 1, sbuf.at[k + 1], rbuf.at[k + 1], right)
+        cl.wait()
+        if s < REACH_L - 1:
+            k = RS_L + s
+            sbuf[k + 1] = rbuf[k] + x_ref[:, rows(RING - REACH_L + 1 + s)]
+            cl = send(k + 1, sbuf.at[k + 1], rbuf.at[k + 1], left)
+
+    sbuf[Y] = x_ref[:, rows(0)] + rbuf[RS_R + REACH_R - 1] + rbuf[RS_L + REACH_L - 1]
+    cy = send(Y, sbuf.at[Y], rbuf.at[Y], partner)
+    cy.wait()
+    out_ref[:, rows(0)] = (sbuf[Y] + rbuf[Y]) / islands
+
+    cr = cl = None
+    for s in range(REACH_L):
+        if s < REACH_R:
+            if cr is not None:
+                cr.wait()
+            cr = send(AG_R + s, out_ref.at[:, rows(RING - s)], out_ref.at[:, rows(RING - s)], right)
+        if cl is not None:
+            cl.wait()
+        cl = send(AG_L + s, out_ref.at[:, rows(s)], out_ref.at[:, rows(s)], left)
+    cr.wait()
+    cl.wait()
+
+
+def all_reduce(own, islands):
+    halves, rows, cols = own.shape
+    chunk = rows // RING
+    return pl.pallas_call(
+        functools.partial(ring_kernel, islands),
+        out_shape=jax.ShapeDtypeStruct(own.shape, own.dtype),
+        in_specs=[pl.BlockSpec(memory_space=pltpu.VMEM)],
+        out_specs=pl.BlockSpec(memory_space=pltpu.VMEM),
+        scratch_shapes=[
+            pltpu.VMEM((COPIES, halves, chunk, cols), own.dtype),
+            pltpu.VMEM((COPIES, halves, chunk, cols), own.dtype),
+            pltpu.SemaphoreType.DMA((COPIES,)),
+            pltpu.SemaphoreType.DMA((COPIES,)),
+        ],
+        compiler_params=pltpu.CompilerParams(
+            collective_id=0, has_side_effects=True, vmem_limit_bytes=48 * 1024 * 1024),
+    )(own)
+
+
 def body(island_delta, params, momentum):
-    replicas = lax.axis_size("island")
+    islands = lax.axis_size("island")
+    inner = lax.axis_size("inner")
     count = 2 * D * KVH * HEAD
-    own_delta = island_delta[0]
-    average = lax.psum(own_delta, "island") / replicas
-    total_sq = lax.psum(jnp.sum(average * average), "inner")
-    return outer_update(average, params, momentum, total_sq / count)
+    average = all_reduce(island_delta[0], islands)
+    sq = jnp.sum(average * average)
+    sq = jnp.sum(lax.all_to_all(jnp.full((inner, 1), sq), "inner", 0, 0, tiled=True))
+    return outer_update(average, params, momentum, sq / count)
 
 
 def solution(mesh):

time: 221 us -> 90.2 us (0.41)
  waiting for transfers between devices: 168 us -> 0 us
  Pallas kernels: 0 us -> 68.1 us
  blocking collectives: 27.8 us -> 10.4 us
  between operations: 14.7 us -> 1.35 us
  local copies, waits for them, and re-layouts: 0.01 us -> 2.23 us
    psum x1 -> x0, waiting for transfers between devices: 168 us -> none  [body(): average = lax.psum(own_delta, 'island') / replicas]
    pallas_call x0 -> x1, Pallas kernels: none -> 68.1 us  [all_reduce(): pl.pallas_call(functools.partial(ring_kernel, islands), out_shape=jax.Sha...]
    psum x1 -> x0, blocking collectives: 27.8 us -> none  [body(): total_sq = lax.psum(jnp.sum(average * average), 'inner')]
    all_to_all x0 -> x1, blocking collectives: none -> 10.4 us  [body(): lax.all_to_all(jnp.full((inner, 1), sq), 'inner', 0, 0, tiled=True)]
  transfers between devices with their start and end apart: 1 -> 0, of which waited for: 1 -> 0; matrix products, arithmetic and copies ran while one was open for 0% -> 0% of each run, Pallas kernels for 0% -> 0%
where the time goes in v7:
time: 90.2 us; the launch traced here: 88.8 us
  Pallas kernels  68.1 us (75%)
  blocking collectives  10.4 us (12%)
  other arithmetic  6.78 us (8%)
  local copies, waits for them, and re-layouts  2.23 us (2%)
  between operations  1.35 us (1%)
    pallas_call x1, Pallas kernels, all_reduce(): pl.pallas_call(functools.partial(ring_kernel, islands), out_shape=jax.Sha...  68.1 us
    all_to_all x1, blocking collectives, body(): lax.all_to_all(jnp.full((inner, 1), sq), 'inner', 0, 0, tiled=True)  10.4 us
    sub x1, other arithmetic, outer_update(): new_params = params - 0.7 * (clipped + 0.9 * new_momentum)  5.03 us

profile of v7, /device:TPU:32, one launch (start us, length us, event | category | flops | bytes accessed | tf_op | source)
XLA Modules:
  0.0 88.8 jit_solution(5795270008154169097)
XLA Ops:
  0.6 0.0 copy-start
  0.6 1.6 %copy-done = f32[1,2,512,512]{3,2,1,0:T(8,128)S(1)} copy-done((f32[1,2,512,512]{3,2,1,0:T(8,128)S(1)}, f32[1,2,512,512]{3,2,1,0:T(8,128)}, u32[]{:S(2)}) %copy-start) | copy-done | bytes 2097176
  2.2 68.1 %shard_map.50 = f32[2,512,512]{2,1,0:T(8,128)S(1)} custom-call(f32[2,512,512]{2,1,0:T(8,128)S(1)} %bitcast.1), custom_call_target="tpu_custom_call" | custom-call | tf_op jit(solution)/shard_map/pallas_call | solution.py:92
  70.3 1.1 %multiply_reduce_fusion = f32[]{:T(128)} fusion(f32[2,512,512]{2,1,0:T(8,128)S(1)} %shard_map.50), kind=kLoop, calls=%fused_computation.2 | loop fusion | flops 1048575 | bytes 2097156 | tf_op jit(solution)/shard_map/reduce_sum | solution.py:113
  71.5 0.6 broadcast_in_dim.3
  72.1 10.4 %all_to_all.6 = f32[16,1,1]{2,1,0:T(1,128)S(1)} all-to-all(f32[16,1,1]{2,1,0:T(1,128)S(1)} %broadcast_in_dim.3), channel_id=1, replica_groups=mesh['island'=16,'inner'=16] {'inner'}, dimensions={0} | all-to-all | bytes 128 | tf_op jit(solution)/shard_map/all_to_all | solution.py:114
  82.5 0.6 reduce_sum.19
  83.8 5.0 %multiply_subtract_fusion = (f32[2,512,512]{2,1,0:T(8,128)}, f32[2,512,512]{2,1,0:T(8,128)}) fusion(f32[2,512,512]{2,1,0:T(8,128)} %param.4, f32[2,512,512]{2,1,0:T(8,128)S(1)} %shard_map.50, f32[]{:T(128)S(6)} %min_shard_map.3, f32[2,512,512]{2,1,0:T(8,128)} %param.5), kind=kLoop, calls=%fused_computation | loop fusion | flops 3670016 | bytes 10485764 | tf_op jit(solution)/shard_map/sub | solution.py:27
Async XLA Ops:
  0.6 1.6 %copy-start = (f32[1,2,512,512]{3,2,1,0:T(8,128)S(1)}, f32[1,2,512,512]{3,2,1,0:T(8,128)}, u32[]{:S(2)}) copy-start(f32[1,2,512,512]{3,2,1,0:T(8,128)} %param.3) | copy-start | bytes 6291460

commit v8 on v7

--- a/solution.py
+++ b/solution.py
@@ -28,7 +28,7 @@
     return (new_params, new_momentum)
 
 
-def ring_kernel(islands, x_ref, out_ref, sbuf, rbuf, ssem, rsem):
+def ring_kernel(islands, inner, x_ref, out_ref, sq_ref, sbuf, rbuf, ssem, rsem, sq_in, sq_ssem, sq_rsem):
     chunk = x_ref.shape[1] // RING
     me = lax.axis_index("island")
     col = lax.axis_index("inner")
@@ -51,7 +51,9 @@
     barrier = pltpu.get_barrier_semaphore()
     for target in (left, right, partner):
         pl.semaphore_signal(barrier, inc=1, device_id={"island": target}, device_id_type=MESH)
-    pl.semaphore_wait(barrier, 3)
+    for o in range(1, inner):
+        pl.semaphore_signal(barrier, inc=1, device_id={"inner": (col + o) % inner}, device_id_type=MESH)
+    pl.semaphore_wait(barrier, 3 + inner - 1)
 
     cr = send(RS_R, x_ref.at[:, rows(REACH_R)], rbuf.at[RS_R], right)
     cl = send(RS_L, x_ref.at[:, rows(RING - REACH_L)], rbuf.at[RS_L], left)
@@ -85,20 +87,44 @@
     cr.wait()
     cl.wait()
 
+    block = out_ref[...]
+    sq_in[col] = jnp.full(sq_in.shape[1:], jnp.sum(block * block), jnp.float32)
+    sends = []
+    for o in range(1, inner):
+        cp = pltpu.make_async_remote_copy(
+            src_ref=sq_in.at[col], dst_ref=sq_in.at[col], send_sem=sq_ssem.at[o], recv_sem=sq_rsem.at[col],
+            device_id={"inner": (col + o) % inner}, device_id_type=MESH)
+        cp.start()
+        sends.append(cp)
+    for o in range(1, inner):
+        src = (col + inner - o) % inner
+        pltpu.make_async_remote_copy(
+            src_ref=sq_in.at[src], dst_ref=sq_in.at[src], send_sem=sq_ssem.at[o], recv_sem=sq_rsem.at[src],
+            device_id={"inner": src}, device_id_type=MESH).wait_recv()
+    for cp in sends:
+        cp.wait_send()
+    total = sq_in[0]
+    for j in range(1, inner):
+        total = total + sq_in[j]
+    sq_ref[...] = total
 
-def all_reduce(own, islands):
+
+def all_reduce(own, islands, inner):
     halves, rows, cols = own.shape
     chunk = rows // RING
     return pl.pallas_call(
-        functools.partial(ring_kernel, islands),
-        out_shape=jax.ShapeDtypeStruct(own.shape, own.dtype),
+        functools.partial(ring_kernel, islands, inner),
+        out_shape=(jax.ShapeDtypeStruct(own.shape, own.dtype), jax.ShapeDtypeStruct((8, 128), jnp.float32)),
         in_specs=[pl.BlockSpec(memory_space=pltpu.VMEM)],
-        out_specs=pl.BlockSpec(memory_space=pltpu.VMEM),
+        out_specs=(pl.BlockSpec(memory_space=pltpu.VMEM), pl.BlockSpec(memory_space=pltpu.VMEM)),
         scratch_shapes=[
             pltpu.VMEM((COPIES, halves, chunk, cols), own.dtype),
             pltpu.VMEM((COPIES, halves, chunk, cols), own.dtype),
             pltpu.SemaphoreType.DMA((COPIES,)),
             pltpu.SemaphoreType.DMA((COPIES,)),
+            pltpu.VMEM((inner, 8, 128), jnp.float32),
+            pltpu.SemaphoreType.DMA((inner,)),
+            pltpu.SemaphoreType.DMA((inner,)),
         ],
         compiler_params=pltpu.CompilerParams(
             collective_id=0, has_side_effects=True, vmem_limit_bytes=48 * 1024 * 1024),
@@ -109,10 +135,8 @@
     islands = lax.axis_size("island")
     inner = lax.axis_size("inner")
     count = 2 * D * KVH * HEAD
-    average = all_reduce(island_delta[0], islands)
-    sq = jnp.sum(average * average)
-    sq = jnp.sum(lax.all_to_all(jnp.full((inner, 1), sq), "inner", 0, 0, tiled=True))
-    return outer_update(average, params, momentum, sq / count)
+    average, sq = all_reduce(island_delta[0], islands, inner)
+    return outer_update(average, params, momentum, sq[0, 0] / count)
 
 
 def solution(mesh):

time: 90.2 us -> 84.9 us (0.941)
  blocking collectives: 10.4 us -> 0 us
  Pallas kernels: 68.1 us -> 76.2 us
  other arithmetic: 6.78 us -> 4.4 us
    all_to_all x1 -> x0, blocking collectives: 10.4 us -> none  [body(): lax.all_to_all(jnp.full((inner, 1), sq), 'inner', 0, 0, tiled=True)]
    pallas_call x1, Pallas kernels: 68.1 us -> 76.2 us  [all_reduce(): pl.pallas_call(functools.partial(ring_kernel, islands, inner), out_shape=...]
    reduce_sum x2 -> x0, other arithmetic: 1.76 us -> none  [the longest x1 1.14 us: body(): sq = jnp.sum(average * average)]
where the time goes in v8:
time: 84.9 us; the launch traced here: 84 us
  Pallas kernels  76.2 us (90%)
  other arithmetic  4.4 us (5%)
  local copies, waits for them, and re-layouts  2.1 us (2%)
  between operations  1.35 us (2%)
    pallas_call x1, Pallas kernels, all_reduce(): pl.pallas_call(functools.partial(ring_kernel, islands, inner), out_shape=...  76.2 us
    sub x1, other arithmetic, outer_update(): new_params = params - 0.7 * (clipped + 0.9 * new_momentum)  4.4 us

profile of v8, /device:TPU:32, one launch (start us, length us, event | category | flops | bytes accessed | tf_op | source)
XLA Modules:
  0.0 84.0 jit_solution(17520110723087051569)
XLA Ops:
  0.6 0.0 copy-start
  0.6 1.6 %copy-done = f32[1,2,512,512]{3,2,1,0:T(8,128)S(1)} copy-done((f32[1,2,512,512]{3,2,1,0:T(8,128)S(1)}, f32[1,2,512,512]{3,2,1,0:T(8,128)}, u32[]{:S(2)}) %copy-start) | copy-done | bytes 2097176
  2.2 0.0 copy-start.1
  2.2 76.2 %shard_map.50 = (f32[2,512,512]{2,1,0:T(8,128)S(1)}, f32[8,128]{1,0:T(8,128)S(1)}) custom-call(f32[2,512,512]{2,1,0:T(8,128)S(1)} %bitcast.2), custom_call_target="tpu_custom_call" | custom-call | tf_op jit(solution)/shard_map/pallas_call | solution.py:115
  78.4 0.5 slice.3
  79.6 0.0 copy-done.1
  79.6 4.4 %multiply_subtract_fusion = (f32[2,512,512]{2,1,0:T(8,128)}, f32[2,512,512]{2,1,0:T(8,128)}) fusion(f32[2,512,512]{2,1,0:T(8,128)S(1)} %copy-done.1, f32[2,512,512]{2,1,0:T(8,128)S(1)} %get-tuple-element.5, f32[]{:T(128)} %bitcast.1, f32[2,512,512]{2,1,0:T(8,128)} %param.5), kind=kLoop, calls=%fused_computation | loop fusion | flops 3670016 | bytes 10485764 | tf_op jit(solution)/shard_map/sub | solution.py:27
Async XLA Ops:
  0.6 1.6 %copy-start = (f32[1,2,512,512]{3,2,1,0:T(8,128)S(1)}, f32[1,2,512,512]{3,2,1,0:T(8,128)}, u32[]{:S(2)}) copy-start(f32[1,2,512,512]{3,2,1,0:T(8,128)} %param.3) | copy-start | bytes 6291460
  2.2 77.4 %copy-start.1 = (f32[2,512,512]{2,1,0:T(8,128)S(1)}, f32[2,512,512]{2,1,0:T(8,128)}, u32[]{:S(2)}) copy-start(f32[2,512,512]{2,1,0:T(8,128)} %param.4) | copy-start | bytes 6291460

commit v9 on v8

--- a/solution.py
+++ b/solution.py
@@ -28,7 +28,7 @@
     return (new_params, new_momentum)
 
 
-def ring_kernel(islands, inner, x_ref, out_ref, sq_ref, sbuf, rbuf, ssem, rsem, sq_in, sq_ssem, sq_rsem):
+def ring_kernel(islands, inner, x_ref, out_ref, sq_ref, sbuf, rbuf, ssem, rsem, sq_in, sq_ssem, sq_rsem, sq_chunk):
     chunk = x_ref.shape[1] // RING
     me = lax.axis_index("island")
     col = lax.axis_index("inner")
@@ -75,6 +75,10 @@
     cy.wait()
     out_ref[:, rows(0)] = (sbuf[Y] + rbuf[Y]) / islands
 
+    def square(k):
+        part = out_ref[:, rows(k)]
+        sq_chunk[(z + k) % RING] = jnp.full(sq_chunk.shape[1:], jnp.sum(part * part), jnp.float32)
+
     cr = cl = None
     for s in range(REACH_L):
         if s < REACH_R:
@@ -84,11 +88,19 @@
         if cl is not None:
             cl.wait()
         cl = send(AG_L + s, out_ref.at[:, rows(s)], out_ref.at[:, rows(s)], left)
+        if s < REACH_R:
+            square(RING - s)
+        if s > 0:
+            square(s)
     cr.wait()
+    square(RING - REACH_R)
     cl.wait()
+    square(REACH_L)
 
-    block = out_ref[...]
-    sq_in[col] = jnp.full(sq_in.shape[1:], jnp.sum(block * block), jnp.float32)
+    mine = sq_chunk[0]
+    for c in range(1, RING):
+        mine = mine + sq_chunk[c]
+    sq_in[col] = mine
     sends = []
     for o in range(1, inner):
         cp = pltpu.make_async_remote_copy(
@@ -125,6 +137,7 @@
             pltpu.VMEM((inner, 8, 128), jnp.float32),
             pltpu.SemaphoreType.DMA((inner,)),
             pltpu.SemaphoreType.DMA((inner,)),
+            pltpu.VMEM((RING, 8, 128), jnp.float32),
         ],
         compiler_params=pltpu.CompilerParams(
             collective_id=0, has_side_effects=True, vmem_limit_bytes=48 * 1024 * 1024),

time: 84.9 us -> 84.4 us (level)
  no operation moved by 1% of the time
where the time goes in v9:
time: 84.4 us; the launch traced here: 83.5 us
  Pallas kernels  75.7 us (90%)
  other arithmetic  4.4 us (5%)
  local copies, waits for them, and re-layouts  2.1 us (2%)
  between operations  1.35 us (2%)
    pallas_call x1, Pallas kernels, all_reduce(): pl.pallas_call(functools.partial(ring_kernel, islands, inner), out_shape=...  75.7 us
    sub x1, other arithmetic, outer_update(): new_params = params - 0.7 * (clipped + 0.9 * new_momentum)  4.4 us

profile of v9, /device:TPU:32, one launch (start us, length us, event | category | flops | bytes accessed | tf_op | source)
XLA Modules:
  0.0 83.5 jit_solution(18282686907871583021)
XLA Ops:
  0.6 0.0 copy-start
  0.6 1.6 %copy-done = f32[1,2,512,512]{3,2,1,0:T(8,128)S(1)} copy-done((f32[1,2,512,512]{3,2,1,0:T(8,128)S(1)}, f32[1,2,512,512]{3,2,1,0:T(8,128)}, u32[]{:S(2)}) %copy-start) | copy-done | bytes 2097176
  2.2 0.0 copy-start.1
  2.2 75.7 %shard_map.50 = (f32[2,512,512]{2,1,0:T(8,128)S(1)}, f32[8,128]{1,0:T(8,128)S(1)}) custom-call(f32[2,512,512]{2,1,0:T(8,128)S(1)} %bitcast.2), custom_call_target="tpu_custom_call" | custom-call | tf_op jit(solution)/shard_map/pallas_call | solution.py:127
  77.9 0.5 slice.3
  79.1 0.0 copy-done.1
  79.1 4.4 %multiply_subtract_fusion = (f32[2,512,512]{2,1,0:T(8,128)}, f32[2,512,512]{2,1,0:T(8,128)}) fusion(f32[2,512,512]{2,1,0:T(8,128)S(1)} %copy-done.1, f32[2,512,512]{2,1,0:T(8,128)S(1)} %get-tuple-element.5, f32[]{:T(128)} %bitcast.1, f32[2,512,512]{2,1,0:T(8,128)} %param.5), kind=kLoop, calls=%fused_computation | loop fusion | flops 3670016 | bytes 10485764 | tf_op jit(solution)/shard_map/sub | solution.py:27
Async XLA Ops:
  0.6 1.6 %copy-start = (f32[1,2,512,512]{3,2,1,0:T(8,128)S(1)}, f32[1,2,512,512]{3,2,1,0:T(8,128)}, u32[]{:S(2)}) copy-start(f32[1,2,512,512]{3,2,1,0:T(8,128)} %param.3) | copy-start | bytes 6291460
  2.2 76.9 %copy-start.1 = (f32[2,512,512]{2,1,0:T(8,128)S(1)}, f32[2,512,512]{2,1,0:T(8,128)}, u32[]{:S(2)}) copy-start(f32[2,512,512]{2,1,0:T(8,128)} %param.4) | copy-start | bytes 6291460

commit v10 on v8

--- a/solution.py
+++ b/solution.py
@@ -28,7 +28,7 @@
     return (new_params, new_momentum)
 
 
-def ring_kernel(islands, inner, x_ref, out_ref, sq_ref, sbuf, rbuf, ssem, rsem, sq_in, sq_ssem, sq_rsem):
+def ring_kernel(islands, inner, x_ref, out_ref, sq_ref, sbuf, rbuf, ssem, rsem, sq_in, sq_ssem, sq_rsem, sq_z, z_ssem, z_rsem):
     chunk = x_ref.shape[1] // RING
     me = lax.axis_index("island")
     col = lax.axis_index("inner")
@@ -53,7 +53,9 @@
         pl.semaphore_signal(barrier, inc=1, device_id={"island": target}, device_id_type=MESH)
     for o in range(1, inner):
         pl.semaphore_signal(barrier, inc=1, device_id={"inner": (col + o) % inner}, device_id_type=MESH)
-    pl.semaphore_wait(barrier, 3 + inner - 1)
+    for o in range(2, RING - 1):
+        pl.semaphore_signal(barrier, inc=1, device_id={"island": base + (z + o) % RING}, device_id_type=MESH)
+    pl.semaphore_wait(barrier, 3 + inner - 1 + RING - 3)
 
     cr = send(RS_R, x_ref.at[:, rows(REACH_R)], rbuf.at[RS_R], right)
     cl = send(RS_L, x_ref.at[:, rows(RING - REACH_L)], rbuf.at[RS_L], left)
@@ -73,10 +75,42 @@
     sbuf[Y] = x_ref[:, rows(0)] + rbuf[RS_R + REACH_R - 1] + rbuf[RS_L + REACH_L - 1]
     cy = send(Y, sbuf.at[Y], rbuf.at[Y], partner)
     cy.wait()
-    out_ref[:, rows(0)] = (sbuf[Y] + rbuf[Y]) / islands
+    mine = (sbuf[Y] + rbuf[Y]) / islands
+    out_ref[:, rows(0)] = mine
+
+    sq_in[col] = jnp.full(sq_in.shape[1:], jnp.sum(mine * mine), jnp.float32)
+    inner_sends = []
+    for o in range(1, inner):
+        cp = pltpu.make_async_remote_copy(
+            src_ref=sq_in.at[col], dst_ref=sq_in.at[col], send_sem=sq_ssem.at[o], recv_sem=sq_rsem.at[col],
+            device_id={"inner": (col + o) % inner}, device_id_type=MESH)
+        cp.start()
+        inner_sends.append(cp)
+    z_sends = []
+
+    def to_z_peers():
+        for o in range(1, inner):
+            src = (col + inner - o) % inner
+            pltpu.make_async_remote_copy(
+                src_ref=sq_in.at[src], dst_ref=sq_in.at[src], send_sem=sq_ssem.at[o], recv_sem=sq_rsem.at[src],
+                device_id={"inner": src}, device_id_type=MESH).wait_recv()
+        for cp in inner_sends:
+            cp.wait_send()
+        over_inner = sq_in[0]
+        for j in range(1, inner):
+            over_inner = over_inner + sq_in[j]
+        sq_z[z] = over_inner
+        for o in range(1, RING):
+            cp = pltpu.make_async_remote_copy(
+                src_ref=sq_z.at[z], dst_ref=sq_z.at[z], send_sem=z_ssem.at[o], recv_sem=z_rsem.at[z],
+                device_id={"island": base + (z + o) % RING}, device_id_type=MESH)
+            cp.start()
+            z_sends.append(cp)
 
     cr = cl = None
     for s in range(REACH_L):
+        if s == 2:
+            to_z_peers()
         if s < REACH_R:
             if cr is not None:
                 cr.wait()
@@ -87,25 +121,16 @@
     cr.wait()
     cl.wait()
 
-    block = out_ref[...]
-    sq_in[col] = jnp.full(sq_in.shape[1:], jnp.sum(block * block), jnp.float32)
-    sends = []
-    for o in range(1, inner):
-        cp = pltpu.make_async_remote_copy(
-            src_ref=sq_in.at[col], dst_ref=sq_in.at[col], send_sem=sq_ssem.at[o], recv_sem=sq_rsem.at[col],
-            device_id={"inner": (col + o) % inner}, device_id_type=MESH)
-        cp.start()
-        sends.append(cp)
-    for o in range(1, inner):
-        src = (col + inner - o) % inner
+    for o in range(1, RING):
+        src = (z + RING - o) % RING
         pltpu.make_async_remote_copy(
-            src_ref=sq_in.at[src], dst_ref=sq_in.at[src], send_sem=sq_ssem.at[o], recv_sem=sq_rsem.at[src],
-            device_id={"inner": src}, device_id_type=MESH).wait_recv()
-    for cp in sends:
+            src_ref=sq_z.at[src], dst_ref=sq_z.at[src], send_sem=z_ssem.at[o], recv_sem=z_rsem.at[src],
+            device_id={"island": base + src}, device_id_type=MESH).wait_recv()
+    for cp in z_sends:
         cp.wait_send()
-    total = sq_in[0]
-    for j in range(1, inner):
-        total = total + sq_in[j]
+    total = sq_z[0]
+    for c in range(1, RING):
+        total = total + sq_z[c]
     sq_ref[...] = total
 
 
@@ -125,6 +150,9 @@
             pltpu.VMEM((inner, 8, 128), jnp.float32),
             pltpu.SemaphoreType.DMA((inner,)),
             pltpu.SemaphoreType.DMA((inner,)),
+            pltpu.VMEM((RING, 8, 128), jnp.float32),
+            pltpu.SemaphoreType.DMA((RING,)),
+            pltpu.SemaphoreType.DMA((RING,)),
         ],
         compiler_params=pltpu.CompilerParams(
             collective_id=0, has_side_effects=True, vmem_limit_bytes=48 * 1024 * 1024),

time: 84.9 us -> 81.1 us (0.955)
  Pallas kernels: 76.2 us -> 73.1 us
    pallas_call x1, Pallas kernels: 76.2 us -> 73.1 us  [all_reduce(): pl.pallas_call(functools.partial(ring_kernel, islands, inner), out_shape=...]
where the time goes in v10:
time: 81.1 us; the launch traced here: 81 us
  Pallas kernels  73.1 us (90%)
  other arithmetic  4.4 us (5%)
  local copies, waits for them, and re-layouts  2.1 us (3%)
  between operations  1.35 us (2%)
    pallas_call x1, Pallas kernels, all_reduce(): pl.pallas_call(functools.partial(ring_kernel, islands, inner), out_shape=...  73.1 us
    sub x1, other arithmetic, outer_update(): new_params = params - 0.7 * (clipped + 0.9 * new_momentum)  4.4 us

profile of v10, /device:TPU:32, one launch (start us, length us, event | category | flops | bytes accessed | tf_op | source)
XLA Modules:
  0.0 81.0 jit_solution(15803551367801000384)
XLA Ops:
  0.6 0.0 copy-start
  0.6 1.6 %copy-done = f32[1,2,512,512]{3,2,1,0:T(8,128)S(1)} copy-done((f32[1,2,512,512]{3,2,1,0:T(8,128)S(1)}, f32[1,2,512,512]{3,2,1,0:T(8,128)}, u32[]{:S(2)}) %copy-start) | copy-done | bytes 2097176
  2.2 0.0 copy-start.1
  2.2 73.1 %shard_map.50 = (f32[2,512,512]{2,1,0:T(8,128)S(1)}, f32[8,128]{1,0:T(8,128)S(1)}) custom-call(f32[2,512,512]{2,1,0:T(8,128)S(1)} %bitcast.2), custom_call_target="tpu_custom_call" | custom-call | tf_op jit(solution)/shard_map/pallas_call | solution.py:140
  75.4 0.5 slice.3
  76.6 0.0 copy-done.1
  76.6 4.4 %multiply_subtract_fusion = (f32[2,512,512]{2,1,0:T(8,128)}, f32[2,512,512]{2,1,0:T(8,128)}) fusion(f32[2,512,512]{2,1,0:T(8,128)S(1)} %copy-done.1, f32[2,512,512]{2,1,0:T(8,128)S(1)} %get-tuple-element.5, f32[]{:T(128)} %bitcast.1, f32[2,512,512]{2,1,0:T(8,128)} %param.5), kind=kLoop, calls=%fused_computation | loop fusion | flops 3670016 | bytes 10485764 | tf_op jit(solution)/shard_map/sub | solution.py:27
Async XLA Ops:
  0.6 1.6 %copy-start = (f32[1,2,512,512]{3,2,1,0:T(8,128)S(1)}, f32[1,2,512,512]{3,2,1,0:T(8,128)}, u32[]{:S(2)}) copy-start(f32[1,2,512,512]{3,2,1,0:T(8,128)} %param.3) | copy-start | bytes 6291460
  2.2 74.4 %copy-start.1 = (f32[2,512,512]{2,1,0:T(8,128)S(1)}, f32[2,512,512]{2,1,0:T(8,128)}, u32[]{:S(2)}) copy-start(f32[2,512,512]{2,1,0:T(8,128)} %param.4) | copy-start | bytes 6291460

commit v11 on v10

--- a/solution.py
+++ b/solution.py
@@ -12,12 +12,11 @@
 KVH = 4
 RING = 8
 MESH = pl.DeviceIdType.MESH
-REACH_R, REACH_L = (RING - 1) // 2, RING // 2
-RS_R, RS_L = 0, REACH_R
-Y = REACH_R + REACH_L
-AG_R = Y + 1
-AG_L = AG_R + REACH_R
-COPIES = AG_L + REACH_L
+CHAINS = ((1, 0, RING // 2), (-1, 0, (RING - 1) // 2), (1, 1, (RING - 1) // 2), (-1, 1, RING // 2))
+RS_BASE = tuple(sum(c[2] for c in CHAINS[:i]) for i in range(len(CHAINS)))
+Y = sum(c[2] for c in CHAINS)
+AG_BASE = tuple(Y + 1 + base for base in RS_BASE)
+COPIES = 2 * Y + 1
 
 
 def outer_update(average, params, momentum, mean_square):
@@ -38,8 +37,13 @@
     left = base + (z + RING - 1) % RING
     partner = (me + RING) % islands
 
-    def rows(k):
-        return pl.ds(pl.multiple_of(((z + k) % RING) * chunk, chunk), chunk)
+    half = chunk // 2
+
+    def rows(k, h=None):
+        start = ((z + k + 2 * RING) % RING) * chunk
+        if h is None:
+            return pl.ds(pl.multiple_of(start, chunk), chunk)
+        return pl.ds(pl.multiple_of(start + h * half, half), half)
 
     def send(k, src, dst, target):
         cp = pltpu.make_async_remote_copy(
@@ -57,22 +61,27 @@
         pl.semaphore_signal(barrier, inc=1, device_id={"island": base + (z + o) % RING}, device_id_type=MESH)
     pl.semaphore_wait(barrier, 3 + inner - 1 + RING - 3)
 
-    cr = send(RS_R, x_ref.at[:, rows(REACH_R)], rbuf.at[RS_R], right)
-    cl = send(RS_L, x_ref.at[:, rows(RING - REACH_L)], rbuf.at[RS_L], left)
-    for s in range(REACH_L):
-        if s < REACH_R:
-            cr.wait()
-            if s < REACH_R - 1:
-                k = RS_R + s
-                sbuf[k + 1] = rbuf[k] + x_ref[:, rows(REACH_R - 1 - s)]
-                cr = send(k + 1, sbuf.at[k + 1], rbuf.at[k + 1], right)
-        cl.wait()
-        if s < REACH_L - 1:
-            k = RS_L + s
-            sbuf[k + 1] = rbuf[k] + x_ref[:, rows(RING - REACH_L + 1 + s)]
-            cl = send(k + 1, sbuf.at[k + 1], rbuf.at[k + 1], left)
-
-    sbuf[Y] = x_ref[:, rows(0)] + rbuf[RS_R + REACH_R - 1] + rbuf[RS_L + REACH_L - 1]
+    pending = [None] * len(CHAINS)
+    for s in range(RING // 2):
+        for i, (d, h, r) in enumerate(CHAINS):
+            if s >= r:
+                continue
+            k = RS_BASE[i] + s
+            target = right if d > 0 else left
+            if s == 0:
+                pending[i] = send(k, x_ref.at[:, rows(d * r, h)], rbuf.at[k, :, pl.ds(0, half)], target)
+                continue
+            pending[i].wait()
+            sbuf[k, :, pl.ds(0, half)] = rbuf[k - 1, :, pl.ds(0, half)] + x_ref[:, rows(d * (r - s), h)]
+            pending[i] = send(k, sbuf.at[k, :, pl.ds(0, half)], rbuf.at[k, :, pl.ds(0, half)], target)
+    for cp in pending:
+        cp.wait()
+    for h in range(2):
+        own = x_ref[:, rows(0, h)]
+        for i, (d, hh, r) in enumerate(CHAINS):
+            if hh == h:
+                own = own + rbuf[RS_BASE[i] + r - 1, :, pl.ds(0, half)]
+        sbuf[Y, :, pl.ds(h * half, half)] = own
     cy = send(Y, sbuf.at[Y], rbuf.at[Y], partner)
     cy.wait()
     mine = (sbuf[Y] + rbuf[Y]) / islands
@@ -107,19 +116,19 @@
             cp.start()
             z_sends.append(cp)
 
-    cr = cl = None
-    for s in range(REACH_L):
+    for s in range(RING // 2):
         if s == 2:
             to_z_peers()
-        if s < REACH_R:
-            if cr is not None:
-                cr.wait()
-            cr = send(AG_R + s, out_ref.at[:, rows(RING - s)], out_ref.at[:, rows(RING - s)], right)
-        if cl is not None:
-            cl.wait()
-        cl = send(AG_L + s, out_ref.at[:, rows(s)], out_ref.at[:, rows(s)], left)
-    cr.wait()
-    cl.wait()
+        for i, (d, h, r) in enumerate(CHAINS):
+            if s >= r:
+                continue
+            if s > 0:
+                pending[i].wait()
+            k = AG_BASE[i] + s
+            place = out_ref.at[:, rows(-d * s, h)]
+            pending[i] = send(k, place, place, right if d > 0 else left)
+    for cp in pending:
+        cp.wait()
 
     for o in range(1, RING):
         src = (z + RING - o) % RING

time: 81.1 us -> 72.4 us (0.89)
  Pallas kernels: 73.1 us -> 64.4 us
    pallas_call x1, Pallas kernels: 73.1 us -> 64.4 us  [all_reduce(): pl.pallas_call(functools.partial(ring_kernel, islands, inner), out_shape=...]
where the time goes in v11:
time: 72.4 us; the launch traced here: 72.3 us
  Pallas kernels  64.4 us (89%)
  other arithmetic  4.4 us (6%)
  local copies, waits for them, and re-layouts  2.1 us (3%)
  between operations  1.35 us (2%)
    pallas_call x1, Pallas kernels, all_reduce(): pl.pallas_call(functools.partial(ring_kernel, islands, inner), out_shape=...  64.4 us
    sub x1, other arithmetic, outer_update(): new_params = params - 0.7 * (clipped + 0.9 * new_momentum)  4.4 us
    unnamed x4, local copies, waits for them, and re-layouts  1.59 us

profile of v11, /device:TPU:32, one launch (start us, length us, event | category | flops | bytes accessed | tf_op | source)
XLA Modules:
  0.0 72.3 jit_solution(14297608838957623782)
XLA Ops:
  0.6 0.0 copy-start
  0.6 1.6 %copy-done = f32[1,2,512,512]{3,2,1,0:T(8,128)S(1)} copy-done((f32[1,2,512,512]{3,2,1,0:T(8,128)S(1)}, f32[1,2,512,512]{3,2,1,0:T(8,128)}, u32[]{:S(2)}) %copy-start) | copy-done | bytes 2097176
  2.2 0.0 copy-start.1
  2.2 64.4 %shard_map.50 = (f32[2,512,512]{2,1,0:T(8,128)S(1)}, f32[8,128]{1,0:T(8,128)S(1)}) custom-call(f32[2,512,512]{2,1,0:T(8,128)S(1)} %bitcast.2), custom_call_target="tpu_custom_call" | custom-call | tf_op jit(solution)/shard_map/pallas_call | solution.py:149
  66.7 0.5 slice.3
  67.9 0.0 copy-done.1
  67.9 4.4 %multiply_subtract_fusion = (f32[2,512,512]{2,1,0:T(8,128)}, f32[2,512,512]{2,1,0:T(8,128)}) fusion(f32[2,512,512]{2,1,0:T(8,128)S(1)} %copy-done.1, f32[2,512,512]{2,1,0:T(8,128)S(1)} %get-tuple-element.5, f32[]{:T(128)} %bitcast.1, f32[2,512,512]{2,1,0:T(8,128)} %param.5), kind=kLoop, calls=%fused_computation | loop fusion | flops 3670016 | bytes 10485764 | tf_op jit(solution)/shard_map/sub | solution.py:26
Async XLA Ops:
  0.6 1.6 %copy-start = (f32[1,2,512,512]{3,2,1,0:T(8,128)S(1)}, f32[1,2,512,512]{3,2,1,0:T(8,128)}, u32[]{:S(2)}) copy-start(f32[1,2,512,512]{3,2,1,0:T(8,128)} %param.3) | copy-start | bytes 6291460
  2.2 65.7 %copy-start.1 = (f32[2,512,512]{2,1,0:T(8,128)S(1)}, f32[2,512,512]{2,1,0:T(8,128)}, u32[]{:S(2)}) copy-start(f32[2,512,512]{2,1,0:T(8,128)} %param.4) | copy-start | bytes 6291460

commit v12 on v11

--- a/solution.py
+++ b/solution.py
@@ -12,7 +12,9 @@
 KVH = 4
 RING = 8
 MESH = pl.DeviceIdType.MESH
-CHAINS = ((1, 0, RING // 2), (-1, 0, (RING - 1) // 2), (1, 1, (RING - 1) // 2), (-1, 1, RING // 2))
+PARTS = 4
+CHAINS = tuple((d, h, RING // 2 if (d > 0) == (h < PARTS // 2) else (RING - 1) // 2)
+               for h in range(PARTS) for d in (1, -1))
 RS_BASE = tuple(sum(c[2] for c in CHAINS[:i]) for i in range(len(CHAINS)))
 Y = sum(c[2] for c in CHAINS)
 AG_BASE = tuple(Y + 1 + base for base in RS_BASE)
@@ -27,7 +29,7 @@
     return (new_params, new_momentum)
 
 
-def ring_kernel(islands, inner, x_ref, out_ref, sq_ref, sbuf, rbuf, ssem, rsem, sq_in, sq_ssem, sq_rsem, sq_z, z_ssem, z_rsem):
+def ring_kernel(islands, inner, x_ref, out_ref, sq_ref, sbuf, rbuf, ssem, rsem, sq_in, sq_ssem, sq_rsem, sq_z, z_ssem, z_rsem, ybuf):
     chunk = x_ref.shape[1] // RING
     me = lax.axis_index("island")
     col = lax.axis_index("inner")
@@ -37,7 +39,7 @@
     left = base + (z + RING - 1) % RING
     partner = (me + RING) % islands
 
-    half = chunk // 2
+    half = chunk // PARTS
 
     def rows(k, h=None):
         start = ((z + k + 2 * RING) % RING) * chunk
@@ -69,22 +71,22 @@
             k = RS_BASE[i] + s
             target = right if d > 0 else left
             if s == 0:
-                pending[i] = send(k, x_ref.at[:, rows(d * r, h)], rbuf.at[k, :, pl.ds(0, half)], target)
+                pending[i] = send(k, x_ref.at[:, rows(d * r, h)], rbuf.at[k], target)
                 continue
             pending[i].wait()
-            sbuf[k, :, pl.ds(0, half)] = rbuf[k - 1, :, pl.ds(0, half)] + x_ref[:, rows(d * (r - s), h)]
-            pending[i] = send(k, sbuf.at[k, :, pl.ds(0, half)], rbuf.at[k, :, pl.ds(0, half)], target)
+            sbuf[k] = rbuf[k - 1] + x_ref[:, rows(d * (r - s), h)]
+            pending[i] = send(k, sbuf.at[k], rbuf.at[k], target)
     for cp in pending:
         cp.wait()
-    for h in range(2):
+    for h in range(PARTS):
         own = x_ref[:, rows(0, h)]
         for i, (d, hh, r) in enumerate(CHAINS):
             if hh == h:
-                own = own + rbuf[RS_BASE[i] + r - 1, :, pl.ds(0, half)]
-        sbuf[Y, :, pl.ds(h * half, half)] = own
-    cy = send(Y, sbuf.at[Y], rbuf.at[Y], partner)
+                own = own + rbuf[RS_BASE[i] + r - 1]
+        ybuf[0, :, pl.ds(h * half, half)] = own
+    cy = send(Y, ybuf.at[0], ybuf.at[1], partner)
     cy.wait()
-    mine = (sbuf[Y] + rbuf[Y]) / islands
+    mine = (ybuf[0] + ybuf[1]) / islands
     out_ref[:, rows(0)] = mine
 
     sq_in[col] = jnp.full(sq_in.shape[1:], jnp.sum(mine * mine), jnp.float32)
@@ -152,8 +154,8 @@
         in_specs=[pl.BlockSpec(memory_space=pltpu.VMEM)],
         out_specs=(pl.BlockSpec(memory_space=pltpu.VMEM), pl.BlockSpec(memory_space=pltpu.VMEM)),
         scratch_shapes=[
-            pltpu.VMEM((COPIES, halves, chunk, cols), own.dtype),
-            pltpu.VMEM((COPIES, halves, chunk, cols), own.dtype),
+            pltpu.VMEM((Y, halves, chunk // PARTS, cols), own.dtype),
+            pltpu.VMEM((Y, halves, chunk // PARTS, cols), own.dtype),
             pltpu.SemaphoreType.DMA((COPIES,)),
             pltpu.SemaphoreType.DMA((COPIES,)),
             pltpu.VMEM((inner, 8, 128), jnp.float32),
@@ -162,6 +164,7 @@
             pltpu.VMEM((RING, 8, 128), jnp.float32),
             pltpu.SemaphoreType.DMA((RING,)),
             pltpu.SemaphoreType.DMA((RING,)),
+            pltpu.VMEM((2, halves, chunk, cols), own.dtype),
         ],
         compiler_params=pltpu.CompilerParams(
             collective_id=0, has_side_effects=True, vmem_limit_bytes=48 * 1024 * 1024),

time: 72.4 us -> 71.2 us (0.983)
  Pallas kernels: 64.4 us -> 63.2 us
    pallas_call x1, Pallas kernels: 64.4 us -> 63.2 us  [all_reduce(): pl.pallas_call(functools.partial(ring_kernel, islands, inner), out_shape=...]
where the time goes in v12:
time: 71.2 us; the launch traced here: 71.1 us
  Pallas kernels  63.2 us (89%)
  other arithmetic  4.4 us (6%)
  local copies, waits for them, and re-layouts  2.1 us (3%)
  between operations  1.35 us (2%)
    pallas_call x1, Pallas kernels, all_reduce(): pl.pallas_call(functools.partial(ring_kernel, islands, inner), out_shape=...  63.2 us
    sub x1, other arithmetic, outer_update(): new_params = params - 0.7 * (clipped + 0.9 * new_momentum)  4.4 us
    unnamed x4, local copies, waits for them, and re-layouts  1.59 us

profile of v12, /device:TPU:32, one launch (start us, length us, event | category | flops | bytes accessed | tf_op | source)
XLA Modules:
  0.0 71.1 jit_solution(8016985805731839915)
XLA Ops:
  0.6 0.0 copy-start
  0.6 1.6 %copy-done = f32[1,2,512,512]{3,2,1,0:T(8,128)S(1)} copy-done((f32[1,2,512,512]{3,2,1,0:T(8,128)S(1)}, f32[1,2,512,512]{3,2,1,0:T(8,128)}, u32[]{:S(2)}) %copy-start) | copy-done | bytes 2097176
  2.2 0.0 copy-start.1
  2.2 63.2 %shard_map.50 = (f32[2,512,512]{2,1,0:T(8,128)S(1)}, f32[8,128]{1,0:T(8,128)S(1)}) custom-call(f32[2,512,512]{2,1,0:T(8,128)S(1)} %bitcast.2), custom_call_target="tpu_custom_call" | custom-call | tf_op jit(solution)/shard_map/pallas_call | solution.py:151
  65.4 0.5 slice.3
  66.7 0.0 copy-done.1
  66.7 4.4 %multiply_subtract_fusion = (f32[2,512,512]{2,1,0:T(8,128)}, f32[2,512,512]{2,1,0:T(8,128)}) fusion(f32[2,512,512]{2,1,0:T(8,128)S(1)} %copy-done.1, f32[2,512,512]{2,1,0:T(8,128)S(1)} %get-tuple-element.5, f32[]{:T(128)} %bitcast.1, f32[2,512,512]{2,1,0:T(8,128)} %param.5), kind=kLoop, calls=%fused_computation | loop fusion | flops 3670016 | bytes 10485764 | tf_op jit(solution)/shard_map/sub | solution.py:28
Async XLA Ops:
  0.6 1.6 %copy-start = (f32[1,2,512,512]{3,2,1,0:T(8,128)S(1)}, f32[1,2,512,512]{3,2,1,0:T(8,128)}, u32[]{:S(2)}) copy-start(f32[1,2,512,512]{3,2,1,0:T(8,128)} %param.3) | copy-start | bytes 6291460
  2.2 64.4 %copy-start.1 = (f32[2,512,512]{2,1,0:T(8,128)S(1)}, f32[2,512,512]{2,1,0:T(8,128)}, u32[]{:S(2)}) copy-start(f32[2,512,512]{2,1,0:T(8,128)} %param.4) | copy-start | bytes 6291460

commit v13 on v12

--- a/solution.py
+++ b/solution.py
@@ -17,8 +17,8 @@
                for h in range(PARTS) for d in (1, -1))
 RS_BASE = tuple(sum(c[2] for c in CHAINS[:i]) for i in range(len(CHAINS)))
 Y = sum(c[2] for c in CHAINS)
-AG_BASE = tuple(Y + 1 + base for base in RS_BASE)
-COPIES = 2 * Y + 1
+AG_BASE = tuple(Y + PARTS + base for base in RS_BASE)
+COPIES = 2 * Y + PARTS
 
 
 def outer_update(average, params, momentum, mean_square):
@@ -76,20 +76,30 @@
             pending[i].wait()
             sbuf[k] = rbuf[k - 1] + x_ref[:, rows(d * (r - s), h)]
             pending[i] = send(k, sbuf.at[k], rbuf.at[k], target)
-    for cp in pending:
-        cp.wait()
+    ycopies = []
     for h in range(PARTS):
         own = x_ref[:, rows(0, h)]
         for i, (d, hh, r) in enumerate(CHAINS):
             if hh == h:
+                pending[i].wait()
                 own = own + rbuf[RS_BASE[i] + r - 1]
-        ybuf[0, :, pl.ds(h * half, half)] = own
-    cy = send(Y, ybuf.at[0], ybuf.at[1], partner)
-    cy.wait()
-    mine = (ybuf[0] + ybuf[1]) / islands
-    out_ref[:, rows(0)] = mine
+        ybuf[0, h] = own
+        ycopies.append(send(Y + h, ybuf.at[0, h], ybuf.at[1, h], partner))
+    squares = []
+    for h in range(PARTS):
+        ycopies[h].wait()
+        mine = (ybuf[0, h] + ybuf[1, h]) / islands
+        out_ref[:, rows(0, h)] = mine
+        squares.append(jnp.sum(mine * mine))
+        for i, (d, hh, r) in enumerate(CHAINS):
+            if hh == h:
+                place = out_ref.at[:, rows(0, h)]
+                pending[i] = send(AG_BASE[i], place, place, right if d > 0 else left)
+    square = squares[0]
+    for part in squares[1:]:
+        square = square + part
 
-    sq_in[col] = jnp.full(sq_in.shape[1:], jnp.sum(mine * mine), jnp.float32)
+    sq_in[col] = jnp.full(sq_in.shape[1:], square, jnp.float32)
     inner_sends = []
     for o in range(1, inner):
         cp = pltpu.make_async_remote_copy(
@@ -118,14 +128,13 @@
             cp.start()
             z_sends.append(cp)
 
-    for s in range(RING // 2):
+    for s in range(1, RING // 2):
         if s == 2:
             to_z_peers()
         for i, (d, h, r) in enumerate(CHAINS):
             if s >= r:
                 continue
-            if s > 0:
-                pending[i].wait()
+            pending[i].wait()
             k = AG_BASE[i] + s
             place = out_ref.at[:, rows(-d * s, h)]
             pending[i] = send(k, place, place, right if d > 0 else left)
@@ -164,7 +173,7 @@
             pltpu.VMEM((RING, 8, 128), jnp.float32),
             pltpu.SemaphoreType.DMA((RING,)),
             pltpu.SemaphoreType.DMA((RING,)),
-            pltpu.VMEM((2, halves, chunk, cols), own.dtype),
+            pltpu.VMEM((2, PARTS, halves, chunk // PARTS, cols), own.dtype),
         ],
         compiler_params=pltpu.CompilerParams(
             collective_id=0, has_side_effects=True, vmem_limit_bytes=48 * 1024 * 1024),

time: 71.2 us -> 66.5 us (0.934); the launches traced: 71.1 us -> 65.6 us
  Pallas kernels: 63.2 us -> 57.7 us
    pallas_call x1, Pallas kernels: 63.2 us -> 57.7 us  [all_reduce(): pl.pallas_call(functools.partial(ring_kernel, islands, inner), out_shape=...]
where the time goes in v13:
time: 66.5 us; the launch traced here: 65.6 us
  Pallas kernels  57.7 us (87%)
  other arithmetic  4.4 us (7%)
  local copies, waits for them, and re-layouts  2.1 us (3%)
  between operations  1.35 us (2%)
    pallas_call x1, Pallas kernels, all_reduce(): pl.pallas_call(functools.partial(ring_kernel, islands, inner), out_shape=...  57.7 us
    sub x1, other arithmetic, outer_update(): new_params = params - 0.7 * (clipped + 0.9 * new_momentum)  4.4 us
    unnamed x4, local copies, waits for them, and re-layouts  1.59 us

profile of v13, /device:TPU:32, one launch (start us, length us, event | category | flops | bytes accessed | tf_op | source)
XLA Modules:
  0.0 65.6 jit_solution(15747311699248613209)
XLA Ops:
  0.6 0.0 copy-start
  0.6 1.6 %copy-done = f32[1,2,512,512]{3,2,1,0:T(8,128)S(1)} copy-done((f32[1,2,512,512]{3,2,1,0:T(8,128)S(1)}, f32[1,2,512,512]{3,2,1,0:T(8,128)}, u32[]{:S(2)}) %copy-start) | copy-done | bytes 2097176
  2.2 0.0 copy-start.1
  2.2 57.7 %shard_map.50 = (f32[2,512,512]{2,1,0:T(8,128)S(1)}, f32[8,128]{1,0:T(8,128)S(1)}) custom-call(f32[2,512,512]{2,1,0:T(8,128)S(1)} %bitcast.2), custom_call_target="tpu_custom_call" | custom-call | tf_op jit(solution)/shard_map/pallas_call | solution.py:160
  59.9 0.5 slice.3
  61.1 0.0 copy-done.1
  61.2 4.4 %multiply_subtract_fusion = (f32[2,512,512]{2,1,0:T(8,128)}, f32[2,512,512]{2,1,0:T(8,128)}) fusion(f32[2,512,512]{2,1,0:T(8,128)S(1)} %copy-done.1, f32[2,512,512]{2,1,0:T(8,128)S(1)} %get-tuple-element.5, f32[]{:T(128)} %bitcast.1, f32[2,512,512]{2,1,0:T(8,128)} %param.5), kind=kLoop, calls=%fused_computation | loop fusion | flops 3670016 | bytes 10485764 | tf_op jit(solution)/shard_map/sub | solution.py:28
Async XLA Ops:
  0.6 1.6 %copy-start = (f32[1,2,512,512]{3,2,1,0:T(8,128)S(1)}, f32[1,2,512,512]{3,2,1,0:T(8,128)}, u32[]{:S(2)}) copy-start(f32[1,2,512,512]{3,2,1,0:T(8,128)} %param.3) | copy-start | bytes 6291460
  2.2 58.9 %copy-start.1 = (f32[2,512,512]{2,1,0:T(8,128)S(1)}, f32[2,512,512]{2,1,0:T(8,128)}, u32[]{:S(2)}) copy-start(f32[2,512,512]{2,1,0:T(8,128)} %param.4) | copy-start | bytes 6291460

commit v14 on v13

--- a/solution.py
+++ b/solution.py
@@ -12,7 +12,7 @@
 KVH = 4
 RING = 8
 MESH = pl.DeviceIdType.MESH
-PARTS = 4
+PARTS = 8
 CHAINS = tuple((d, h, RING // 2 if (d > 0) == (h < PARTS // 2) else (RING - 1) // 2)
                for h in range(PARTS) for d in (1, -1))
 RS_BASE = tuple(sum(c[2] for c in CHAINS[:i]) for i in range(len(CHAINS)))

time: 66.5 us -> 66 us (level)
  no operation moved by 1% of the time
where the time goes in v14:
time: 66 us; the launch traced here: 65.2 us
  Pallas kernels  57.4 us (87%)
  other arithmetic  4.4 us (7%)
  local copies, waits for them, and re-layouts  2.1 us (3%)
  between operations  1.35 us (2%)
    pallas_call x1, Pallas kernels, all_reduce(): pl.pallas_call(functools.partial(ring_kernel, islands, inner), out_shape=...  57.4 us
    sub x1, other arithmetic, outer_update(): new_params = params - 0.7 * (clipped + 0.9 * new_momentum)  4.4 us
    unnamed x4, local copies, waits for them, and re-layouts  1.59 us

profile of v14, /device:TPU:32, one launch (start us, length us, event | category | flops | bytes accessed | tf_op | source)
XLA Modules:
  0.0 65.2 jit_solution(15336171995093753498)
XLA Ops:
  0.6 0.0 copy-start
  0.6 1.6 %copy-done = f32[1,2,512,512]{3,2,1,0:T(8,128)S(1)} copy-done((f32[1,2,512,512]{3,2,1,0:T(8,128)S(1)}, f32[1,2,512,512]{3,2,1,0:T(8,128)}, u32[]{:S(2)}) %copy-start) | copy-done | bytes 2097176
  2.2 0.0 copy-start.1
  2.2 57.4 %shard_map.50 = (f32[2,512,512]{2,1,0:T(8,128)S(1)}, f32[8,128]{1,0:T(8,128)S(1)}) custom-call(f32[2,512,512]{2,1,0:T(8,128)S(1)} %bitcast.2), custom_call_target="tpu_custom_call" | custom-call | tf_op jit(solution)/shard_map/pallas_call | solution.py:160
  59.6 0.5 slice.3
  60.8 0.0 copy-done.1
  60.8 4.4 %multiply_subtract_fusion = (f32[2,512,512]{2,1,0:T(8,128)}, f32[2,512,512]{2,1,0:T(8,128)}) fusion(f32[2,512,512]{2,1,0:T(8,128)S(1)} %copy-done.1, f32[2,512,512]{2,1,0:T(8,128)S(1)} %get-tuple-element.5, f32[]{:T(128)} %bitcast.1, f32[2,512,512]{2,1,0:T(8,128)} %param.5), kind=kLoop, calls=%fused_computation | loop fusion | flops 3670016 | bytes 10485764 | tf_op jit(solution)/shard_map/sub | solution.py:28
Async XLA Ops:
  0.6 1.6 %copy-start = (f32[1,2,512,512]{3,2,1,0:T(8,128)S(1)}, f32[1,2,512,512]{3,2,1,0:T(8,128)}, u32[]{:S(2)}) copy-start(f32[1,2,512,512]{3,2,1,0:T(8,128)} %param.3) | copy-start | bytes 6291460
  2.2 58.6 %copy-start.1 = (f32[2,512,512]{2,1,0:T(8,128)S(1)}, f32[2,512,512]{2,1,0:T(8,128)}, u32[]{:S(2)}) copy-start(f32[2,512,512]{2,1,0:T(8,128)} %param.4) | copy-start | bytes 6291460

commit v15 on v14

--- a/solution.py
+++ b/solution.py
@@ -29,8 +29,8 @@
     return (new_params, new_momentum)
 
 
-def ring_kernel(islands, inner, x_ref, out_ref, sq_ref, sbuf, rbuf, ssem, rsem, sq_in, sq_ssem, sq_rsem, sq_z, z_ssem, z_rsem, ybuf):
-    chunk = x_ref.shape[1] // RING
+def ring_kernel(islands, inner, x_hbm, out_ref, sq_ref, sbuf, rbuf, ssem, rsem, sq_in, sq_ssem, sq_rsem, sq_z, z_ssem, z_rsem, ybuf, x_ref, x_sem):
+    chunk = x_hbm.shape[1] // RING
     me = lax.axis_index("island")
     col = lax.axis_index("inner")
     z = me % RING
@@ -54,6 +54,8 @@
         cp.start()
         return cp
 
+    load = pltpu.make_async_copy(x_hbm, x_ref, x_sem)
+    load.start()
     barrier = pltpu.get_barrier_semaphore()
     for target in (left, right, partner):
         pl.semaphore_signal(barrier, inc=1, device_id={"island": target}, device_id_type=MESH)
@@ -71,8 +73,10 @@
             k = RS_BASE[i] + s
             target = right if d > 0 else left
             if s == 0:
-                pending[i] = send(k, x_ref.at[:, rows(d * r, h)], rbuf.at[k], target)
+                pending[i] = send(k, x_hbm.at[:, rows(d * r, h)], rbuf.at[k], target)
                 continue
+            if s == 1 and i == 0:
+                load.wait()
             pending[i].wait()
             sbuf[k] = rbuf[k - 1] + x_ref[:, rows(d * (r - s), h)]
             pending[i] = send(k, sbuf.at[k], rbuf.at[k], target)
@@ -160,7 +164,7 @@
     return pl.pallas_call(
         functools.partial(ring_kernel, islands, inner),
         out_shape=(jax.ShapeDtypeStruct(own.shape, own.dtype), jax.ShapeDtypeStruct((8, 128), jnp.float32)),
-        in_specs=[pl.BlockSpec(memory_space=pltpu.VMEM)],
+        in_specs=[pl.BlockSpec(memory_space=pl.ANY)],
         out_specs=(pl.BlockSpec(memory_space=pltpu.VMEM), pl.BlockSpec(memory_space=pltpu.VMEM)),
         scratch_shapes=[
             pltpu.VMEM((Y, halves, chunk // PARTS, cols), own.dtype),
@@ -174,9 +178,11 @@
             pltpu.SemaphoreType.DMA((RING,)),
             pltpu.SemaphoreType.DMA((RING,)),
             pltpu.VMEM((2, PARTS, halves, chunk // PARTS, cols), own.dtype),
+            pltpu.VMEM(own.shape, own.dtype),
+            pltpu.SemaphoreType.DMA(()),
         ],
         compiler_params=pltpu.CompilerParams(
-            collective_id=0, has_side_effects=True, vmem_limit_bytes=48 * 1024 * 1024),
+            collective_id=0, has_side_effects=True, vmem_limit_bytes=67043328),
     )(own)
 
 

time: 66 us -> 68.1 us (1.032)
  Pallas kernels: 57.4 us -> 59.2 us
  other arithmetic: 4.4 us -> 5.66 us
  local copies, waits for them, and re-layouts: 2.1 us -> 1.19 us
    pallas_call x1, Pallas kernels: 57.4 us -> 59.2 us  [all_reduce(): pl.pallas_call(functools.partial(ring_kernel, islands, inner), out_shape=...]
    unnamed x4 -> x0, local copies, waits for them, and re-layouts: 1.59 us -> none
    sub x1, other arithmetic: 4.4 us -> 5.66 us  [outer_update(): new_params = params - 0.7 * (clipped + 0.9 * new_momentum)]
where the time goes in v15:
time: 68.1 us; the launch traced here: 67.4 us
  Pallas kernels  59.2 us (87%)
  other arithmetic  5.66 us (8%)
  between operations  1.33 us (2%)
  local copies, waits for them, and re-layouts  1.19 us (2%)
    pallas_call x1, Pallas kernels, all_reduce(): pl.pallas_call(functools.partial(ring_kernel, islands, inner), out_shape=...  59.2 us
    sub x1, other arithmetic, outer_update(): new_params = params - 0.7 * (clipped + 0.9 * new_momentum)  5.66 us

profile of v15, /device:TPU:32, one launch (start us, length us, event | category | flops | bytes accessed | tf_op | source)
XLA Modules:
  0.0 67.4 jit_solution(12699600163925028339)
XLA Ops:
  0.6 59.2 %shard_map.50 = (f32[2,512,512]{2,1,0:T(8,128)}, f32[8,128]{1,0:T(8,128)}) custom-call(f32[2,512,512]{2,1,0:T(8,128)} %bitcast.2), custom_call_target="tpu_custom_call" | custom-call | tf_op jit(solution)/shard_map/pallas_call | solution.py:164
  59.8 1.2 %slice.3 = f32[1,1]{1,0:T(1,128)} slice(f32[8,128]{1,0:T(8,128)} %get-tuple-element.4), slice={[0:1], [0:1]} | slice | bytes 8 | tf_op jit(solution)/shard_map/slice | solution.py:194
  61.7 5.7 %multiply_subtract_fusion = (f32[2,512,512]{2,1,0:T(8,128)}, f32[2,512,512]{2,1,0:T(8,128)}) fusion(f32[2,512,512]{2,1,0:T(8,128)} %param.4, f32[2,512,512]{2,1,0:T(8,128)} %get-tuple-element.5, f32[]{:T(128)} %bitcast.1, f32[2,512,512]{2,1,0:T(8,128)} %param.5), kind=kLoop, calls=%fused_computation | loop fusion | flops 3670016 | bytes 10485764 | tf_op jit(solution)/shard_map/sub | solution.py:28

commit v16 on v14

--- a/solution.py
+++ b/solution.py
@@ -151,7 +151,7 @@
     total = sq_z[0]
     for c in range(1, RING):
         total = total + sq_z[c]
-    sq_ref[...] = total
+    sq_ref[...] = total[0:1, 0:1]
 
 
 def all_reduce(own, islands, inner):
@@ -159,7 +159,7 @@
     chunk = rows // RING
     return pl.pallas_call(
         functools.partial(ring_kernel, islands, inner),
-        out_shape=(jax.ShapeDtypeStruct(own.shape, own.dtype), jax.ShapeDtypeStruct((8, 128), jnp.float32)),
+        out_shape=(jax.ShapeDtypeStruct(own.shape, own.dtype), jax.ShapeDtypeStruct((1, 1), jnp.float32)),
         in_specs=[pl.BlockSpec(memory_space=pltpu.VMEM)],
         out_specs=(pl.BlockSpec(memory_space=pltpu.VMEM), pl.BlockSpec(memory_space=pltpu.VMEM)),
         scratch_shapes=[
@@ -185,7 +185,7 @@
     inner = lax.axis_size("inner")
     count = 2 * D * KVH * HEAD
     average, sq = all_reduce(island_delta[0], islands, inner)
-    return outer_update(average, params, momentum, sq[0, 0] / count)
+    return outer_update(average, params, momentum, sq.reshape(()) / count)
 
 
 def solution(mesh):

time: 66 us -> 66 us (level)
  no operation moved by 1% of the time
where the time goes in v16:
time: 66 us; the launch traced here: 65.3 us
  Pallas kernels  58 us (88%)
  other arithmetic  4.4 us (7%)
  local copies, waits for them, and re-layouts  1.59 us (2%)
  between operations  1.33 us (2%)
    pallas_call x1, Pallas kernels, all_reduce(): pl.pallas_call(functools.partial(ring_kernel, islands, inner), out_shape=...  58 us
    sub x1, other arithmetic, outer_update(): new_params = params - 0.7 * (clipped + 0.9 * new_momentum)  4.4 us
    unnamed x4, local copies, waits for them, and re-layouts  1.59 us

profile of v16, /device:TPU:32, one launch (start us, length us, event | category | flops | bytes accessed | tf_op | source)
XLA Modules:
  0.0 65.3 jit_solution(16089925758725697557)
XLA Ops:
  0.6 0.0 copy-start
  0.6 1.6 %copy-done = f32[1,2,512,512]{3,2,1,0:T(8,128)S(1)} copy-done((f32[1,2,512,512]{3,2,1,0:T(8,128)S(1)}, f32[1,2,512,512]{3,2,1,0:T(8,128)}, u32[]{:S(2)}) %copy-start) | copy-done | bytes 2097176
  2.2 0.0 copy-start.1
  2.2 58.0 %shard_map.50 = (f32[2,512,512]{2,1,0:T(8,128)S(1)}, f32[1,1]{1,0:T(1,128)}) custom-call(f32[2,512,512]{2,1,0:T(8,128)S(1)} %bitcast.2), custom_call_target="tpu_custom_call" | custom-call | tf_op jit(solution)/shard_map/pallas_call | solution.py:160
  60.9 0.0 copy-done.1
  60.9 4.4 %multiply_subtract_fusion = (f32[2,512,512]{2,1,0:T(8,128)}, f32[2,512,512]{2,1,0:T(8,128)}) fusion(f32[2,512,512]{2,1,0:T(8,128)S(1)} %copy-done.1, f32[2,512,512]{2,1,0:T(8,128)S(1)} %get-tuple-element.5, f32[]{:T(128)} %bitcast.1, f32[2,512,512]{2,1,0:T(8,128)} %param.5), kind=kLoop, calls=%fused_computation | loop fusion | flops 3670016 | bytes 10485764 | tf_op jit(solution)/shard_map/sub | solution.py:28
Async XLA Ops:
  0.6 1.6 %copy-start = (f32[1,2,512,512]{3,2,1,0:T(8,128)S(1)}, f32[1,2,512,512]{3,2,1,0:T(8,128)}, u32[]{:S(2)}) copy-start(f32[1,2,512,512]{3,2,1,0:T(8,128)} %param.3) | copy-start | bytes 6291460
  2.2 58.6 %copy-start.1 = (f32[2,512,512]{2,1,0:T(8,128)S(1)}, f32[2,512,512]{2,1,0:T(8,128)}, u32[]{:S(2)}) copy-start(f32[2,512,512]{2,1,0:T(8,128)} %param.4) | copy-start | bytes 6291460

commit v17 on v14

--- a/solution.py
+++ b/solution.py
@@ -129,7 +129,7 @@
             z_sends.append(cp)
 
     for s in range(1, RING // 2):
-        if s == 2:
+        if s == 1:
             to_z_peers()
         for i, (d, h, r) in enumerate(CHAINS):
             if s >= r:

time: 66 us -> 69.8 us (1.058)
  the two profiles are of different devices: /device:TPU:32 before, /device:TPU:1 now
where the time goes in v17:
time: 69.8 us; the launch traced here: 69.7 us
  Pallas kernels  61.8 us (89%)
  other arithmetic  4.4 us (6%)
  local copies, waits for them, and re-layouts  2.1 us (3%)
  between operations  1.35 us (2%)
    pallas_call x1, Pallas kernels, all_reduce(): pl.pallas_call(functools.partial(ring_kernel, islands, inner), out_shape=...  61.8 us
    sub x1, other arithmetic, outer_update(): new_params = params - 0.7 * (clipped + 0.9 * new_momentum)  4.4 us
    unnamed x4, local copies, waits for them, and re-layouts  1.59 us

profile of v17, /device:TPU:1, one launch (start us, length us, event | category | flops | bytes accessed | tf_op | source)
XLA Modules:
  0.0 69.7 jit_solution(2386081111071679373)
XLA Ops:
  0.6 0.0 copy-start
  0.6 1.6 %copy-done = f32[1,2,512,512]{3,2,1,0:T(8,128)S(1)} copy-done((f32[1,2,512,512]{3,2,1,0:T(8,128)S(1)}, f32[1,2,512,512]{3,2,1,0:T(8,128)}, u32[]{:S(2)}) %copy-start) | copy-done | bytes 2097176
  2.2 0.0 copy-start.1
  2.2 61.8 %shard_map.50 = (f32[2,512,512]{2,1,0:T(8,128)S(1)}, f32[8,128]{1,0:T(8,128)S(1)}) custom-call(f32[2,512,512]{2,1,0:T(8,128)S(1)} %bitcast.2), custom_call_target="tpu_custom_call" | custom-call | tf_op jit(solution)/shard_map/pallas_call | solution.py:160
  64.0 0.5 slice.3
  65.3 0.0 copy-done.1
  65.3 4.4 %multiply_subtract_fusion = (f32[2,512,512]{2,1,0:T(8,128)}, f32[2,512,512]{2,1,0:T(8,128)}) fusion(f32[2,512,512]{2,1,0:T(8,128)S(1)} %copy-done.1, f32[2,512,512]{2,1,0:T(8,128)S(1)} %get-tuple-element.5, f32[]{:T(128)} %bitcast.1, f32[2,512,512]{2,1,0:T(8,128)} %param.5), kind=kLoop, calls=%fused_computation | loop fusion | flops 3670016 | bytes 10485764 | tf_op jit(solution)/shard_map/sub | solution.py:28
Async XLA Ops:
  0.6 1.6 %copy-start = (f32[1,2,512,512]{3,2,1,0:T(8,128)S(1)}, f32[1,2,512,512]{3,2,1,0:T(8,128)}, u32[]{:S(2)}) copy-start(f32[1,2,512,512]{3,2,1,0:T(8,128)} %param.3) | copy-start | bytes 6291460
  2.2 63.0 %copy-start.1 = (f32[2,512,512]{2,1,0:T(8,128)S(1)}, f32[2,512,512]{2,1,0:T(8,128)}, u32[]{:S(2)}) copy-start(f32[2,512,512]{2,1,0:T(8,128)} %param.4) | copy-start | bytes 6291460

commit v18 on v17

--- a/solution.py
+++ b/solution.py
@@ -129,7 +129,7 @@
             z_sends.append(cp)
 
     for s in range(1, RING // 2):
-        if s == 1:
+        if s == 3:
             to_z_peers()
         for i, (d, h, r) in enumerate(CHAINS):
             if s >= r:

time: 69.8 us -> 65.8 us (0.943)
  the two profiles are of different devices: /device:TPU:1 before, /device:TPU:32 now
where the time goes in v18:
time: 65.8 us; the launch traced here: 65.2 us
  Pallas kernels  57.4 us (87%)
  other arithmetic  4.4 us (7%)
  local copies, waits for them, and re-layouts  2.1 us (3%)
  between operations  1.35 us (2%)
    pallas_call x1, Pallas kernels, all_reduce(): pl.pallas_call(functools.partial(ring_kernel, islands, inner), out_shape=...  57.4 us
    sub x1, other arithmetic, outer_update(): new_params = params - 0.7 * (clipped + 0.9 * new_momentum)  4.4 us
    unnamed x4, local copies, waits for them, and re-layouts  1.59 us

profile of v18, /device:TPU:32, one launch (start us, length us, event | category | flops | bytes accessed | tf_op | source)
XLA Modules:
  0.0 65.2 jit_solution(11108180551307263230)
XLA Ops:
  0.6 0.0 copy-start
  0.6 1.6 %copy-done = f32[1,2,512,512]{3,2,1,0:T(8,128)S(1)} copy-done((f32[1,2,512,512]{3,2,1,0:T(8,128)S(1)}, f32[1,2,512,512]{3,2,1,0:T(8,128)}, u32[]{:S(2)}) %copy-start) | copy-done | bytes 2097176
  2.2 0.0 copy-start.1
  2.2 57.4 %shard_map.50 = (f32[2,512,512]{2,1,0:T(8,128)S(1)}, f32[8,128]{1,0:T(8,128)S(1)}) custom-call(f32[2,512,512]{2,1,0:T(8,128)S(1)} %bitcast.2), custom_call_target="tpu_custom_call" | custom-call | tf_op jit(solution)/shard_map/pallas_call | solution.py:160
  59.6 0.5 slice.3
  60.8 0.0 copy-done.1
  60.8 4.4 %multiply_subtract_fusion = (f32[2,512,512]{2,1,0:T(8,128)}, f32[2,512,512]{2,1,0:T(8,128)}) fusion(f32[2,512,512]{2,1,0:T(8,128)S(1)} %copy-done.1, f32[2,512,512]{2,1,0:T(8,128)S(1)} %get-tuple-element.5, f32[]{:T(128)} %bitcast.1, f32[2,512,512]{2,1,0:T(8,128)} %param.5), kind=kLoop, calls=%fused_computation | loop fusion | flops 3670016 | bytes 10485764 | tf_op jit(solution)/shard_map/sub | solution.py:28
Async XLA Ops:
  0.6 1.6 %copy-start = (f32[1,2,512,512]{3,2,1,0:T(8,128)S(1)}, f32[1,2,512,512]{3,2,1,0:T(8,128)}, u32[]{:S(2)}) copy-start(f32[1,2,512,512]{3,2,1,0:T(8,128)} %param.3) | copy-start | bytes 6291460
  2.2 58.6 %copy-start.1 = (f32[2,512,512]{2,1,0:T(8,128)S(1)}, f32[2,512,512]{2,1,0:T(8,128)}, u32[]{:S(2)}) copy-start(f32[2,512,512]{2,1,0:T(8,128)} %param.4) | copy-start | bytes 6291460
